TPU v7x, 32 devices: a whole 2x2x4 slice. The times are simulated.
32 devices in a mesh: dp: 8 (over y, x, core), expert: 4 (over z).
Axes of the slice: x: 2, y: 2, z: 4, core: 2. Of those that a mesh axis runs over, the one named last changes fastest.
Arguments:
- tokens: bfloat16 [1024, 2048], P('expert'), may hold values from -6 to 6
- grad_out: bfloat16 [1024, 2048], P('expert'), may hold values from -6 to 6
- expert_ids: int32 [1024, 1], P('expert'), may hold values from 0 to 3; in each aligned block of 256 rows (0 to 255, 256 to 511, ...) at most 160 rows name the same one
- gate_prob: float32 [1024, 1], P('expert'), may hold values from 0.2 to 1
- w_gate: bfloat16 [4, 2048, 4096], P('expert', None, 'dp'), may hold values from -0.125 to 0.125
- w_up: bfloat16 [4, 2048, 4096], P('expert', None, 'dp'), may hold values from -0.125 to 0.125
- w_down: bfloat16 [4, 4096, 2048], P('expert', 'dp'), may hold values from -0.09375 to 0.09375
Outputs:
- grad_tokens: bfloat16 [1024, 2048], P('expert')
- grad_gate: bfloat16 [4, 2048, 4096], P('expert', None, 'dp')
- grad_up: bfloat16 [4, 2048, 4096], P('expert', None, 'dp')
- grad_down: bfloat16 [4, 4096, 2048], P('expert', 'dp')
Inputs may be any that keep to these rules, and one draw needn't show every extreme that they name: `expert_ids`: within the 256 tokens of one group no expert is named more than 160 times; in some group's tokens one expert is named exactly 160 times.
All inputs are finite; a program needn't handle non-finite values.
Results may differ from a plain program's by a relative error of at most 0.012.
Values may be sent and summed in bfloat16 or wider, within the bound.
No kernel may reach another device: no remote copies, remote signals or barrier semaphores. Data moves between devices by JAX's collectives and lax.ppermute only.
A program may use at most 128 MiB of HBM per device.

v0:
```python
import jax
import jax.numpy as jnp
from jax import lax
from jax.sharding import PartitionSpec as P


def silu_parts(pre_gate):
    sigma = jax.nn.sigmoid(pre_gate)
    return (pre_gate * sigma, sigma * (1.0 + pre_gate * (1.0 - sigma)))


def per_device(tokens, grad_out, expert_ids, gate_prob, w_gate, w_up, w_down):
    expert_count = lax.axis_size("expert")
    replica_count = lax.axis_size("dp")
    tok_count = tokens.shape[0]
    width_all = tokens.shape[1]
    capacity = max(2, (5 * tok_count + 2 * expert_count - 1) // (2 * expert_count))
    routed = expert_ids[:, 0]
    one_hot = (routed[:, None] == jnp.arange(expert_count, dtype=jnp.int32)[None, :]).astype(
        jnp.int32
    )
    slot_index = jnp.sum((jnp.cumsum(one_hot, axis=0) - one_hot) * one_hot, axis=1)
    target = routed * capacity + slot_index
    assign = (
        target[None, :] == jnp.arange(expert_count * capacity, dtype=jnp.int32)[:, None]
    ).astype(jnp.bfloat16)
    scaled = (gate_prob * grad_out.astype(jnp.float32)).astype(jnp.bfloat16)
    input_slots = jnp.dot(assign, tokens, preferred_element_type=jnp.float32).astype(jnp.bfloat16)
    scaled_slots = jnp.dot(assign, scaled, preferred_element_type=jnp.float32).astype(jnp.bfloat16)
    hidden_part = w_gate.shape[2]
    w_pair = jnp.concatenate([w_gate[0], w_up[0]], axis=1)
    down_rows = w_down[0]
    contract_last = (((1,), (1,)), ((), ()))
    contract_first = (((0,), (0,)), ((), ()))
    share = width_all // replica_count
    offset = lax.axis_index("dp") * share
    input_cols = lax.dynamic_slice_in_dim(input_slots, offset, share, 1)
    scaled_cols = lax.dynamic_slice_in_dim(scaled_slots, offset, share, 1)
    got_input, got_scaled = (
        lax.all_to_all(input_cols, "expert", split_axis=0, concat_axis=0, tiled=True),
        lax.all_to_all(scaled_cols, "expert", split_axis=0, concat_axis=0, tiled=True),
    )
    all_inputs, all_scaled = (
        lax.all_gather(got_input, "dp", axis=1, tiled=True),
        lax.all_gather(got_scaled, "dp", axis=1, tiled=True),
    )
    pre_act = jnp.dot(all_inputs, w_pair, preferred_element_type=jnp.float32)
    pre_gate = pre_act[:, :hidden_part]
    pre_up = pre_act[:, hidden_part:]
    activated, slope = silu_parts(pre_gate)
    hidden = (activated * pre_up).astype(jnp.bfloat16)
    hidden_grad = lax.dot_general(
        all_scaled, down_rows, contract_last, preferred_element_type=jnp.float32
    )
    down_grad = lax.dot_general(
        hidden, all_scaled, contract_first, preferred_element_type=jnp.float32
    )
    up_grad = (hidden_grad * activated).astype(jnp.bfloat16)
    gate_grad = (hidden_grad * pre_up * slope).astype(jnp.bfloat16)
    pair_grad = jnp.concatenate([gate_grad, up_grad], axis=1)
    weight_grad = lax.dot_general(
        all_inputs, pair_grad, contract_first, preferred_element_type=jnp.float32
    )
    terms = lax.dot_general(pair_grad, w_pair, contract_last, preferred_element_type=jnp.float32)
    weight_grad, down_grad, terms = (weight_grad, down_grad, terms)
    summed = lax.psum_scatter(terms.astype(jnp.bfloat16), "dp", scatter_dimension=1, tiled=True)
    returned_rows = lax.all_to_all(summed, "expert", split_axis=0, concat_axis=0, tiled=True)
    token_cols = lax.dot_general(
        assign, returned_rows, contract_first, preferred_element_type=jnp.float32
    ).astype(jnp.bfloat16)
    grad_tokens = lax.all_gather(token_cols, "dp", axis=1, tiled=True)
    gate_wgrad = weight_grad[:, :hidden_part].astype(jnp.bfloat16)
    up_wgrad = weight_grad[:, hidden_part:].astype(jnp.bfloat16)
    return (grad_tokens, gate_wgrad[None], up_wgrad[None], down_grad.astype(jnp.bfloat16)[None])


def solution(mesh):
    placed = (
        P("expert", None),
        P("expert", None),
        P("expert", None),
        P("expert", None),
        P("expert", None, "dp"),
        P("expert", None, "dp"),
        P("expert", "dp", None),
    )
    return jax.shard_map(
        per_device,
        mesh=mesh,
        in_specs=placed,
        out_specs=(
            P("expert", None),
            P("expert", None, "dp"),
            P("expert", None, "dp"),
            P("expert", "dp", None),
        ),
        check_vma=False,
    )
```

profile of v0, /device:TPU:0, one launch (start us, length us, event | category | flops | bytes accessed | tf_op | source)
XLA Modules:
  0.0 191.5 jit_solution(14495183250338226475)
XLA Ops:
  7.2 0.0 copy-start
  7.2 0.0 all-gather.6.cloned.1.call-start
  7.2 0.8 compare_convert_fusion
  8.1 1.2 reduce-window.6
  9.3 0.1 slice.26
  9.3 0.1 copy.11
  9.5 0.1 copy.12
  9.6 0.1 add_bitcast_fusion
  9.7 0.7 fusion.14
  10.4 0.7 multiply_add_fusion
  11.0 0.0 copy-start.1
  11.0 0.0 copy-start.2
  11.0 2.2 %fusion.7 = bf16[640,2048]{1,0:T(8,128)(2,1)S(1)} fusion(bf16[256,2048]{1,0:T(8,128)(2,1)} %param.7, s32[256]{0:T(256)S(1)} %multiply_add_fusion), kind=kOutput, calls=%fused_computation.23 | convolution fusion | flops 671252480 | bytes 3671040 | tf_op jit(solution)/shard_map/dot_general | solution.py:28
  13.2 0.1 dynamic-slice_convert_fusion
  13.3 16.5 %all_to_all.36 = bf16[4,160,256]{2,1,0:T(8,128)(2,1)} all-to-all(bf16[4,160,256]{2,1,0:T(8,128)(2,1)S(1)} %bitcast.50), channel_id=1, replica_groups=mesh['dp'=8,'expert'=4] {'expert'}, dimensions={0} | all-to-all | bytes 655360 | tf_op jit(solution)/shard_map/all_to_all | solution.py:40
  29.8 0.0 all-gather.6.cloned.1.call-update
  29.8 0.0 all-gather.4.cloned.1.call-start
  29.8 0.0 copy-done.1
  29.9 0.0 copy-done.2
  29.9 0.9 fusion.5
  30.8 0.1 dynamic-slice_convert_fusion.1
  30.9 12.1 %all_to_all.37 = bf16[4,160,256]{2,1,0:T(8,128)(2,1)} all-to-all(bf16[4,160,256]{2,1,0:T(8,128)(2,1)S(1)} %bitcast.49), channel_id=1, replica_groups=mesh['dp'=8,'expert'=4] {'expert'}, dimensions={0} | all-to-all | bytes 655360 | tf_op jit(solution)/shard_map/all_to_all | solution.py:41
  43.0 0.0 all-gather.4.cloned.1.call-update
  43.1 0.0 reduce-scatter.2.cloned.1.call-start
  43.1 16.5 %all-gather.6.cloned.1.call-done = bf16[640,2048]{1,0:T(8,128)(2,1)} async-done(((bf16[640,256]{1,0:T(8,128)(2,1)}), bf16[640,2048]{1,0:T(8,128)(2,1)}) %all-gather.6.cloned.1.call-update) | async-done | bytes 2621456 | tf_op jit(solution)/shard_map/all_gather | solution.py:44
  59.6 8.0 %fusion.1 = f32[640,1024]{0,1:T(8,128)} fusion(bf16[640,2048]{1,0:T(8,128)(2,1)} %all-gather.6.cloned.1.call-done, bf16[2048,512]{1,0:T(8,128)(2,1)} %bitcast.58, bf16[2048,512]{1,0:T(8,128)(2,1)} %bitcast.60), kind=kOutput, calls=%fused_computation.5 | convolution fusion | flops 2692743168 | bytes 9437184 | tf_op jit(solution)/shard_map/dot_general | solution.py:47
  67.6 24.4 %all-gather.4.cloned.1.call-done = bf16[640,2048]{1,0:T(8,128)(2,1)} async-done(((bf16[640,256]{1,0:T(8,128)(2,1)}), bf16[640,2048]{1,0:T(8,128)(2,1)}) %all-gather.4.cloned.1.call-update) | async-done | bytes 2621456 | tf_op jit(solution)/shard_map/all_gather | solution.py:45
  92.0 0.0 copy-done
  92.0 0.0 copy-start.4
  92.0 0.0 copy-start.5
  92.0 4.7 %multiply_convert_fusion.3 = (bf16[640,512]{0,1:T(8,128)(2,1)S(1)}, bf16[640,512]{0,1:T(8,128)(2,1)S(1)}) fusion(f32[640,1024]{0,1:T(8,128)} %fusion.1, bf16[640,2048]{1,0:T(8,128)(2,1)} %all-gather.4.cloned.1.call-done, bf16[1,512,2048]{2,1,0:T(8,128)(2,1)S(1)} %copy-done), kind=kOutput, calls=%fused_computation.14 | convolution fusion | flops 1346437120 | bytes 8650752 | tf_op jit(solution)/shard_map/dot_general | solution.py:52
  96.7 0.0 copy-done.4
  96.7 0.0 copy-done.5
  96.7 4.3 %convolution_convert_fusion.1 = bf16[640,2048]{1,0:T(8,128)(2,1)} fusion(bf16[2048,512]{1,0:T(8,128)(2,1)S(1)} %bitcast.59, bf16[2048,512]{1,0:T(8,128)(2,1)S(1)} %bitcast.61, bf16[640,512]{0,1:T(8,128)(2,1)S(1)} %get-tuple-element.7, bf16[640,512]{0,1:T(8,128)(2,1)S(1)} %get-tuple-element.6), kind=kOutput, calls=%fused_computation.2 | convolution fusion | flops 2696675328 | bytes 8126464 | tf_op jit(solution)/shard_map/dot_general | solution.py:64
  101.1 0.0 reduce-scatter.2.cloned.1.call-update
  101.1 0.0 all-gather.8.cloned.1.call-start
  101.1 43.7 %reduce-scatter.2.cloned.1.call-done = bf16[640,256]{1,0:T(8,128)(2,1)} async-done(((bf16[640,2048]{1,0:T(8,128)(2,1)}), bf16[640,256]{1,0:T(8,128)(2,1)}) %reduce-scatter.2.cloned.1.call-update) | async-done | bytes 327696 | tf_op jit(solution)/shard_map/reduce_scatter | solution.py:66
  144.9 14.9 %all_to_all.38 = bf16[4,160,256]{2,1,0:T(8,128)(2,1)S(1)} all-to-all(bf16[4,160,256]{2,1,0:T(8,128)(2,1)} %bitcast.51), channel_id=1, replica_groups=mesh['dp'=8,'expert'=4] {'expert'}, dimensions={0} | all-to-all | bytes 655360 | tf_op jit(solution)/shard_map/all_to_all | solution.py:67
  159.8 1.0 convolution_convert_fusion.3
  160.8 0.0 all-gather.8.cloned.1.call-update
  160.8 0.0 copy-start.3
  160.8 5.8 %fusion = bf16[1,512,2048]{2,1,0:T(8,128)(2,1)} fusion(bf16[640,2048]{1,0:T(8,128)(2,1)} %all-gather.4.cloned.1.call-done, f32[640,1024]{0,1:T(8,128)} %fusion.1), kind=kOutput, calls=%fused_computation.4 | convolution fusion | flops 1345191936 | bytes 7340032 | tf_op jit(solution)/shard_map/dot_general | solution.py:55
  166.6 0.0 copy-done.3
  166.6 4.6 %convolution_convert_fusion = bf16[2048,1024]{1,0:T(8,128)(2,1)S(1)} fusion(bf16[640,2048]{1,0:T(8,128)(2,1)S(1)} %copy-done.3, bf16[640,512]{0,1:T(8,128)(2,1)S(1)} %get-tuple-element.7, bf16[640,512]{0,1:T(8,128)(2,1)S(1)} %get-tuple-element.6), kind=kOutput, calls=%fused_computation.1 | convolution fusion | flops 2689073152 | bytes 8126464 | tf_op jit(solution)/shard_map/dot_general | solution.py:61
  171.3 2.3 %slice_bitcast_fusion = (bf16[1,2048,512]{2,1,0:T(8,128)(2,1)}, bf16[1,2048,512]{2,1,0:T(8,128)(2,1)}) fusion(bf16[2048,1024]{1,0:T(8,128)(2,1)S(1)} %convolution_convert_fusion), kind=kLoop, calls=%fused_computation.6 | loop fusion | bytes 8388608 | tf_op jit(solution)/shard_map/broadcast_in_dim | solution.py:74
  173.6 9.1 %all-gather.8.cloned.1.call-done = bf16[256,2048]{1,0:T(8,128)(2,1)} async-done(((bf16[256,256]{1,0:T(8,128)(2,1)}), bf16[256,2048]{1,0:T(8,128)(2,1)}) %all-gather.8.cloned.1.call-update) | async-done | bytes 1048592 | tf_op jit(solution)/shard_map/all_gather | solution.py:71
  182.7 2.3 %copy.19 = bf16[256,2048]{1,0:T(8,128)(2,1)} copy(bf16[256,2048]{1,0:T(8,128)(2,1)} %all-gather.8.cloned.1.call-done) | data formatting | bytes 2097152
  (2 shorter events, 0.0 us)
Async XLA Ops:
  7.2 84.8 %copy-start = (bf16[1,512,2048]{2,1,0:T(8,128)(2,1)S(1)}, bf16[1,512,2048]{2,1,0:T(8,128)(2,1)}, u32[]{:S(2)}) copy-start(bf16[1,512,2048]{2,1,0:T(8,128)(2,1)} %param.13) | copy-start | bytes 6291460
  7.2 52.4 %all-gather.6.cloned.1.call-start = ((), (), s32[]{:S(2)}) async-start(), calls=%async_computation.5 | async-start | bytes 2949120 | tf_op jit(solution)/shard_map/all_gather | solution.py:44
  11.0 18.8 %copy-start.1 = (bf16[256,2048]{1,0:T(8,128)(2,1)S(1)}, bf16[256,2048]{1,0:T(8,128)(2,1)}, u32[]{:S(2)}) copy-start(bf16[256,2048]{1,0:T(8,128)(2,1)} %param.8) | copy-start | bytes 3145732
  11.0 18.8 %copy-start.2 = (f32[256,1]{0,1:T(1,128)S(1)}, f32[256,1]{0,1:T(1,128)}, u32[]{:S(2)}) copy-start(f32[256,1]{0,1:T(1,128)} %param.10) | copy-start | bytes 3076
  29.8 62.2 %all-gather.4.cloned.1.call-start = ((), (), s32[]{:S(2)}) async-start(), calls=%async_computation.4 | async-start | bytes 2949120 | tf_op jit(solution)/shard_map/all_gather | solution.py:45
  43.1 101.8 %reduce-scatter.2.cloned.1.call-start = ((), (), s32[]{:S(2)}) async-start(), calls=%async_computation.6 | async-start | bytes 2949120 | tf_op jit(solution)/shard_map/reduce_scatter | solution.py:66
  92.0 4.7 %copy-start.4 = (bf16[1,2048,512]{2,1,0:T(8,128)(2,1)S(1)}, bf16[1,2048,512]{2,1,0:T(8,128)(2,1)}, u32[]{:S(2)}) copy-start(bf16[1,2048,512]{2,1,0:T(8,128)(2,1)} %param.12) | copy-start | bytes 6291460
  92.0 4.7 %copy-start.5 = (bf16[1,2048,512]{2,1,0:T(8,128)(2,1)S(1)}, bf16[1,2048,512]{2,1,0:T(8,128)(2,1)}, u32[]{:S(2)}) copy-start(bf16[1,2048,512]{2,1,0:T(8,128)(2,1)} %param.11) | copy-start | bytes 6291460
  101.1 81.6 %all-gather.8.cloned.1.call-start = ((), (), s32[]{:S(2)}) async-start(), calls=%async_computation.7 | async-start | bytes 1179648 | tf_op jit(solution)/shard_map/all_gather | solution.py:71
  160.8 5.8 %copy-start.3 = (bf16[640,2048]{1,0:T(8,128)(2,1)S(1)}, bf16[640,2048]{1,0:T(8,128)(2,1)}, u32[]{:S(2)}) copy-start(bf16[640,2048]{1,0:T(8,128)(2,1)} %all-gather.6.cloned.1.call-done) | copy-start | bytes 7864324
Sparse Core Ops, SparseCore 0:
  29.9 29.6 all-gather.5
  61.4 30.4 all-gather.3
  101.2 43.6 reduce-scatter.1
  160.9 21.6 all-gather.7
where the time goes:
time: 192 us; the launch traced here: 191 us
  waiting for transfers between devices  93.8 us (49%)
  blocking collectives  43.5 us (23%)
  matrix products  31.7 us (17%)
  between operations  13.9 us (7%)
  local copies, waits for them, and re-layouts  4.99 us (3%)
  other arithmetic  3.52 us (2%)
    reduce_scatter x1, waiting for transfers between devices, per_device(): lax.psum_scatter(terms.astype(jnp.bfloat16), 'dp', scatter_dimension=1, t...  43.7 us
    all_gather x1, waiting for transfers between devices, per_device(): lax.all_gather(got_scaled, 'dp', axis=1, tiled=True)  24.4 us
    all_to_all x1, blocking collectives, per_device(): lax.all_to_all(input_cols, 'expert', split_axis=0, concat_axis=0, tiled=T...  16.5 us
    all_gather x1, waiting for transfers between devices, per_device(): lax.all_gather(got_input, 'dp', axis=1, tiled=True)  16.5 us
    all_to_all x1, blocking collectives, per_device(): lax.all_to_all(summed, 'expert', split_axis=0, concat_axis=0, tiled=True)  14.9 us
    all_to_all x1, blocking collectives, per_device(): lax.all_to_all(scaled_cols, 'expert', split_axis=0, concat_axis=0, tiled=...  12.1 us
    all_gather x1, waiting for transfers between devices, per_device(): grad_tokens = lax.all_gather(token_cols, 'dp', axis=1, tiled=True)  9.11 us
    dot_general x1, matrix products, per_device(): pre_act = jnp.dot(all_inputs, w_pair, preferred_element_type=jnp.float32)  8.03 us
  transfers between devices with their start and end apart: 4, of which 4 were waited for; matrix products, arithmetic and copies ran while one was open for 11% of the time, Pallas kernels for 0%

commit v1 on v0

--- a/solution.py
+++ b/solution.py
@@ -1,7 +1,16 @@
+import functools
 import jax
 import jax.numpy as jnp
 from jax import lax
+from jax.experimental import pallas as pl
+from jax.experimental.pallas import tpu as pltpu
 from jax.sharding import PartitionSpec as P
+
+BF16 = jnp.bfloat16
+F32 = jnp.float32
+LAST = (((1,), (1,)), ((), ()))
+FIRST = (((0,), (0,)), ((), ()))
+VMEM = pltpu.MemorySpace.VMEM
 
 
 def silu_parts(pre_gate):
@@ -9,7 +18,7 @@
     return (pre_gate * sigma, sigma * (1.0 + pre_gate * (1.0 - sigma)))
 
 
-def per_device(tokens, grad_out, expert_ids, gate_prob, w_gate, w_up, w_down):
+def per_device_any(tokens, grad_out, expert_ids, gate_prob, w_gate, w_up, w_down):
     expert_count = lax.axis_size("expert")
     replica_count = lax.axis_size("dp")
     tok_count = tokens.shape[0]
@@ -74,6 +83,270 @@
     return (grad_tokens, gate_wgrad[None], up_wgrad[None], down_grad.astype(jnp.bfloat16)[None])
 
 
+def call(body, outs, operands, flops, limit, scratch=()):
+    nbytes = sum(a.size * a.dtype.itemsize for a in operands)
+    nbytes += sum(o.size * o.dtype.itemsize for o in outs)
+    return pl.pallas_call(
+        body,
+        out_shape=outs,
+        in_specs=[pl.BlockSpec(memory_space=VMEM)] * len(operands),
+        out_specs=[pl.BlockSpec(memory_space=VMEM)] * len(outs),
+        scratch_shapes=list(scratch),
+        compiler_params=pltpu.CompilerParams(vmem_limit_bytes=limit << 20),
+        cost_estimate=pl.CostEstimate(flops=flops, bytes_accessed=nbytes, transcendentals=0),
+    )(*operands)
+
+
+def shape(*dims, dtype=BF16):
+    return jax.ShapeDtypeStruct(dims, dtype)
+
+
+def cols(block, width):
+    return pl.ds(pl.multiple_of(block * width, width), width)
+
+
+def dispatch_kernel(capacity, share, tok, grad, ids, prob, send1, send2, send3, own, back):
+    here = lax.axis_index("expert")
+    block = lax.axis_index("dp")
+    count = tok.shape[0]
+    relative = jnp.bitwise_xor(ids[...], here)
+    lane = lax.broadcasted_iota(jnp.int32, (count, 128), 1)
+    hit = (relative == lane).astype(F32)
+    row = lax.broadcasted_iota(jnp.int32, (count, count), 0)
+    col = lax.broadcasted_iota(jnp.int32, (count, count), 1)
+    earlier = (col < row).astype(BF16)
+    before = jnp.dot(earlier, hit.astype(BF16), preferred_element_type=F32)
+    slot = jnp.sum(before * hit, axis=1, keepdims=True)
+    target = relative.astype(F32) * capacity + slot
+    places = own.shape[0] * 4
+    spots = lax.broadcasted_iota(jnp.int32, (count, places), 1)
+    target_int = target.astype(jnp.int32)
+    back[...] = (target_int == spots).astype(F32).astype(BF16)
+    across = jnp.transpose(jnp.broadcast_to(target, (count, 128)))[0:1, :].astype(jnp.int32)
+    spots_t = lax.broadcasted_iota(jnp.int32, (places, count), 0)
+    assign = (across == spots_t).astype(F32).astype(BF16)
+    own[...] = assign[:capacity]
+    x_part = tok[:, cols(block, share)]
+    y_part = (prob[...] * grad[:, cols(block, share)].astype(F32)).astype(BF16)
+    for k, ref in ((1, send1), (2, send2), (3, send3)):
+        pick = assign[k * capacity : (k + 1) * capacity]
+        ref[:capacity] = jnp.dot(pick, x_part, preferred_element_type=F32).astype(BF16)
+        ref[capacity:] = jnp.dot(pick, y_part, preferred_element_type=F32).astype(BF16)
+
+
+def expert_math(share, x_all, y_all, w_gate, w_up, w_down, hidden, gate_grad, up_grad, even, odd):
+    block = lax.axis_index("dp")
+    rows = x_all.shape[0]
+    pre_gate = jnp.dot(x_all[...], w_gate[...], preferred_element_type=F32)
+    pre_up = jnp.dot(x_all[...], w_up[...], preferred_element_type=F32)
+    hidden_grad = lax.dot_general(y_all[...], w_down[...], LAST, preferred_element_type=F32)
+    activated, slope = silu_parts(pre_gate)
+    hidden[...] = (activated * pre_up).astype(BF16)
+    gate_grad[...] = (hidden_grad * pre_up * slope).astype(BF16)
+    up_grad[...] = (hidden_grad * activated).astype(BF16)
+    for k in range(8):
+        piece = cols(jnp.bitwise_xor(block, k), share)
+        term = lax.dot_general(gate_grad[...], w_gate[piece, :], LAST, preferred_element_type=F32)
+        term += lax.dot_general(up_grad[...], w_up[piece, :], LAST, preferred_element_type=F32)
+        (odd if k % 2 else even)[k // 2] = term.astype(BF16)
+
+
+def own_kernel(share, tok, grad, prob, own, w_gate, w_up, w_down, x_all, y_all, *rest):
+    scaled = (prob[...] * grad[...].astype(F32)).astype(BF16)
+    x_all[...] = jnp.dot(own[...], tok[...], preferred_element_type=F32).astype(BF16)
+    y_all[...] = jnp.dot(own[...], scaled, preferred_element_type=F32).astype(BF16)
+    expert_math(share, x_all, y_all, w_gate, w_up, w_down, *rest)
+
+
+def chunk_kernel(share, *refs):
+    blocks, halves, rest = refs[:6], refs[6:10], refs[10:]
+    w_gate, w_up, w_down, x_all, y_all = rest[:5]
+    block = lax.axis_index("dp")
+    rows = x_all.shape[0]
+    for k, ref in enumerate(blocks):
+        piece = cols(jnp.bitwise_xor(block, k), share)
+        x_all[:, piece] = ref[:rows]
+        y_all[:, piece] = ref[rows:]
+    for k in (6, 7):
+        piece = cols(jnp.bitwise_xor(block, k), share)
+        x_all[:, piece] = halves[2 * (k - 6)][...]
+        y_all[:, piece] = halves[2 * (k - 6) + 1][...]
+    expert_math(share, x_all, y_all, w_gate, w_up, w_down, *rest[5:])
+
+
+def pair_wgrad_kernel(x0, x1, x2, g0, g1, g2, u0, u1, u2, gate_out, up_out):
+    gate = 0.0
+    up = 0.0
+    for x, g, u in ((x0, g0, u0), (x1, g1, u1), (x2, g2, u2)):
+        gate += lax.dot_general(x[...], g[...], FIRST, preferred_element_type=F32)
+        up += lax.dot_general(x[...], u[...], FIRST, preferred_element_type=F32)
+    gate_out[...] = gate.astype(BF16)
+    up_out[...] = up.astype(BF16)
+
+
+def wgrad_kernel(a0, a1, a2, b0, b1, b2, out):
+    total = lax.dot_general(a0[...], b0[...], FIRST, preferred_element_type=F32)
+    total += lax.dot_general(a1[...], b1[...], FIRST, preferred_element_type=F32)
+    total += lax.dot_general(a2[...], b2[...], FIRST, preferred_element_type=F32)
+    out[...] = total.astype(BF16)
+
+
+def combine_kernel(back, r0, r1, r2, r3, out, rows):
+    capacity = r0.shape[0]
+    for k, ref in enumerate((r0, r1, r2, r3)):
+        rows[k * capacity : (k + 1) * capacity] = ref[...]
+    out[...] = jnp.dot(back[...], rows[...], preferred_element_type=F32).astype(BF16)
+
+
+def place_kernel(share, *refs):
+    out = refs[-1]
+    block = lax.axis_index("dp")
+    half = out.shape[0] // 2
+    for k, ref in enumerate(refs[:6]):
+        out[:, cols(jnp.bitwise_xor(block, k), share)] = ref[...]
+    for k in (6, 7):
+        piece = cols(jnp.bitwise_xor(block, k), share)
+        out[:half, piece] = refs[2 * k - 6][...]
+        out[half:, piece] = refs[2 * k - 5][...]
+
+
+def swap(array, axis, distance):
+    size = lax.axis_size(axis)
+    return lax.ppermute(array, axis, [(i, i ^ distance) for i in range(size)])
+
+
+def gather_blocks(block):
+    half = block.shape[0] // 2
+    by_two = swap(block, "dp", 2)
+    by_four = swap(block, "dp", 4)
+    first = swap(by_two[:half], "dp", 4)
+    second = swap(by_four[half:], "dp", 2)
+    return (
+        block,
+        swap(block, "dp", 1),
+        by_two,
+        swap(by_two, "dp", 1),
+        by_four,
+        swap(by_four, "dp", 1),
+        first,
+        second,
+        swap(first, "dp", 1),
+        swap(second, "dp", 1),
+    )
+
+
+def scatter_blocks(even, odd):
+    other = swap(odd, "dp", 1)
+    pair = [(even[j].astype(F32) + other[j].astype(F32)).astype(BF16) for j in range(4)]
+    total = pair[0].astype(F32)
+    for j in range(1, 4):
+        total += swap(pair[j], "dp", 2 * j).astype(F32)
+    return total.astype(BF16)
+
+
+def expert_outs(rows, width, hidden, share):
+    return [
+        shape(rows, width),
+        shape(rows, width),
+        shape(rows, hidden),
+        shape(rows, hidden),
+        shape(rows, hidden),
+        shape(4, rows, share),
+        shape(4, rows, share),
+    ]
+
+
+def per_device_blocks(tokens, grad_out, expert_ids, gate_prob, w_gate, w_up, w_down):
+    count, width = tokens.shape
+    experts = lax.axis_size("expert")
+    share = width // lax.axis_size("dp")
+    capacity = max(2, (5 * count + 2 * experts - 1) // (2 * experts))
+    hidden_part = w_gate.shape[2]
+    weights = (w_gate[0], w_up[0], w_down[0])
+
+    send1, send2, send3, own, back = call(
+        functools.partial(dispatch_kernel, capacity, share),
+        [shape(2 * capacity, share)] * 3
+        + [shape(capacity, count), shape(count, experts * capacity)],
+        (tokens, grad_out, expert_ids, gate_prob),
+        4 * 3 * capacity * count * share,
+        8,
+    )
+    got1 = swap(send1, "expert", 1)
+    got3 = swap(send3, "expert", 3)
+    got2 = swap(send2, "expert", 2)
+
+    def math_flops(rows):
+        return 10 * rows * width * hidden_part
+
+    own_out = call(
+        functools.partial(own_kernel, share),
+        expert_outs(capacity, width, hidden_part, share),
+        (tokens, grad_out, gate_prob, own) + weights,
+        math_flops(capacity),
+        16,
+    )
+    ret0 = scatter_blocks(own_out[5], own_out[6])
+
+    block_a = jnp.concatenate(
+        [got1[:capacity], got3[:capacity], got1[capacity:], got3[capacity:]], axis=0
+    )
+    blocks_a = gather_blocks(block_a)
+    out_a = call(
+        functools.partial(chunk_kernel, share),
+        expert_outs(2 * capacity, width, hidden_part, share),
+        blocks_a + weights,
+        math_flops(2 * capacity),
+        16,
+    )
+    summed_a = scatter_blocks(out_a[5], out_a[6])
+    ret1 = swap(summed_a[:capacity], "expert", 1)
+    ret3 = swap(summed_a[capacity:], "expert", 3)
+
+    blocks_b = gather_blocks(got2)
+    out_b = call(
+        functools.partial(chunk_kernel, share),
+        expert_outs(capacity, width, hidden_part, share),
+        blocks_b + weights,
+        math_flops(capacity),
+        16,
+    )
+    ret2 = swap(scatter_blocks(out_b[5], out_b[6]), "expert", 2)
+
+    (token_cols,) = call(
+        combine_kernel,
+        [shape(count, share)],
+        (back, ret0, ret1, ret2, ret3),
+        2 * count * experts * capacity * share,
+        8,
+        [pltpu.VMEM((experts * capacity, share), BF16)],
+    )
+    (grad_tokens,) = call(
+        functools.partial(place_kernel, share),
+        [shape(count, width)],
+        gather_blocks(token_cols),
+        count * width,
+        8,
+    )
+    parts = (own_out, out_a, out_b)
+    rows_all = experts * capacity
+    gate_wgrad, up_wgrad = call(
+        pair_wgrad_kernel,
+        [shape(width, hidden_part)] * 2,
+        [o[0] for o in parts] + [o[3] for o in parts] + [o[4] for o in parts],
+        4 * rows_all * width * hidden_part,
+        24,
+    )
+    (down_wgrad,) = call(
+        wgrad_kernel,
+        [shape(hidden_part, width)],
+        [o[2] for o in parts] + [o[1] for o in parts],
+        2 * rows_all * width * hidden_part,
+        16,
+    )
+    return (grad_tokens, gate_wgrad[None], up_wgrad[None], down_wgrad[None])
+
+
 def solution(mesh):
     placed = (
         P("expert", None),
@@ -84,8 +357,9 @@
         P("expert", None, "dp"),
         P("expert", "dp", None),
     )
+    fits = mesh.shape["dp"] == 8 and mesh.shape["expert"] == 4
     return jax.shard_map(
-        per_device,
+        per_device_blocks if fits else per_device_any,
         mesh=mesh,
         in_specs=placed,
         out_specs=(

time: 192 us -> 110 us (0.57)
  waiting for transfers between devices: 93.8 us -> 32.6 us
  starting transfers between devices: 0.16 us -> 44.7 us
  blocking collectives: 43.5 us -> 0 us
  matrix products: 31.7 us -> 0 us
  Pallas kernels: 0 us -> 22.5 us
  between operations: 13.9 us -> 0.86 us
  local copies, waits for them, and re-layouts: 4.99 us -> 8.19 us
  other arithmetic: 3.52 us -> 0.47 us
    all_gather x3 -> x0, waiting for transfers between devices: 50 us -> none  [the longest x1 24.4 us: per_device(): lax.all_gather(got_scaled, 'dp', axis=1, tiled=True)]
    ppermute x0 -> x45, starting transfers between devices: none -> 44.7 us  [swap(): return lax.ppermute(array, axis, [(i, i ^ distance) for i in range(size)])]
    reduce_scatter x1 -> x0, waiting for transfers between devices: 43.7 us -> none  [per_device(): lax.psum_scatter(terms.astype(jnp.bfloat16), 'dp', scatter_dimension=1, t...]
    all_to_all x3 -> x0, blocking collectives: 43.5 us -> none  [the longest x1 16.5 us: per_device(): lax.all_to_all(input_cols, 'expert', split_axis=0, concat_axis=0, tiled=T...]
    ppermute x0 -> x45, waiting for transfers between devices: none -> 32.6 us  [swap(): return lax.ppermute(array, axis, [(i, i ^ distance) for i in range(size)])]
    dot_general x8 -> x0, matrix products: 31.7 us -> none  [the longest x1 8.03 us: per_device(): pre_act = jnp.dot(all_inputs, w_pair, preferred_element_type=jnp.float32)]
    pallas_call x0 -> x8, Pallas kernels: none -> 22.5 us  [call(): pl.pallas_call(body, out_shape=outs, in_specs=[pl.BlockSpec(memory_space=...]
    unnamed x13 -> x18, local copies, waits for them, and re-layouts: 2.33 us -> 8.11 us
  transfers between devices with their start and end apart: 4 -> 45, of which waited for: 4 -> 18; matrix products, arithmetic and copies ran while one was open for 11% -> 1% of each run, Pallas kernels for 0% -> 19%
where the time goes in v1:
time: 110 us; the launch traced here: 109 us
  starting transfers between devices  44.7 us (41%)
  waiting for transfers between devices  32.6 us (30%)
  Pallas kernels  22.5 us (20%)
  local copies, waits for them, and re-layouts  8.19 us (7%)
    ppermute x45, starting transfers between devices, swap(): return lax.ppermute(array, axis, [(i, i ^ distance) for i in range(size)])  44.7 us
    ppermute x45, waiting for transfers between devices, swap(): return lax.ppermute(array, axis, [(i, i ^ distance) for i in range(size)])  32.6 us
    pallas_call x8, Pallas kernels, call(): pl.pallas_call(body, out_shape=outs, in_specs=[pl.BlockSpec(memory_space=...  22.5 us
    unnamed x18, local copies, waits for them, and re-layouts  8.11 us
  transfers between devices with their start and end apart: 45, of which 18 were waited for; matrix products, arithmetic and copies ran while one was open for 1% of the time, Pallas kernels for 19%

profile of v1, /device:TPU:0, one launch (start us, length us, event | category | flops | bytes accessed | tf_op | source)
XLA Modules:
  0.0 109.4 jit_solution(4951613302877901178)
XLA Ops:
  1.4 0.8 copy.11.ids
  2.3 1.2 %copy-done.4 = bf16[256,2048]{1,0:T(8,128)(2,1)S(1)} copy-done((bf16[256,2048]{1,0:T(8,128)(2,1)S(1)}, bf16[256,2048]{1,0:T(8,128)(2,1)}, u32[]{:S(2)}) %copy-start.4) | copy-done | bytes 1048600
  3.5 1.2 %copy-done.6 = bf16[256,2048]{1,0:T(8,128)(2,1)S(1)} copy-done((bf16[256,2048]{1,0:T(8,128)(2,1)S(1)}, bf16[256,2048]{1,0:T(8,128)(2,1)}, u32[]{:S(2)}) %copy-start.6) | copy-done | bytes 1048600
  4.7 0.8 shard_map.102
  5.6 3.1 %collective-permute-start.4 = (bf16[320,256]{1,0:T(8,128)(2,1)S(1)}, bf16[320,256]{1,0:T(8,128)(2,1)S(1)}, u32[]{:S(2)}, u32[]{:S(2)}) collective-permute-start(bf16[320,256]{1,0:T(8,128)(2,1)S(1)} %get-tuple-element.36), channel_id=1, source_target_pairs={{0,1},{1,0},{2,3},{3,2},{4,5},{5,4},{6,7},{7,6},{8,9},{9,8},{10,11... | collective-permute-start | bytes 491528 | tf_op jit(solution)/shard_map/ppermute | solution.py:215
  8.7 2.5 %collective-permute-start.5 = (bf16[320,256]{1,0:T(8,128)(2,1)S(1)}, bf16[320,256]{1,0:T(8,128)(2,1)S(1)}, u32[]{:S(2)}, u32[]{:S(2)}) collective-permute-start(bf16[320,256]{1,0:T(8,128)(2,1)S(1)} %get-tuple-element.37), channel_id=1, source_target_pairs={{0,3},{1,2},{2,1},{3,0},{4,7},{5,6},{6,5},{7,4},{8,11},{9,10},{10,... | collective-permute-start | bytes 491528 | tf_op jit(solution)/shard_map/ppermute | solution.py:215
  11.3 2.0 %collective-permute-done.4 = bf16[320,256]{1,0:T(8,128)(2,1)S(1)} collective-permute-done((bf16[320,256]{1,0:T(8,128)(2,1)S(1)}, bf16[320,256]{1,0:T(8,128)(2,1)S(1)}, u32[]{:S(2)}, u32[]{:S(2)}) %collective-permute-start.4) | collective-permute-done | bytes 163872 | tf_op jit(solution)/shard_map/ppermute | solution.py:215
  13.3 6.5 %collective-permute-done.5 = bf16[320,256]{1,0:T(8,128)(2,1)S(1)} collective-permute-done((bf16[320,256]{1,0:T(8,128)(2,1)S(1)}, bf16[320,256]{1,0:T(8,128)(2,1)S(1)}, u32[]{:S(2)}, u32[]{:S(2)}) %collective-permute-start.5) | collective-permute-done | bytes 163872 | tf_op jit(solution)/shard_map/ppermute | solution.py:215
  19.9 1.6 %collective-permute-start.9 = (bf16[640,256]{1,0:T(8,128)(2,1)S(1)}, bf16[640,256]{1,0:T(8,128)(2,1)S(1)}, u32[]{:S(2)}, u32[]{:S(2)}) collective-permute-start(bf16[640,256]{1,0:T(8,128)(2,1)S(1)} %pad_maximum_fusion.refs_0_), channel_id=1, source_target_pairs={{0,16},{4,20},{8,24},{12,28},{16,0},{20,4},{24,8},{28,12},{1,17},{... | collective-permute-start | bytes 983048 | tf_op jit(solution)/shard_map/ppermute | solution.py:215
  21.4 1.5 %collective-permute-start.7 = (bf16[640,256]{1,0:T(8,128)(2,1)S(1)}, bf16[640,256]{1,0:T(8,128)(2,1)S(1)}, u32[]{:S(2)}, u32[]{:S(2)}) collective-permute-start(bf16[640,256]{1,0:T(8,128)(2,1)S(1)} %pad_maximum_fusion.refs_0_), channel_id=1, source_target_pairs={{0,8},{4,12},{8,0},{12,4},{16,24},{20,28},{24,16},{28,20},{1,9},{5... | collective-permute-start | bytes 983048 | tf_op jit(solution)/shard_map/ppermute | solution.py:215
  22.9 2.8 %collective-permute-done.20.refs_0_ = bf16[320,256]{1,0:T(8,128)(2,1)S(1)} collective-permute-done((bf16[320,256]{1,0:T(8,128)(2,1)S(1)}, bf16[320,256]{1,0:T(8,128)(2,1)S(1)}, u32[]{:S(2)}, u32[]{:S(2)}) %collective-permute-start.20) | collective-permute-done | bytes 163872 | tf_op jit(solution)/shard_map/ppermute | solution.py:215
  25.7 1.5 %collective-permute-start.24 = (bf16[320,256]{1,0:T(8,128)(2,1)S(1)}, bf16[320,256]{1,0:T(8,128)(2,1)S(1)}, u32[]{:S(2)}, u32[]{:S(2)}) collective-permute-start(bf16[320,256]{1,0:T(8,128)(2,1)S(1)} %collective-permute-done.20.refs_0_), channel_id=1, source_target_pairs={{0,16},{4,20},{8,24},{12,28},{16,0},{20,4},{24,8},{28,12},{1,17},{... | collective-permute-start | bytes 491528 | tf_op jit(solution)/shard_map/ppermute | solution.py:215
  27.2 1.5 %collective-permute-start.22 = (bf16[320,256]{1,0:T(8,128)(2,1)S(1)}, bf16[320,256]{1,0:T(8,128)(2,1)S(1)}, u32[]{:S(2)}, u32[]{:S(2)}) collective-permute-start(bf16[320,256]{1,0:T(8,128)(2,1)S(1)} %collective-permute-done.20.refs_0_), channel_id=1, source_target_pairs={{0,8},{4,12},{8,0},{12,4},{16,24},{20,28},{24,16},{28,20},{1,9},{5... | collective-permute-start | bytes 491528 | tf_op jit(solution)/shard_map/ppermute | solution.py:215
  28.7 2.3 %collective-permute-done.24.refs_4_ = bf16[320,256]{1,0:T(8,128)(2,1)S(1)} collective-permute-done((bf16[320,256]{1,0:T(8,128)(2,1)S(1)}, bf16[320,256]{1,0:T(8,128)(2,1)S(1)}, u32[]{:S(2)}, u32[]{:S(2)}) %collective-permute-start.24) | collective-permute-done | bytes 163872 | tf_op jit(solution)/shard_map/ppermute | solution.py:215
  31.0 1.5 %collective-permute-start.27 = (bf16[160,256]{1,0:T(8,128)(2,1)S(1)}, bf16[160,256]{1,0:T(8,128)(2,1)S(1)}, u32[]{:S(2)}, u32[]{:S(2)}) collective-permute-start(bf16[160,256]{1,0:T(8,128)(2,1)S(1)} %slice.160), channel_id=1, source_target_pairs={{0,8},{4,12},{8,0},{12,4},{16,24},{20,28},{24,16},{28,20},{1,9},{5... | collective-permute-start | bytes 245768 | tf_op jit(solution)/shard_map/ppermute | solution.py:215
  33.2 0.9 collective-permute-start.26
  34.1 1.0 collective-permute-start.12
  35.5 1.9 %collective-permute-start.11 = (bf16[320,256]{1,0:T(8,128)(2,1)S(1)}, bf16[320,256]{1,0:T(8,128)(2,1)S(1)}, u32[]{:S(2)}, u32[]{:S(2)}) collective-permute-start(bf16[320,256]{1,0:T(8,128)(2,1)S(1)} %slice.152), channel_id=1, source_target_pairs={{0,16},{4,20},{8,24},{12,28},{16,0},{20,4},{24,8},{28,12},{1,17},{... | collective-permute-start | bytes 491528 | tf_op jit(solution)/shard_map/ppermute | solution.py:215
  37.6 3.2 %collective-permute-done.12.refs_7_ = bf16[320,256]{1,0:T(8,128)(2,1)S(1)} collective-permute-done((bf16[320,256]{1,0:T(8,128)(2,1)S(1)}, bf16[320,256]{1,0:T(8,128)(2,1)S(1)}, u32[]{:S(2)}, u32[]{:S(2)}) %collective-permute-start.12) | collective-permute-done | bytes 163872 | tf_op jit(solution)/shard_map/ppermute | solution.py:215
  40.8 1.2 %collective-permute-done.11.refs_6_ = bf16[320,256]{1,0:T(8,128)(2,1)S(1)} collective-permute-done((bf16[320,256]{1,0:T(8,128)(2,1)S(1)}, bf16[320,256]{1,0:T(8,128)(2,1)S(1)}, u32[]{:S(2)}, u32[]{:S(2)}) %collective-permute-start.11) | collective-permute-done | bytes 163872 | tf_op jit(solution)/shard_map/ppermute | solution.py:215
  42.0 1.6 %copy-done.2 = bf16[1,512,2048]{2,1,0:T(8,128)(2,1)S(1)} copy-done((bf16[1,512,2048]{2,1,0:T(8,128)(2,1)S(1)}, bf16[1,512,2048]{2,1,0:T(8,128)(2,1)}, u32[]{:S(2)}) %copy-start.2) | copy-done | bytes 2097176
  43.6 1.2 %copy-done.5 = bf16[256,2048]{1,0:T(8,128)(2,1)S(1)} copy-done((bf16[256,2048]{1,0:T(8,128)(2,1)S(1)}, bf16[256,2048]{1,0:T(8,128)(2,1)}, u32[]{:S(2)}) %copy-start.5) | copy-done | bytes 1048600
  44.8 1.2 %copy-done.7 = bf16[256,2048]{1,0:T(8,128)(2,1)S(1)} copy-done((bf16[256,2048]{1,0:T(8,128)(2,1)S(1)}, bf16[256,2048]{1,0:T(8,128)(2,1)}, u32[]{:S(2)}) %copy-start.7) | copy-done | bytes 1048600
  46.1 3.3 %shard_map.103 = (bf16[160,2048]{1,0:T(8,128)(2,1)S(1)}, bf16[160,2048]{1,0:T(8,128)(2,1)S(1)}, bf16[160,512]{1,0:T(8,128)(2,1)S(1)}, bf16[160,512]{1,0:T(8,128)...) custom-call(bf16[256,2048]{1,0:T(8,128)(2,1)S(1)} %copy-done.5, ...), custom_call_target="tpu_custom_call" | custom-call | flops 1677721600 | bytes 10929152 | tf_op jit(solution)/shard_map/pallas_call | solution.py:89
  51.0 4.0 %shard_map.104 = (bf16[320,2048]{1,0:T(8,128)(2,1)S(1)}, bf16[320,2048]{1,0:T(8,128)(2,1)S(1)}, bf16[320,512]{1,0:T(8,128)(2,1)S(1)}, bf16[320,512]{1,0:T(8,128)...) custom-call(bf16[640,256]{1,0:T(8,128)(2,1)S(1)} %pad_maximum_fusion.ref, ...), custom_call_target="tpu_custom_call" | custom-call | flops 3355443200 | bytes 13828096 | tf_op jit(solution)/shard_map/pallas_call | solution.py:89
  55.2 3.0 %shard_map.105 = (bf16[160,2048]{1,0:T(8,128)(2,1)S(1)}, bf16[160,2048]{1,0:T(8,128)(2,1)S(1)}, bf16[160,512]{1,0:T(8,128)(2,1)S(1)}, bf16[160,512]{1,0:T(8,128)...) custom-call(bf16[320,256]{1,0:T(8,128)(2,1)S(1)} %collective-permute-don, ...), custom_call_target="tpu_custom_call" | custom-call | flops 1677721600 | bytes 10059776 | tf_op jit(solution)/shard_map/pallas_call | solution.py:89
  58.8 1.0 collective-permute-start.1
  59.8 2.3 %collective-permute-start.3 = (bf16[160,256]{1,0:T(8,128)(2,1)S(1)}, bf16[160,256]{1,0:T(8,128)(2,1)S(1)}, u32[]{:S(2)}, u32[]{:S(2)}) collective-permute-start(bf16[160,256]{1,0:T(8,128)(2,1)S(1)} %get-tuple-element.67), channel_id=1, source_target_pairs={{0,24},{4,28},{8,16},{12,20},{16,8},{20,12},{24,0},{28,4},{1,25},{... | collective-permute-start | bytes 245768 | tf_op jit(solution)/shard_map/ppermute | solution.py:215
  62.5 1.5 %collective-permute-start.33 = (bf16[160,256]{1,0:T(8,128)(2,1)S(1)}, bf16[160,256]{1,0:T(8,128)(2,1)S(1)}, u32[]{:S(2)}, u32[]{:S(2)}) collective-permute-start(bf16[160,256]{1,0:T(8,128)(2,1)S(1)} %get-tuple-element.64), channel_id=1, source_target_pairs={{0,24},{4,28},{8,16},{12,20},{16,8},{20,12},{24,0},{28,4},{1,25},{... | collective-permute-start | bytes 245768 | tf_op jit(solution)/shard_map/ppermute | solution.py:215
  64.0 1.7 %collective-permute-start.32 = (bf16[160,256]{1,0:T(8,128)(2,1)S(1)}, bf16[160,256]{1,0:T(8,128)(2,1)S(1)}, u32[]{:S(2)}, u32[]{:S(2)}) collective-permute-start(bf16[160,256]{1,0:T(8,128)(2,1)S(1)} %get-tuple-element.65), channel_id=1, source_target_pairs={{0,16},{4,20},{8,24},{12,28},{16,0},{20,4},{24,8},{28,12},{1,17},{... | collective-permute-start | bytes 245768 | tf_op jit(solution)/shard_map/ppermute | solution.py:215
  65.8 1.8 %collective-permute-done.31 = bf16[160,256]{1,0:T(8,128)(2,1)S(1)} collective-permute-done((bf16[160,256]{1,0:T(8,128)(2,1)S(1)}, bf16[160,256]{1,0:T(8,128)(2,1)S(1)}, u32[]{:S(2)}, u32[]{:S(2)}) %collective-permute-start.31) | collective-permute-done | bytes 81952 | tf_op jit(solution)/shard_map/ppermute | solution.py:215
  67.6 1.3 %collective-permute-start.16 = (bf16[320,256]{1,0:T(8,128)(2,1)S(1)}, bf16[320,256]{1,0:T(8,128)(2,1)S(1)}, u32[]{:S(2)}, u32[]{:S(2)}) collective-permute-start(bf16[320,256]{1,0:T(8,128)(2,1)S(1)} %get-tuple-element.60), channel_id=1, source_target_pairs={{0,8},{4,12},{8,0},{12,4},{16,24},{20,28},{24,16},{28,20},{1,9},{5... | collective-permute-start | bytes 491528 | tf_op jit(solution)/shard_map/ppermute | solution.py:215
  68.9 1.0 collective-permute-done.33
  69.9 1.0 collective-permute-start.18
  71.7 2.7 %collective-permute-done.16 = bf16[320,256]{1,0:T(8,128)(2,1)S(1)} collective-permute-done((bf16[320,256]{1,0:T(8,128)(2,1)S(1)}, bf16[320,256]{1,0:T(8,128)(2,1)S(1)}, u32[]{:S(2)}, u32[]{:S(2)}) %collective-permute-start.16) | collective-permute-done | bytes 163872 | tf_op jit(solution)/shard_map/ppermute | solution.py:215
  74.4 2.0 %collective-permute-start.2 = (bf16[160,256]{1,0:T(8,128)(2,1)S(1)}, bf16[160,256]{1,0:T(8,128)(2,1)S(1)}, u32[]{:S(2)}, u32[]{:S(2)}) collective-permute-start(bf16[160,256]{1,0:T(8,128)(2,1)S(1)} %get-tuple-element.68), channel_id=1, source_target_pairs={{0,16},{4,20},{8,24},{12,28},{16,0},{20,4},{24,8},{28,12},{1,17},{... | collective-permute-start | bytes 245768 | tf_op jit(solution)/shard_map/ppermute | solution.py:215
  76.4 1.4 %collective-permute-done.18 = bf16[320,256]{1,0:T(8,128)(2,1)S(1)} collective-permute-done((bf16[320,256]{1,0:T(8,128)(2,1)S(1)}, bf16[320,256]{1,0:T(8,128)(2,1)S(1)}, u32[]{:S(2)}, u32[]{:S(2)}) %collective-permute-start.18) | collective-permute-done | bytes 163872 | tf_op jit(solution)/shard_map/ppermute | solution.py:215
  77.8 4.7 %collective-permute-start.34 = (bf16[160,256]{1,0:T(8,128)(2,1)S(1)}, bf16[160,256]{1,0:T(8,128)(2,1)S(1)}, u32[]{:S(2)}, u32[]{:S(2)}) collective-permute-start(bf16[160,256]{1,0:T(8,128)(2,1)S(1)} %fusion.9), channel_id=1, source_target_pairs={{0,2},{1,3},{2,0},{3,1},{4,6},{5,7},{6,4},{7,5},{8,10},{9,11},{10,... | collective-permute-start | bytes 245768 | tf_op jit(solution)/shard_map/ppermute | solution.py:215
  82.8 3.2 %collective-permute-start.19 = (bf16[160,256]{1,0:T(8,128)(2,1)S(1)}, bf16[160,256]{1,0:T(8,128)(2,1)S(1)}, u32[]{:S(2)}, u32[]{:S(2)}) collective-permute-start(bf16[160,256]{1,0:T(8,128)(2,1)S(1)} %get-tuple-element.70), channel_id=1, source_target_pairs={{0,1},{1,0},{2,3},{3,2},{4,5},{5,4},{6,7},{7,6},{8,9},{9,8},{10,11... | collective-permute-start | bytes 245768 | tf_op jit(solution)/shard_map/ppermute | solution.py:215
  86.0 1.4 %collective-permute-done.34.r2 = bf16[160,256]{1,0:T(8,128)(2,1)S(1)} collective-permute-done((bf16[160,256]{1,0:T(8,128)(2,1)S(1)}, bf16[160,256]{1,0:T(8,128)(2,1)S(1)}, u32[]{:S(2)}, u32[]{:S(2)}) %collective-permute-start.34) | collective-permute-done | bytes 81952 | tf_op jit(solution)/shard_map/ppermute | solution.py:215
  87.4 1.7 %collective-permute-done.35.r3 = bf16[160,256]{1,0:T(8,128)(2,1)S(1)} collective-permute-done((bf16[160,256]{1,0:T(8,128)(2,1)S(1)}, bf16[160,256]{1,0:T(8,128)(2,1)S(1)}, u32[]{:S(2)}, u32[]{:S(2)}) %collective-permute-start.35) | collective-permute-done | bytes 81952 | tf_op jit(solution)/shard_map/ppermute | solution.py:215
  89.5 0.9 collective-permute-start.39
  90.4 1.2 %collective-permute-start.37 = (bf16[256,256]{1,0:T(8,128)(2,1)S(1)}, bf16[256,256]{1,0:T(8,128)(2,1)S(1)}, u32[]{:S(2)}, u32[]{:S(2)}) collective-permute-start(bf16[256,256]{1,0:T(8,128)(2,1)S(1)} %shard_map.106.refs_0_), channel_id=1, source_target_pairs={{0,8},{4,12},{8,0},{12,4},{16,24},{20,28},{24,16},{28,20},{1,9},{5... | collective-permute-start | bytes 393224 | tf_op jit(solution)/shard_map/ppermute | solution.py:215
  91.6 2.9 %collective-permute-done.39.refs_4_ = bf16[256,256]{1,0:T(8,128)(2,1)S(1)} collective-permute-done((bf16[256,256]{1,0:T(8,128)(2,1)S(1)}, bf16[256,256]{1,0:T(8,128)(2,1)S(1)}, u32[]{:S(2)}, u32[]{:S(2)}) %collective-permute-start.39) | collective-permute-done | bytes 131104 | tf_op jit(solution)/shard_map/ppermute | solution.py:215
  95.9 1.4 %collective-permute-start.41 = (bf16[128,256]{1,0:T(8,128)(2,1)S(1)}, bf16[128,256]{1,0:T(8,128)(2,1)S(1)}, u32[]{:S(2)}, u32[]{:S(2)}) collective-permute-start(bf16[128,256]{1,0:T(8,128)(2,1)S(1)} %slice.166), channel_id=1, source_target_pairs={{0,16},{4,20},{8,24},{12,28},{16,0},{20,4},{24,8},{28,12},{1,17},{... | collective-permute-start | bytes 196616 | tf_op jit(solution)/shard_map/ppermute | solution.py:215
  97.8 6.2 %shard_map.108 = (bf16[2048,512]{1,0:T(8,128)(2,1)}, bf16[2048,512]{1,0:T(8,128)(2,1)}) custom-call(bf16[160,2048]{1,0:T(8,128)(2,1)S(1)} %get-tuple-element.43.x0, bf16[320,2048]{1,0:T(8,128)(2,1)S(1)} %get-tuple-element.44.x1, bf16[160,2048]{1,0:T(8,128)(2,1)S(1)} %get-tuple-element.45.x2, bf16[160,512]{1,0:T(8,128)(2,1)S(1)} %get-tuple-element.46.g0, ...), custom_call_target="tpu_custom_call" | custom-call | flops 2684354560 | bytes 8126464 | tf_op jit(solution)/shard_map/pallas_call | solution.py:89
  104.6 3.7 %shard_map.109 = bf16[512,2048]{1,0:T(8,128)(2,1)} custom-call(bf16[160,512]{1,0:T(8,128)(2,1)S(1)} %get-tuple-element.54.a0, bf16[320,512]{1,0:T(8,128)(2,1)S(1)} %get-tuple-element.55.a1, bf16[160,512]{1,0:T(8,128)(2,1)S(1)} %get-tuple-element.56.a2, bf16[160,2048]{1,0:T(8,128)(2,1)S(1)} %get-tuple-element.57.b0, ...), custom_call_target="tpu_custom_call" | custom-call | flops 1342177280 | bytes 5373952 | tf_op jit(solution)/shard_map/pallas_call | solution.py:89
  108.3 1.1 %shard_map.107 = bf16[256,2048]{1,0:T(8,128)(2,1)} custom-call(bf16[256,256]{1,0:T(8,128)(2,1)S(1)} %shard_map.106.refs_0_, bf16[256,256]{1,0:T(8,128)(2,1)S(1)} %collective-permute-done.36.refs_1_, bf16[256,256]{1,0:T(8,128)(2,1)S(1)} %collective-permute-done.37.refs_2_, bf16[256,256]{1,0:T(8,128)(2,1)S(1)} %collective-permute-done.38.refs_3_, ...), custom_call_target="tpu_custom_call" | custom-call | flops 524288 | bytes 2097152 | tf_op jit(solution)/shard_map/pallas_call | solution.py:89
  (84 shorter events, 9.1 us)
Async XLA Ops:
  4.7 37.3 %copy-start = (bf16[1,2048,512]{2,1,0:T(8,128)(2,1)S(1)}, bf16[1,2048,512]{2,1,0:T(8,128)(2,1)}, u32[]{:S(2)}) copy-start(bf16[1,2048,512]{2,1,0:T(8,128)(2,1)} %param.11) | copy-start | bytes 6291460
  4.7 37.3 %copy-start.1 = (bf16[1,2048,512]{2,1,0:T(8,128)(2,1)S(1)}, bf16[1,2048,512]{2,1,0:T(8,128)(2,1)}, u32[]{:S(2)}) copy-start(bf16[1,2048,512]{2,1,0:T(8,128)(2,1)} %param.12) | copy-start | bytes 6291460
  5.6 7.7 %collective-permute-start.4 = (bf16[320,256]{1,0:T(8,128)(2,1)S(1)}, bf16[320,256]{1,0:T(8,128)(2,1)S(1)}, u32[]{:S(2)}, u32[]{:S(2)}) collective-permute-start(bf16[320,256]{1,0:T(8,128)(2,1)S(1)} %get-tuple-element.36), channel_id=1, source_target_pairs={{0,1},{1,0},{2,3},{3,2},{4,5},{5,4},{6,7},{7,6},{8,9},{9,8},{10,11... | collective-permute-start | bytes 491528 | tf_op jit(solution)/shard_map/ppermute | solution.py:215
  8.7 11.1 %collective-permute-start.5 = (bf16[320,256]{1,0:T(8,128)(2,1)S(1)}, bf16[320,256]{1,0:T(8,128)(2,1)S(1)}, u32[]{:S(2)}, u32[]{:S(2)}) collective-permute-start(bf16[320,256]{1,0:T(8,128)(2,1)S(1)} %get-tuple-element.37), channel_id=1, source_target_pairs={{0,3},{1,2},{2,1},{3,0},{4,7},{5,6},{6,5},{7,4},{8,11},{9,10},{10,... | collective-permute-start | bytes 491528 | tf_op jit(solution)/shard_map/ppermute | solution.py:215
  11.1 14.6 %collective-permute-start.20 = (bf16[320,256]{1,0:T(8,128)(2,1)S(1)}, bf16[320,256]{1,0:T(8,128)(2,1)S(1)}, u32[]{:S(2)}, u32[]{:S(2)}) collective-permute-start(bf16[320,256]{1,0:T(8,128)(2,1)S(1)} %get-tuple-element.40), channel_id=1, source_target_pairs={{0,2},{1,3},{2,0},{3,1},{4,6},{5,7},{6,4},{7,5},{8,10},{9,11},{10,... | collective-permute-start | bytes 491528 | tf_op jit(solution)/shard_map/ppermute | solution.py:215
  19.9 14.3 %collective-permute-start.9 = (bf16[640,256]{1,0:T(8,128)(2,1)S(1)}, bf16[640,256]{1,0:T(8,128)(2,1)S(1)}, u32[]{:S(2)}, u32[]{:S(2)}) collective-permute-start(bf16[640,256]{1,0:T(8,128)(2,1)S(1)} %pad_maximum_fusion.refs_0_), channel_id=1, source_target_pairs={{0,16},{4,20},{8,24},{12,28},{16,0},{20,4},{24,8},{28,12},{1,17},{... | collective-permute-start | bytes 983048 | tf_op jit(solution)/shard_map/ppermute | solution.py:215
  21.4 12.7 %collective-permute-start.7 = (bf16[640,256]{1,0:T(8,128)(2,1)S(1)}, bf16[640,256]{1,0:T(8,128)(2,1)S(1)}, u32[]{:S(2)}, u32[]{:S(2)}) collective-permute-start(bf16[640,256]{1,0:T(8,128)(2,1)S(1)} %pad_maximum_fusion.refs_0_), channel_id=1, source_target_pairs={{0,8},{4,12},{8,0},{12,4},{16,24},{20,28},{24,16},{28,20},{1,9},{5... | collective-permute-start | bytes 983048 | tf_op jit(solution)/shard_map/ppermute | solution.py:215
  25.7 5.3 %collective-permute-start.24 = (bf16[320,256]{1,0:T(8,128)(2,1)S(1)}, bf16[320,256]{1,0:T(8,128)(2,1)S(1)}, u32[]{:S(2)}, u32[]{:S(2)}) collective-permute-start(bf16[320,256]{1,0:T(8,128)(2,1)S(1)} %collective-permute-done.20.refs_0_), channel_id=1, source_target_pairs={{0,16},{4,20},{8,24},{12,28},{16,0},{20,4},{24,8},{28,12},{1,17},{... | collective-permute-start | bytes 491528 | tf_op jit(solution)/shard_map/ppermute | solution.py:215
  27.2 6.0 %collective-permute-start.22 = (bf16[320,256]{1,0:T(8,128)(2,1)S(1)}, bf16[320,256]{1,0:T(8,128)(2,1)S(1)}, u32[]{:S(2)}, u32[]{:S(2)}) collective-permute-start(bf16[320,256]{1,0:T(8,128)(2,1)S(1)} %collective-permute-done.20.refs_0_), channel_id=1, source_target_pairs={{0,8},{4,12},{8,0},{12,4},{16,24},{20,28},{24,16},{28,20},{1,9},{5... | collective-permute-start | bytes 491528 | tf_op jit(solution)/shard_map/ppermute | solution.py:215
  28.7 6.4 %collective-permute-start.21 = (bf16[320,256]{1,0:T(8,128)(2,1)S(1)}, bf16[320,256]{1,0:T(8,128)(2,1)S(1)}, u32[]{:S(2)}, u32[]{:S(2)}) collective-permute-start(bf16[320,256]{1,0:T(8,128)(2,1)S(1)} %collective-permute-done.20.refs_0_), channel_id=1, source_target_pairs={{0,4},{4,0},{8,12},{12,8},{16,20},{20,16},{24,28},{28,24},{1,5},{5... | collective-permute-start | bytes 491528 | tf_op jit(solution)/shard_map/ppermute | solution.py:215
  31.0 4.4 %collective-permute-start.27 = (bf16[160,256]{1,0:T(8,128)(2,1)S(1)}, bf16[160,256]{1,0:T(8,128)(2,1)S(1)}, u32[]{:S(2)}, u32[]{:S(2)}) collective-permute-start(bf16[160,256]{1,0:T(8,128)(2,1)S(1)} %slice.160), channel_id=1, source_target_pairs={{0,8},{4,12},{8,0},{12,4},{16,24},{20,28},{24,16},{28,20},{1,9},{5... | collective-permute-start | bytes 245768 | tf_op jit(solution)/shard_map/ppermute | solution.py:215
  33.2 4.4 %collective-permute-start.26 = (bf16[160,256]{1,0:T(8,128)(2,1)S(1)}, bf16[160,256]{1,0:T(8,128)(2,1)S(1)}, u32[]{:S(2)}, u32[]{:S(2)}) collective-permute-start(bf16[160,256]{1,0:T(8,128)(2,1)S(1)} %slice.159), channel_id=1, source_target_pairs={{0,16},{4,20},{8,24},{12,28},{16,0},{20,4},{24,8},{28,12},{1,17},{... | collective-permute-start | bytes 245768 | tf_op jit(solution)/shard_map/ppermute | solution.py:215
  34.1 15.3 %collective-permute-start.6 = (bf16[640,256]{1,0:T(8,128)(2,1)S(1)}, bf16[640,256]{1,0:T(8,128)(2,1)S(1)}, u32[]{:S(2)}, u32[]{:S(2)}) collective-permute-start(bf16[640,256]{1,0:T(8,128)(2,1)S(1)} %pad_maximum_fusion.refs_0_), channel_id=1, source_target_pairs={{0,4},{4,0},{8,12},{12,8},{16,20},{20,16},{24,28},{28,24},{1,5},{5... | collective-permute-start | bytes 983048 | tf_op jit(solution)/shard_map/ppermute | solution.py:215
  34.1 6.7 %collective-permute-start.12 = (bf16[320,256]{1,0:T(8,128)(2,1)S(1)}, bf16[320,256]{1,0:T(8,128)(2,1)S(1)}, u32[]{:S(2)}, u32[]{:S(2)}) collective-permute-start(bf16[320,256]{1,0:T(8,128)(2,1)S(1)} %slice.153), channel_id=1, source_target_pairs={{0,8},{4,12},{8,0},{12,4},{16,24},{20,28},{24,16},{28,20},{1,9},{5... | collective-permute-start | bytes 491528 | tf_op jit(solution)/shard_map/ppermute | solution.py:215
  35.1 14.9 %collective-permute-start.10 = (bf16[640,256]{1,0:T(8,128)(2,1)S(1)}, bf16[640,256]{1,0:T(8,128)(2,1)S(1)}, u32[]{:S(2)}, u32[]{:S(2)}) collective-permute-start(bf16[640,256]{1,0:T(8,128)(2,1)S(1)} %collective-permute-done.9.refs_4_), channel_id=1, source_target_pairs={{0,4},{4,0},{8,12},{12,8},{16,20},{20,16},{24,28},{28,24},{1,5},{5... | collective-permute-start | bytes 983048 | tf_op jit(solution)/shard_map/ppermute | solution.py:215
  35.5 6.5 %collective-permute-start.11 = (bf16[320,256]{1,0:T(8,128)(2,1)S(1)}, bf16[320,256]{1,0:T(8,128)(2,1)S(1)}, u32[]{:S(2)}, u32[]{:S(2)}) collective-permute-start(bf16[320,256]{1,0:T(8,128)(2,1)S(1)} %slice.152), channel_id=1, source_target_pairs={{0,16},{4,20},{8,24},{12,28},{16,0},{20,4},{24,8},{28,12},{1,17},{... | collective-permute-start | bytes 491528 | tf_op jit(solution)/shard_map/ppermute | solution.py:215
  37.6 13.0 %collective-permute-start.8 = (bf16[640,256]{1,0:T(8,128)(2,1)S(1)}, bf16[640,256]{1,0:T(8,128)(2,1)S(1)}, u32[]{:S(2)}, u32[]{:S(2)}) collective-permute-start(bf16[640,256]{1,0:T(8,128)(2,1)S(1)} %collective-permute-done.7.refs_2_), channel_id=1, source_target_pairs={{0,4},{4,0},{8,12},{12,8},{16,20},{20,16},{24,28},{28,24},{1,5},{5... | collective-permute-start | bytes 983048 | tf_op jit(solution)/shard_map/ppermute | solution.py:215
  40.8 9.2 %collective-permute-start.14 = (bf16[320,256]{1,0:T(8,128)(2,1)S(1)}, bf16[320,256]{1,0:T(8,128)(2,1)S(1)}, u32[]{:S(2)}, u32[]{:S(2)}) collective-permute-start(bf16[320,256]{1,0:T(8,128)(2,1)S(1)} %collective-permute-done.12.refs_7_), channel_id=1, source_target_pairs={{0,4},{4,0},{8,12},{12,8},{16,20},{20,16},{24,28},{28,24},{1,5},{5... | collective-permute-start | bytes 491528 | tf_op jit(solution)/shard_map/ppermute | solution.py:215
  42.0 8.5 %collective-permute-start.13 = (bf16[320,256]{1,0:T(8,128)(2,1)S(1)}, bf16[320,256]{1,0:T(8,128)(2,1)S(1)}, u32[]{:S(2)}, u32[]{:S(2)}) collective-permute-start(bf16[320,256]{1,0:T(8,128)(2,1)S(1)} %collective-permute-done.11.refs_6_), channel_id=1, source_target_pairs={{0,4},{4,0},{8,12},{12,8},{16,20},{20,16},{24,28},{28,24},{1,5},{5... | collective-permute-start | bytes 491528 | tf_op jit(solution)/shard_map/ppermute | solution.py:215
  46.1 5.0 %copy-start.3 = (bf16[1,512,2048]{2,1,0:T(8,128)(2,1)S(1)}, bf16[1,512,2048]{2,1,0:T(8,128)(2,1)}, u32[]{:S(2)}) copy-start(bf16[1,512,2048]{2,1,0:T(8,128)(2,1)} %param.13) | copy-start | bytes 6291460
  49.4 9.3 %collective-permute-start = (bf16[4,160,256]{2,1,0:T(8,128)(2,1)S(1)}, bf16[4,160,256]{2,1,0:T(8,128)(2,1)S(1)}, u32[]{:S(2)}, u32[]{:S(2)}) collective-permute-start(bf16[4,160,256]{2,1,0:T(8,128)(2,1)S(1)} %get-tuple-element.35), channel_id=1, source_target_pairs={{0,4},{4,0},{8,12},{12,8},{16,20},{20,16},{24,28},{28,24},{1,5},{5... | collective-permute-start | bytes 983048 | tf_op jit(solution)/shard_map/ppermute | solution.py:215
  50.0 5.2 %collective-permute-start.25 = (bf16[320,256]{1,0:T(8,128)(2,1)S(1)}, bf16[320,256]{1,0:T(8,128)(2,1)S(1)}, u32[]{:S(2)}, u32[]{:S(2)}) collective-permute-start(bf16[320,256]{1,0:T(8,128)(2,1)S(1)} %collective-permute-done.24.refs_4_), channel_id=1, source_target_pairs={{0,4},{4,0},{8,12},{12,8},{16,20},{20,16},{24,28},{28,24},{1,5},{5... | collective-permute-start | bytes 491528 | tf_op jit(solution)/shard_map/ppermute | solution.py:215
  50.1 5.1 %collective-permute-start.23 = (bf16[320,256]{1,0:T(8,128)(2,1)S(1)}, bf16[320,256]{1,0:T(8,128)(2,1)S(1)}, u32[]{:S(2)}, u32[]{:S(2)}) collective-permute-start(bf16[320,256]{1,0:T(8,128)(2,1)S(1)} %collective-permute-done.22.refs_2_), channel_id=1, source_target_pairs={{0,4},{4,0},{8,12},{12,8},{16,20},{20,16},{24,28},{28,24},{1,5},{5... | collective-permute-start | bytes 491528 | tf_op jit(solution)/shard_map/ppermute | solution.py:215
  50.5 4.5 %collective-permute-start.29 = (bf16[160,256]{1,0:T(8,128)(2,1)S(1)}, bf16[160,256]{1,0:T(8,128)(2,1)S(1)}, u32[]{:S(2)}, u32[]{:S(2)}) collective-permute-start(bf16[160,256]{1,0:T(8,128)(2,1)S(1)} %collective-permute-done.27.refs_7_), channel_id=1, source_target_pairs={{0,4},{4,0},{8,12},{12,8},{16,20},{20,16},{24,28},{28,24},{1,5},{5... | collective-permute-start | bytes 245768 | tf_op jit(solution)/shard_map/ppermute | solution.py:215
  50.6 4.6 %collective-permute-start.28 = (bf16[160,256]{1,0:T(8,128)(2,1)S(1)}, bf16[160,256]{1,0:T(8,128)(2,1)S(1)}, u32[]{:S(2)}, u32[]{:S(2)}) collective-permute-start(bf16[160,256]{1,0:T(8,128)(2,1)S(1)} %collective-permute-done.26.refs_6_), channel_id=1, source_target_pairs={{0,4},{4,0},{8,12},{12,8},{16,20},{20,16},{24,28},{28,24},{1,5},{5... | collective-permute-start | bytes 245768 | tf_op jit(solution)/shard_map/ppermute | solution.py:215
  55.0 8.9 %collective-permute-start.15 = (bf16[4,320,256]{2,1,0:T(8,128)(2,1)S(1)}, bf16[4,320,256]{2,1,0:T(8,128)(2,1)S(1)}, u32[]{:S(2)}, u32[]{:S(2)}) collective-permute-start(bf16[4,320,256]{2,1,0:T(8,128)(2,1)S(1)} %get-tuple-element.39), channel_id=1, source_target_pairs={{0,4},{4,0},{8,12},{12,8},{16,20},{20,16},{24,28},{28,24},{1,5},{5... | collective-permute-start | bytes 1966088 | tf_op jit(solution)/shard_map/ppermute | solution.py:215
  58.2 3.8 %collective-permute-start.30 = (bf16[4,160,256]{2,1,0:T(8,128)(2,1)S(1)}, bf16[4,160,256]{2,1,0:T(8,128)(2,1)S(1)}, u32[]{:S(2)}, u32[]{:S(2)}) collective-permute-start(bf16[4,160,256]{2,1,0:T(8,128)(2,1)S(1)} %get-tuple-element.42), channel_id=1, source_target_pairs={{0,4},{4,0},{8,12},{12,8},{16,20},{20,16},{24,28},{28,24},{1,5},{5... | collective-permute-start | bytes 983048 | tf_op jit(solution)/shard_map/ppermute | solution.py:215
  58.8 24.0 %collective-permute-start.1 = (bf16[160,256]{1,0:T(8,128)(2,1)S(1)}, bf16[160,256]{1,0:T(8,128)(2,1)S(1)}, u32[]{:S(2)}, u32[]{:S(2)}) collective-permute-start(bf16[160,256]{1,0:T(8,128)(2,1)S(1)} %get-tuple-element.66), channel_id=1, source_target_pairs={{0,8},{4,12},{8,0},{12,4},{16,24},{20,28},{24,16},{28,20},{1,9},{5... | collective-permute-start | bytes 245768 | tf_op jit(solution)/shard_map/ppermute | solution.py:215
  59.8 26.1 %collective-permute-start.3 = (bf16[160,256]{1,0:T(8,128)(2,1)S(1)}, bf16[160,256]{1,0:T(8,128)(2,1)S(1)}, u32[]{:S(2)}, u32[]{:S(2)}) collective-permute-start(bf16[160,256]{1,0:T(8,128)(2,1)S(1)} %get-tuple-element.67), channel_id=1, source_target_pairs={{0,24},{4,28},{8,16},{12,20},{16,8},{20,12},{24,0},{28,4},{1,25},{... | collective-permute-start | bytes 245768 | tf_op jit(solution)/shard_map/ppermute | solution.py:215
  62.1 5.4 %collective-permute-start.31 = (bf16[160,256]{1,0:T(8,128)(2,1)S(1)}, bf16[160,256]{1,0:T(8,128)(2,1)S(1)}, u32[]{:S(2)}, u32[]{:S(2)}) collective-permute-start(bf16[160,256]{1,0:T(8,128)(2,1)S(1)} %get-tuple-element.63), channel_id=1, source_target_pairs={{0,8},{4,12},{8,0},{12,4},{16,24},{20,28},{24,16},{28,20},{1,9},{5... | collective-permute-start | bytes 245768 | tf_op jit(solution)/shard_map/ppermute | solution.py:215
  62.5 7.4 %collective-permute-start.33 = (bf16[160,256]{1,0:T(8,128)(2,1)S(1)}, bf16[160,256]{1,0:T(8,128)(2,1)S(1)}, u32[]{:S(2)}, u32[]{:S(2)}) collective-permute-start(bf16[160,256]{1,0:T(8,128)(2,1)S(1)} %get-tuple-element.64), channel_id=1, source_target_pairs={{0,24},{4,28},{8,16},{12,20},{16,8},{20,12},{24,0},{28,4},{1,25},{... | collective-permute-start | bytes 245768 | tf_op jit(solution)/shard_map/ppermute | solution.py:215
  64.0 6.9 %collective-permute-start.32 = (bf16[160,256]{1,0:T(8,128)(2,1)S(1)}, bf16[160,256]{1,0:T(8,128)(2,1)S(1)}, u32[]{:S(2)}, u32[]{:S(2)}) collective-permute-start(bf16[160,256]{1,0:T(8,128)(2,1)S(1)} %get-tuple-element.65), channel_id=1, source_target_pairs={{0,16},{4,20},{8,24},{12,28},{16,0},{20,4},{24,8},{28,12},{1,17},{... | collective-permute-start | bytes 245768 | tf_op jit(solution)/shard_map/ppermute | solution.py:215
  67.6 6.8 %collective-permute-start.16 = (bf16[320,256]{1,0:T(8,128)(2,1)S(1)}, bf16[320,256]{1,0:T(8,128)(2,1)S(1)}, u32[]{:S(2)}, u32[]{:S(2)}) collective-permute-start(bf16[320,256]{1,0:T(8,128)(2,1)S(1)} %get-tuple-element.60), channel_id=1, source_target_pairs={{0,8},{4,12},{8,0},{12,4},{16,24},{20,28},{24,16},{28,20},{1,9},{5... | collective-permute-start | bytes 491528 | tf_op jit(solution)/shard_map/ppermute | solution.py:215
  69.9 7.9 %collective-permute-start.18 = (bf16[320,256]{1,0:T(8,128)(2,1)S(1)}, bf16[320,256]{1,0:T(8,128)(2,1)S(1)}, u32[]{:S(2)}, u32[]{:S(2)}) collective-permute-start(bf16[320,256]{1,0:T(8,128)(2,1)S(1)} %get-tuple-element.61), channel_id=1, source_target_pairs={{0,24},{4,28},{8,16},{12,20},{16,8},{20,12},{24,0},{28,4},{1,25},{... | collective-permute-start | bytes 491528 | tf_op jit(solution)/shard_map/ppermute | solution.py:215
  70.9 11.6 %collective-permute-start.17 = (bf16[320,256]{1,0:T(8,128)(2,1)S(1)}, bf16[320,256]{1,0:T(8,128)(2,1)S(1)}, u32[]{:S(2)}, u32[]{:S(2)}) collective-permute-start(bf16[320,256]{1,0:T(8,128)(2,1)S(1)} %get-tuple-element.62), channel_id=1, source_target_pairs={{0,16},{4,20},{8,24},{12,28},{16,0},{20,4},{24,8},{28,12},{1,17},{... | collective-permute-start | bytes 491528 | tf_op jit(solution)/shard_map/ppermute | solution.py:215
  74.4 11.6 %collective-permute-start.2 = (bf16[160,256]{1,0:T(8,128)(2,1)S(1)}, bf16[160,256]{1,0:T(8,128)(2,1)S(1)}, u32[]{:S(2)}, u32[]{:S(2)}) collective-permute-start(bf16[160,256]{1,0:T(8,128)(2,1)S(1)} %get-tuple-element.68), channel_id=1, source_target_pairs={{0,16},{4,20},{8,24},{12,28},{16,0},{20,4},{24,8},{28,12},{1,17},{... | collective-permute-start | bytes 245768 | tf_op jit(solution)/shard_map/ppermute | solution.py:215
  77.8 9.6 %collective-permute-start.34 = (bf16[160,256]{1,0:T(8,128)(2,1)S(1)}, bf16[160,256]{1,0:T(8,128)(2,1)S(1)}, u32[]{:S(2)}, u32[]{:S(2)}) collective-permute-start(bf16[160,256]{1,0:T(8,128)(2,1)S(1)} %fusion.9), channel_id=1, source_target_pairs={{0,2},{1,3},{2,0},{3,1},{4,6},{5,7},{6,4},{7,5},{8,10},{9,11},{10,... | collective-permute-start | bytes 245768 | tf_op jit(solution)/shard_map/ppermute | solution.py:215
  82.6 6.5 %collective-permute-start.35 = (bf16[160,256]{1,0:T(8,128)(2,1)S(1)}, bf16[160,256]{1,0:T(8,128)(2,1)S(1)}, u32[]{:S(2)}, u32[]{:S(2)}) collective-permute-start(bf16[160,256]{1,0:T(8,128)(2,1)S(1)} %get-tuple-element.69), channel_id=1, source_target_pairs={{0,3},{1,2},{2,1},{3,0},{4,7},{5,6},{6,5},{7,4},{8,11},{9,10},{10,... | collective-permute-start | bytes 245768 | tf_op jit(solution)/shard_map/ppermute | solution.py:215
  82.8 6.5 %collective-permute-start.19 = (bf16[160,256]{1,0:T(8,128)(2,1)S(1)}, bf16[160,256]{1,0:T(8,128)(2,1)S(1)}, u32[]{:S(2)}, u32[]{:S(2)}) collective-permute-start(bf16[160,256]{1,0:T(8,128)(2,1)S(1)} %get-tuple-element.70), channel_id=1, source_target_pairs={{0,1},{1,0},{2,3},{3,2},{4,5},{5,4},{6,7},{7,6},{8,9},{9,8},{10,11... | collective-permute-start | bytes 245768 | tf_op jit(solution)/shard_map/ppermute | solution.py:215
  89.5 5.0 %collective-permute-start.39 = (bf16[256,256]{1,0:T(8,128)(2,1)S(1)}, bf16[256,256]{1,0:T(8,128)(2,1)S(1)}, u32[]{:S(2)}, u32[]{:S(2)}) collective-permute-start(bf16[256,256]{1,0:T(8,128)(2,1)S(1)} %shard_map.106.refs_0_), channel_id=1, source_target_pairs={{0,16},{4,20},{8,24},{12,28},{16,0},{20,4},{24,8},{28,12},{1,17},{... | collective-permute-start | bytes 393224 | tf_op jit(solution)/shard_map/ppermute | solution.py:215
  90.4 5.5 %collective-permute-start.37 = (bf16[256,256]{1,0:T(8,128)(2,1)S(1)}, bf16[256,256]{1,0:T(8,128)(2,1)S(1)}, u32[]{:S(2)}, u32[]{:S(2)}) collective-permute-start(bf16[256,256]{1,0:T(8,128)(2,1)S(1)} %shard_map.106.refs_0_), channel_id=1, source_target_pairs={{0,8},{4,12},{8,0},{12,4},{16,24},{20,28},{24,16},{28,20},{1,9},{5... | collective-permute-start | bytes 393224 | tf_op jit(solution)/shard_map/ppermute | solution.py:215
  91.6 16.6 %collective-permute-start.36 = (bf16[256,256]{1,0:T(8,128)(2,1)S(1)}, bf16[256,256]{1,0:T(8,128)(2,1)S(1)}, u32[]{:S(2)}, u32[]{:S(2)}) collective-permute-start(bf16[256,256]{1,0:T(8,128)(2,1)S(1)} %shard_map.106.refs_0_), channel_id=1, source_target_pairs={{0,4},{4,0},{8,12},{12,8},{16,20},{20,16},{24,28},{28,24},{1,5},{5... | collective-permute-start | bytes 393224 | tf_op jit(solution)/shard_map/ppermute | solution.py:215
  94.6 9.5 %collective-permute-start.42 = (bf16[128,256]{1,0:T(8,128)(2,1)S(1)}, bf16[128,256]{1,0:T(8,128)(2,1)S(1)}, u32[]{:S(2)}, u32[]{:S(2)}) collective-permute-start(bf16[128,256]{1,0:T(8,128)(2,1)S(1)} %slice.167), channel_id=1, source_target_pairs={{0,8},{4,12},{8,0},{12,4},{16,24},{20,28},{24,16},{28,20},{1,9},{5... | collective-permute-start | bytes 196616 | tf_op jit(solution)/shard_map/ppermute | solution.py:215
  95.9 8.1 %collective-permute-start.41 = (bf16[128,256]{1,0:T(8,128)(2,1)S(1)}, bf16[128,256]{1,0:T(8,128)(2,1)S(1)}, u32[]{:S(2)}, u32[]{:S(2)}) collective-permute-start(bf16[128,256]{1,0:T(8,128)(2,1)S(1)} %slice.166), channel_id=1, source_target_pairs={{0,16},{4,20},{8,24},{12,28},{16,0},{20,4},{24,8},{28,12},{1,17},{... | collective-permute-start | bytes 196616 | tf_op jit(solution)/shard_map/ppermute | solution.py:215
  97.3 11.0 %collective-permute-start.40 = (bf16[256,256]{1,0:T(8,128)(2,1)S(1)}, bf16[256,256]{1,0:T(8,128)(2,1)S(1)}, u32[]{:S(2)}, u32[]{:S(2)}) collective-permute-start(bf16[256,256]{1,0:T(8,128)(2,1)S(1)} %collective-permute-done.39.refs_4_), channel_id=1, source_target_pairs={{0,4},{4,0},{8,12},{12,8},{16,20},{20,16},{24,28},{28,24},{1,5},{5... | collective-permute-start | bytes 393224 | tf_op jit(solution)/shard_map/ppermute | solution.py:215
  97.3 11.0 %collective-permute-start.38 = (bf16[256,256]{1,0:T(8,128)(2,1)S(1)}, bf16[256,256]{1,0:T(8,128)(2,1)S(1)}, u32[]{:S(2)}, u32[]{:S(2)}) collective-permute-start(bf16[256,256]{1,0:T(8,128)(2,1)S(1)} %collective-permute-done.37.refs_2_), channel_id=1, source_target_pairs={{0,4},{4,0},{8,12},{12,8},{16,20},{20,16},{24,28},{28,24},{1,5},{5... | collective-permute-start | bytes 393224 | tf_op jit(solution)/shard_map/ppermute | solution.py:215
  104.1 4.2 %collective-permute-start.44 = (bf16[128,256]{1,0:T(8,128)(2,1)S(1)}, bf16[128,256]{1,0:T(8,128)(2,1)S(1)}, u32[]{:S(2)}, u32[]{:S(2)}) collective-permute-start(bf16[128,256]{1,0:T(8,128)(2,1)S(1)} %collective-permute-done.42.refs_7_), channel_id=1, source_target_pairs={{0,4},{4,0},{8,12},{12,8},{16,20},{20,16},{24,28},{28,24},{1,5},{5... | collective-permute-start | bytes 196616 | tf_op jit(solution)/shard_map/ppermute | solution.py:215
  104.1 4.2 %collective-permute-start.43 = (bf16[128,256]{1,0:T(8,128)(2,1)S(1)}, bf16[128,256]{1,0:T(8,128)(2,1)S(1)}, u32[]{:S(2)}, u32[]{:S(2)}) collective-permute-start(bf16[128,256]{1,0:T(8,128)(2,1)S(1)} %collective-permute-done.41.refs_6_), channel_id=1, source_target_pairs={{0,4},{4,0},{8,12},{12,8},{16,20},{20,16},{24,28},{28,24},{1,5},{5... | collective-permute-start | bytes 196616 | tf_op jit(solution)/shard_map/ppermute | solution.py:215
  (5 other events, 6.5 us)

commit v2 on v0

--- a/solution.py
+++ b/solution.py
@@ -1,7 +1,16 @@
+import functools
 import jax
 import jax.numpy as jnp
 from jax import lax
+from jax.experimental import pallas as pl
+from jax.experimental.pallas import tpu as pltpu
 from jax.sharding import PartitionSpec as P
+
+BF16 = jnp.bfloat16
+F32 = jnp.float32
+LAST = (((1,), (1,)), ((), ()))
+FIRST = (((0,), (0,)), ((), ()))
+VMEM = pltpu.MemorySpace.VMEM
 
 
 def silu_parts(pre_gate):
@@ -9,7 +18,7 @@
     return (pre_gate * sigma, sigma * (1.0 + pre_gate * (1.0 - sigma)))
 
 
-def per_device(tokens, grad_out, expert_ids, gate_prob, w_gate, w_up, w_down):
+def per_device_any(tokens, grad_out, expert_ids, gate_prob, w_gate, w_up, w_down):
     expert_count = lax.axis_size("expert")
     replica_count = lax.axis_size("dp")
     tok_count = tokens.shape[0]
@@ -74,6 +83,347 @@
     return (grad_tokens, gate_wgrad[None], up_wgrad[None], down_grad.astype(jnp.bfloat16)[None])
 
 
+SMALL = 1000
+HBM = pltpu.MemorySpace.HBM
+
+
+def call(body, outs, operands, flops, limit, scratch=(), far=0, aliases=None):
+    nbytes = sum(a.size * a.dtype.itemsize for a in operands)
+    nbytes += sum(o.size * o.dtype.itemsize for o in outs)
+    return pl.pallas_call(
+        body,
+        out_shape=outs,
+        in_specs=[pl.BlockSpec(memory_space=HBM)] * far
+        + [pl.BlockSpec(memory_space=VMEM)] * (len(operands) - far),
+        out_specs=[pl.BlockSpec(memory_space=VMEM)] * len(outs),
+        scratch_shapes=list(scratch),
+        input_output_aliases=aliases or {},
+        compiler_params=pltpu.CompilerParams(vmem_limit_bytes=limit << 20),
+        cost_estimate=pl.CostEstimate(flops=flops, bytes_accessed=nbytes, transcendentals=0),
+    )(*[pltpu.with_memory_space_constraint(a, HBM) for a in operands[:far]], *operands[far:])
+
+
+def shape(*dims, dtype=BF16):
+    return jax.ShapeDtypeStruct(dims, dtype)
+
+
+def cols(block, width):
+    return pl.ds(pl.multiple_of(block * width, width), width)
+
+
+def column(row):
+    return jnp.transpose(jnp.broadcast_to(row, (128, row.shape[1])))[:, 0:1]
+
+
+def start_copies(sems, *pairs):
+    copies = [pltpu.make_async_copy(src, dst, sems.at[j]) for j, (src, dst) in enumerate(pairs)]
+    for copy in copies:
+        copy.start()
+    return copies
+
+
+def dispatch_kernel(
+    capacity, share, ids_far, prob_far, tok, grad, send1, send2, send3, assign,
+    ids, prob, tok_part, grad_part, sems,
+):
+    here = lax.axis_index("expert")
+    piece = cols(lax.axis_index("dp"), share)
+    ids_copy, prob_copy, tok_copy, grad_copy = start_copies(
+        sems,
+        (ids_far, ids),
+        (prob_far, prob),
+        (tok.at[:, piece], tok_part),
+        (grad.at[:, piece], grad_part),
+    )
+    ids_copy.wait()
+    count = tok.shape[0]
+    places = assign.shape[0]
+    relative = jnp.bitwise_xor(ids[...], here)
+    expert = lax.broadcasted_iota(jnp.int32, (8, count), 0)
+    hit = (relative == expert).astype(F32)
+    row = lax.broadcasted_iota(jnp.int32, (count, count), 0)
+    col = lax.broadcasted_iota(jnp.int32, (count, count), 1)
+    earlier = (row < col).astype(F32).astype(BF16)
+    before = jnp.dot(hit.astype(BF16), earlier, preferred_element_type=F32)
+    slot = jnp.sum(before * hit, axis=0, keepdims=True).astype(jnp.int32)
+    target = relative * capacity + slot
+    spots = lax.broadcasted_iota(jnp.int32, (places, count), 0)
+    assign[...] = (target == spots).astype(F32).astype(BF16)
+    prob_copy.wait()
+    weight = column(prob[...])
+    tok_copy.wait()
+    for k, ref in ((1, send1), (3, send3), (2, send2)):
+        pick = assign[k * capacity : (k + 1) * capacity]
+        ref[:capacity] = jnp.dot(pick, tok_part[...], preferred_element_type=F32).astype(BF16)
+    grad_copy.wait()
+    y_part = (weight * grad_part[...].astype(F32)).astype(BF16)
+    for k, ref in ((1, send1), (3, send3), (2, send2)):
+        pick = assign[k * capacity : (k + 1) * capacity]
+        ref[capacity:] = jnp.dot(pick, y_part, preferred_element_type=F32).astype(BF16)
+
+
+def expert_math(
+    share, start, x_all, y_all, w_gate, w_up, w_down, hidden, gate_grad, up_grad, even, odd,
+    ready=(lambda: None,) * 3,
+):
+    block = lax.axis_index("dp")
+    rows = x_all.shape[0]
+    ready[0]()
+    pre_gate = jnp.dot(x_all[...], w_gate[...], preferred_element_type=F32)
+    ready[1]()
+    pre_up = jnp.dot(x_all[...], w_up[...], preferred_element_type=F32)
+    ready[2]()
+    hidden_grad = lax.dot_general(y_all[...], w_down[...], LAST, preferred_element_type=F32)
+    activated, slope = silu_parts(pre_gate)
+    hidden[...] = (activated * pre_up).astype(BF16)
+    gate_grad[...] = (hidden_grad * pre_up * slope).astype(BF16)
+    up_grad[...] = (hidden_grad * activated).astype(BF16)
+    for k in range(8):
+        piece = cols(jnp.bitwise_xor(block, k), share)
+        term = lax.dot_general(gate_grad[...], w_gate[piece, :], LAST, preferred_element_type=F32)
+        term += lax.dot_general(up_grad[...], w_up[piece, :], LAST, preferred_element_type=F32)
+        (odd if k % 2 else even)[k // 2, start : start + rows] = term.astype(BF16)
+
+
+def own_kernel(
+    share, start, prob_far, tok_far, grad_far, gate_far, up_far, down_far, assign,
+    x_all, y_all, hidden, gate_grad, up_grad, even, odd, w_gate, w_up, w_down,
+    prob, tok, grad, sems,
+):
+    prob_copy, tok_copy, grad_copy, *weight_copies = start_copies(
+        sems,
+        (prob_far, prob),
+        (tok_far, tok),
+        (grad_far, grad),
+        (gate_far, w_gate),
+        (up_far, w_up),
+        (down_far, w_down),
+    )
+    own = assign[: x_all.shape[0]]
+    tok_copy.wait()
+    x_all[...] = jnp.dot(own, tok[...], preferred_element_type=F32).astype(BF16)
+    prob_copy.wait()
+    grad_copy.wait()
+    scaled = (column(prob[...]) * grad[...].astype(F32)).astype(BF16)
+    y_all[...] = jnp.dot(own, scaled, preferred_element_type=F32).astype(BF16)
+    expert_math(
+        share, start, x_all, y_all, w_gate, w_up, w_down, hidden, gate_grad, up_grad, even, odd,
+        [copy.wait for copy in weight_copies],
+    )
+
+
+def chunk_kernel(share, extra, *refs):
+    block_ref, by_two, by_four, first, second, across = refs[:6]
+    rest = refs[6 + extra :]
+    w_gate, w_up, w_down, x_all, y_all = rest[:5]
+    block = lax.axis_index("dp")
+    half = block_ref.shape[0] // 2
+    near = [halves_of(ref) for ref in parts_of(across, 4)]
+    mine = [halves_of(block_ref), halves_of(by_two), halves_of(by_four), (first, second)]
+    for k in range(8):
+        x_part, y_part = (near if k % 2 else mine)[k // 2]
+        piece = cols(jnp.bitwise_xor(block, k), share)
+        x_all[:, piece] = x_part[...]
+        y_all[:, piece] = y_part[...]
+    expert_math(share, 0, x_all, y_all, w_gate, w_up, w_down, *rest[5:])
+
+
+def wgrad_kernel(a0, a1, a2, b0, b1, b2, out):
+    total = lax.dot_general(a0[...], b0[...], FIRST, preferred_element_type=F32)
+    total += lax.dot_general(a1[...], b1[...], FIRST, preferred_element_type=F32)
+    total += lax.dot_general(a2[...], b2[...], FIRST, preferred_element_type=F32)
+    out[...] = total.astype(BF16)
+
+
+def combine_kernel(assign, r0, r1, r2, r3, out, rows):
+    capacity = r0.shape[0]
+    for k, ref in enumerate((r0, r1, r2, r3)):
+        rows[k * capacity : (k + 1) * capacity] = ref[...]
+    out[...] = lax.dot_general(assign[...], rows[...], FIRST, preferred_element_type=F32).astype(BF16)
+
+
+def place_kernel(share, *refs):
+    out = refs[-1]
+    block = lax.axis_index("dp")
+    near = parts_of(refs[4], 4)
+    for k in range(8):
+        piece = cols(jnp.bitwise_xor(block, k), share)
+        out[:, piece] = (near if k % 2 else refs)[k // 2][...]
+
+
+def fence(*arrays):
+    return lax.optimization_barrier(arrays)
+
+
+def swap(array, axis, distance):
+    size = lax.axis_size(axis)
+    return lax.ppermute(array, axis, [(i, i ^ distance) for i in range(size)])
+
+
+def halves_of(ref):
+    half = ref.shape[0] // 2
+    return (ref.at[pl.ds(0, half)], ref.at[pl.ds(half, half)])
+
+
+def parts_of(ref, count):
+    rows = ref.shape[0] // count
+    return [ref.at[pl.ds(j * rows, rows)] for j in range(count)]
+
+
+def core_pairs(even, other):
+    return [(even[j].astype(F32) + other[j].astype(F32)).astype(BF16) for j in range(4)]
+
+
+def total_of(parts):
+    return sum(part.astype(F32) for part in parts).astype(BF16)
+
+
+def expert_outs(rows, width, hidden, share, all_rows=None):
+    return [
+        shape(rows, width),
+        shape(rows, width),
+        shape(rows, hidden),
+        shape(rows, hidden),
+        shape(rows, hidden),
+        shape(4, all_rows or rows, share),
+        shape(4, all_rows or rows, share),
+    ]
+
+
+def per_device_blocks(tokens, grad_out, expert_ids, gate_prob, w_gate, w_up, w_down):
+    count, width = tokens.shape
+    experts = lax.axis_size("expert")
+    share = width // lax.axis_size("dp")
+    capacity = max(2, (5 * count + 2 * experts - 1) // (2 * experts))
+    hidden_part = w_gate.shape[2]
+    weights = (w_gate[0], w_up[0], w_down[0])
+
+    ids = expert_ids.T
+    prob = gate_prob.T
+    send1, send2, send3, assign = call(
+        functools.partial(dispatch_kernel, capacity, share),
+        [shape(2 * capacity, share)] * 3 + [shape(experts * capacity, count)],
+        (ids, prob, tokens, grad_out),
+        SMALL,
+        8,
+        [pltpu.VMEM((1, count), jnp.int32), pltpu.VMEM((1, count), F32)]
+        + [pltpu.VMEM((count, share), BF16)] * 2
+        + [pltpu.SemaphoreType.DMA((4,))],
+        far=4,
+    )
+    got1 = swap(send1, "expert", 1)
+    got3 = swap(send3, "expert", 3)
+    own_out = call(
+        functools.partial(own_kernel, share, 2 * capacity),
+        expert_outs(capacity, width, hidden_part, share, 3 * capacity)
+        + [shape(*w.shape) for w in weights],
+        (prob, tokens, grad_out) + weights + (assign,),
+        SMALL,
+        20,
+        [pltpu.VMEM((1, count), F32)]
+        + [pltpu.VMEM((count, width), BF16)] * 2
+        + [pltpu.SemaphoreType.DMA((6,))],
+        far=6,
+    )
+    send2, *own_out = fence(send2, *own_out)
+    block_b = swap(send2, "expert", 2)
+    got1, got3, *own_out = fence(got1, got3, *own_out)
+    weights = tuple(own_out[7:])
+
+    block_a = jnp.concatenate(
+        [got1[:capacity], got3[:capacity], got1[capacity:], got3[capacity:]], axis=0
+    )
+    half_a, half_b = 2 * capacity, capacity
+    two_a = swap(block_a, "dp", 2)
+    four_a = swap(block_a, "dp", 4)
+    block_a, two_a, four_a, block_b = fence(block_a, two_a, four_a, block_b)
+
+    first_a = swap(two_a[:half_a], "dp", 4)
+    second_a = swap(four_a[half_a:], "dp", 2)
+    two_b = swap(block_b, "dp", 2)
+    four_b = swap(block_b, "dp", 4)
+    first_a, second_a, two_b, four_b = fence(first_a, second_a, two_b, four_b)
+
+    across_a = swap(jnp.concatenate([block_a, two_a, four_a, first_a, second_a]), "dp", 1)
+    first_b = swap(two_b[:half_b], "dp", 4)
+    second_b = swap(four_b[half_b:], "dp", 2)
+    out_a = call(
+        functools.partial(chunk_kernel, share, 2),
+        expert_outs(2 * capacity, width, hidden_part, share, 3 * capacity),
+        (block_a, two_a, four_a, first_a, second_a, across_a, own_out[5], own_out[6]) + weights,
+        SMALL,
+        16,
+        aliases={6: 5, 7: 6},
+    )
+    first_b, second_b, *out_a = fence(first_b, second_b, *out_a)
+
+    other_a = swap(out_a[6], "dp", 1)
+    across_b = swap(jnp.concatenate([block_b, two_b, four_b, first_b, second_b]), "dp", 1)
+    other_a, across_b = fence(other_a, across_b)
+
+    pairs_a = core_pairs(out_a[5], other_a)
+    sums_a = [swap(pairs_a[j], "dp", 2 * j) for j in range(1, 4)]
+    out_b = call(
+        functools.partial(chunk_kernel, share, 0),
+        expert_outs(capacity, width, hidden_part, share),
+        (block_b, two_b, four_b, first_b, second_b, across_b) + weights,
+        SMALL,
+        16,
+    )
+    out_b = fence(*out_b)
+    sums_a[0], *rest = fence(sums_a[0], swap(out_b[6], "dp", 1), *out_b)
+    other_b, out_b = rest[0], rest[1:]
+
+    parts = (own_out, out_a, out_b)
+    rows_all = experts * capacity
+
+    def wgrad(left, right, rows, width_out):
+        (out,) = call(
+            wgrad_kernel,
+            [shape(rows, width_out)],
+            [o[left] for o in parts] + [o[right] for o in parts],
+            2 * rows_all * rows * width_out,
+            16,
+        )
+        return out
+
+    pairs_b = core_pairs(out_b[5], other_b)
+    sums_b = [swap(pairs_b[j], "dp", 2 * j) for j in range(1, 4)]
+    gate_wgrad = wgrad(0, 3, width, hidden_part)
+    *rest, gate_wgrad = fence(*sums_a, *sums_b, gate_wgrad)
+    sums_a, sums_b = rest[:3], rest[3:]
+
+    summed_a = total_of([pairs_a[0]] + sums_a)
+    ret0 = summed_a[2 * capacity :]
+    ret1 = swap(summed_a[:capacity], "expert", 1)
+    ret3 = swap(summed_a[capacity : 2 * capacity], "expert", 3)
+    ret2 = swap(total_of([pairs_b[0]] + sums_b), "expert", 2)
+    up_wgrad = wgrad(0, 4, width, hidden_part)
+    ret1, ret2, ret3, up_wgrad = fence(ret1, ret2, ret3, up_wgrad)
+    (token_cols,) = call(
+        combine_kernel,
+        [shape(count, share)],
+        (assign, ret0, ret1, ret2, ret3),
+        SMALL,
+        8,
+        [pltpu.VMEM((experts * capacity, share), BF16)],
+    )
+    down_wgrad = wgrad(2, 1, hidden_part, width)
+    six = swap(token_cols, "dp", 6)
+    two = swap(token_cols, "dp", 2)
+    four = swap(token_cols, "dp", 4)
+    two, four, six, down_wgrad = fence(two, four, six, down_wgrad)
+    across = swap(jnp.concatenate([token_cols, two, four, six]), "dp", 1)
+    (grad_tokens,) = call(
+        functools.partial(place_kernel, share),
+        [shape(count, width)],
+        (token_cols, two, four, six, across),
+        SMALL,
+        8,
+    )
+    return (grad_tokens, gate_wgrad[None], up_wgrad[None], down_wgrad[None])
+
+
 def solution(mesh):
     placed = (
         P("expert", None),
@@ -84,8 +434,9 @@
         P("expert", None, "dp"),
         P("expert", "dp", None),
     )
+    fits = mesh.shape["dp"] == 8 and mesh.shape["expert"] == 4
     return jax.shard_map(
-        per_device,
+        per_device_blocks if fits else per_device_any,
         mesh=mesh,
         in_specs=placed,
         out_specs=(

time: 192 us -> 88.3 us (0.46)
  waiting for transfers between devices: 93.8 us -> 26.5 us
  blocking collectives: 43.5 us -> 0 us
  starting transfers between devices: 0.16 us -> 33 us
  matrix products: 31.7 us -> 0 us
  Pallas kernels: 0 us -> 27.1 us
  between operations: 13.9 us -> 0.86 us
  local copies, waits for them, and re-layouts: 4.99 us -> 0.22 us
  other arithmetic: 3.52 us -> 0.5 us
    all_gather x3 -> x0, waiting for transfers between devices: 50 us -> none  [the longest x1 24.4 us: per_device(): lax.all_gather(got_scaled, 'dp', axis=1, tiled=True)]
    reduce_scatter x1 -> x0, waiting for transfers between devices: 43.7 us -> none  [per_device(): lax.psum_scatter(terms.astype(jnp.bfloat16), 'dp', scatter_dimension=1, t...]
    all_to_all x3 -> x0, blocking collectives: 43.5 us -> none  [the longest x1 16.5 us: per_device(): lax.all_to_all(input_cols, 'expert', split_axis=0, concat_axis=0, tiled=T...]
    ppermute x0 -> x28, starting transfers between devices: none -> 33 us  [swap(): return lax.ppermute(array, axis, [(i, i ^ distance) for i in range(size)])]
    dot_general x8 -> x0, matrix products: 31.7 us -> none  [the longest x1 8.03 us: per_device(): pre_act = jnp.dot(all_inputs, w_pair, preferred_element_type=jnp.float32)]
    pallas_call x0 -> x9, Pallas kernels: none -> 27.1 us  [call(): pl.pallas_call(body, out_shape=outs, in_specs=[pl.BlockSpec(memory_space=...]
    ppermute x0 -> x28, waiting for transfers between devices: none -> 26.5 us  [swap(): return lax.ppermute(array, axis, [(i, i ^ distance) for i in range(size)])]
    broadcast_in_dim x1 -> x0, local copies, waits for them, and re-layouts: 2.28 us -> none  [per_device(): up_wgrad[None]]
  transfers between devices with their start and end apart: 4 -> 28, of which waited for: 4 -> 12; matrix products, arithmetic and copies ran while one was open for 11% -> 1% of each run, Pallas kernels for 0% -> 24%
where the time goes in v2:
time: 88.3 us; the launch traced here: 88.2 us
  starting transfers between devices  33 us (37%)
  Pallas kernels  27.1 us (31%)
  waiting for transfers between devices  26.5 us (30%)
    ppermute x28, starting transfers between devices, swap(): return lax.ppermute(array, axis, [(i, i ^ distance) for i in range(size)])  33 us
    pallas_call x9, Pallas kernels, call(): pl.pallas_call(body, out_shape=outs, in_specs=[pl.BlockSpec(memory_space=...  27.1 us
    ppermute x28, waiting for transfers between devices, swap(): return lax.ppermute(array, axis, [(i, i ^ distance) for i in range(size)])  26.5 us
  transfers between devices with their start and end apart: 28, of which 12 were waited for; matrix products, arithmetic and copies ran while one was open for 1% of the time, Pallas kernels for 24%

profile of v2, /device:TPU:0, one launch (start us, length us, event | category | flops | bytes accessed | tf_op | source)
XLA Modules:
  0.0 88.2 jit_solution(2110755710977557756)
XLA Ops:
  0.6 1.7 %shard_map.102 = (bf16[320,256]{1,0:T(8,128)(2,1)S(1)}, bf16[320,256]{1,0:T(8,128)(2,1)S(1)}, bf16[320,256]{1,0:T(8,128)(2,1)S(1)}, bf16[640,256]{1,0:T(8,128)(2,1)S(1)}) custom-call(s32[1,256]{1,0:T(1,128)} %bitcast.38, f32[1,256]{1,0:T(1,128)} %bitcast.36, bf16[256,2048]{1,0:T(8,128)(2,1)} %tok_far.1, bf16[256,2048]{1,0:T(8,128)(2,1)} %grad_far.1), custom_call_target="tpu_custom_call" | custom-call | flops 1000 | bytes 2918400 | tf_op jit(solution)/shard_map/pallas_call | solution.py:93
  2.3 3.1 %collective-permute-start = (bf16[320,256]{1,0:T(8,128)(2,1)S(1)}, bf16[320,256]{1,0:T(8,128)(2,1)S(1)}, u32[]{:S(2)}, u32[]{:S(2)}) collective-permute-start(bf16[320,256]{1,0:T(8,128)(2,1)S(1)} %get-tuple-element.98), channel_id=1, source_target_pairs={{0,1},{1,0},{2,3},{3,2},{4,5},{5,4},{6,7},{7,6},{8,9},{9,8},{10,11... | collective-permute-start | bytes 491528 | tf_op jit(solution)/shard_map/ppermute | solution.py:260
  5.4 2.5 %collective-permute-start.1 = (bf16[320,256]{1,0:T(8,128)(2,1)S(1)}, bf16[320,256]{1,0:T(8,128)(2,1)S(1)}, u32[]{:S(2)}, u32[]{:S(2)}) collective-permute-start(bf16[320,256]{1,0:T(8,128)(2,1)S(1)} %get-tuple-element.99), channel_id=1, source_target_pairs={{0,3},{1,2},{2,1},{3,0},{4,7},{5,6},{6,5},{7,4},{8,11},{9,10},{10,... | collective-permute-start | bytes 491528 | tf_op jit(solution)/shard_map/ppermute | solution.py:260
  7.9 5.8 %shard_map.103 = (bf16[160,2048]{1,0:T(8,128)(2,1)S(1)}, bf16[160,2048]{1,0:T(8,128)(2,1)S(1)}, bf16[160,512]{1,0:T(8,128)(2,1)S(1)}, bf16[160,512]{1,0:T(8,128)...) custom-call(f32[1,256]{1,0:T(1,128)} %bitcast.37, ...), custom_call_target="tpu_custom_call" | custom-call | flops 1000 | bytes 18777088 | tf_op jit(solution)/shard_map/pallas_call | solution.py:93
  13.7 1.7 %collective-permute-done.1 = bf16[320,256]{1,0:T(8,128)(2,1)S(1)} collective-permute-done((bf16[320,256]{1,0:T(8,128)(2,1)S(1)}, bf16[320,256]{1,0:T(8,128)(2,1)S(1)}, u32[]{:S(2)}, u32[]{:S(2)}) %collective-permute-start.1) | collective-permute-done | bytes 163872 | tf_op jit(solution)/shard_map/ppermute | solution.py:260
  15.5 1.6 %collective-permute-start.2 = (bf16[640,256]{1,0:T(8,128)(2,1)S(1)}, bf16[640,256]{1,0:T(8,128)(2,1)S(1)}, u32[]{:S(2)}, u32[]{:S(2)}) collective-permute-start(bf16[640,256]{1,0:T(8,128)(2,1)S(1)} %pad_maximum_fusion.1.refs_0_), channel_id=1, source_target_pairs={{0,8},{4,12},{8,0},{12,4},{16,24},{20,28},{24,16},{28,20},{1,9},{5... | collective-permute-start | bytes 983048 | tf_op jit(solution)/shard_map/ppermute | solution.py:260
  17.0 1.5 %collective-permute-start.3 = (bf16[640,256]{1,0:T(8,128)(2,1)S(1)}, bf16[640,256]{1,0:T(8,128)(2,1)S(1)}, u32[]{:S(2)}, u32[]{:S(2)}) collective-permute-start(bf16[640,256]{1,0:T(8,128)(2,1)S(1)} %pad_maximum_fusion.1.refs_0_), channel_id=1, source_target_pairs={{0,16},{4,20},{8,24},{12,28},{16,0},{20,4},{24,8},{28,12},{1,17},{... | collective-permute-start | bytes 983048 | tf_op jit(solution)/shard_map/ppermute | solution.py:260
  18.5 1.8 %collective-permute-start.4 = (bf16[320,256]{1,0:T(8,128)(2,1)S(1)}, bf16[320,256]{1,0:T(8,128)(2,1)S(1)}, u32[]{:S(2)}, u32[]{:S(2)}) collective-permute-start(bf16[320,256]{1,0:T(8,128)(2,1)S(1)} %get-tuple-element.123), channel_id=1, source_target_pairs={{0,2},{1,3},{2,0},{3,1},{4,6},{5,7},{6,4},{7,5},{8,10},{9,11},{10,... | collective-permute-start | bytes 491528 | tf_op jit(solution)/shard_map/ppermute | solution.py:260
  20.3 6.2 %collective-permute-done.4.refs_0_ = bf16[320,256]{1,0:T(8,128)(2,1)S(1)} collective-permute-done((bf16[320,256]{1,0:T(8,128)(2,1)S(1)}, bf16[320,256]{1,0:T(8,128)(2,1)S(1)}, u32[]{:S(2)}, u32[]{:S(2)}) %collective-permute-start.4) | collective-permute-done | bytes 163872 | tf_op jit(solution)/shard_map/ppermute | solution.py:260
  26.5 0.5 collective-permute-start.7
  27.1 0.5 collective-permute-start.8
  27.6 1.6 %collective-permute-start.5 = (bf16[320,256]{1,0:T(8,128)(2,1)S(1)}, bf16[320,256]{1,0:T(8,128)(2,1)S(1)}, u32[]{:S(2)}, u32[]{:S(2)}) collective-permute-start(bf16[320,256]{1,0:T(8,128)(2,1)S(1)} %slice.85), channel_id=1, source_target_pairs={{0,16},{4,20},{8,24},{12,28},{16,0},{20,4},{24,8},{28,12},{1,17},{... | collective-permute-start | bytes 491528 | tf_op jit(solution)/shard_map/ppermute | solution.py:260
  29.2 1.6 %collective-permute-start.6 = (bf16[320,256]{1,0:T(8,128)(2,1)S(1)}, bf16[320,256]{1,0:T(8,128)(2,1)S(1)}, u32[]{:S(2)}, u32[]{:S(2)}) collective-permute-start(bf16[320,256]{1,0:T(8,128)(2,1)S(1)} %slice.86), channel_id=1, source_target_pairs={{0,8},{4,12},{8,0},{12,4},{16,24},{20,28},{24,16},{28,20},{1,9},{5... | collective-permute-start | bytes 491528 | tf_op jit(solution)/shard_map/ppermute | solution.py:260
  30.8 3.3 %collective-permute-done.5.refs_3_ = bf16[320,256]{1,0:T(8,128)(2,1)S(1)} collective-permute-done((bf16[320,256]{1,0:T(8,128)(2,1)S(1)}, bf16[320,256]{1,0:T(8,128)(2,1)S(1)}, u32[]{:S(2)}, u32[]{:S(2)}) %collective-permute-start.5) | collective-permute-done | bytes 163872 | tf_op jit(solution)/shard_map/ppermute | solution.py:260
  34.1 0.4 collective-permute-done.6.refs_4_
  34.7 0.6 collective-permute-start.9
  35.3 1.5 %collective-permute-start.10 = (bf16[160,256]{1,0:T(8,128)(2,1)S(1)}, bf16[160,256]{1,0:T(8,128)(2,1)S(1)}, u32[]{:S(2)}, u32[]{:S(2)}) collective-permute-start(bf16[160,256]{1,0:T(8,128)(2,1)S(1)} %slice.88), channel_id=1, source_target_pairs={{0,8},{4,12},{8,0},{12,4},{16,24},{20,28},{24,16},{28,20},{1,9},{5... | collective-permute-start | bytes 245768 | tf_op jit(solution)/shard_map/ppermute | solution.py:260
  36.8 0.9 %collective-permute-done.11.refs_5_ = bf16[2560,256]{1,0:T(8,128)(2,1)S(1)} collective-permute-done((bf16[2560,256]{1,0:T(8,128)(2,1)S(1)}, bf16[2560,256]{1,0:T(8,128)(2,1)S(1)}, u32[]{:S(2)}, u32[]{:S(2)}) %collective-permute-start.11) | collective-permute-done | bytes 1310752 | tf_op jit(solution)/shard_map/ppermute | solution.py:260
  37.7 4.0 %shard_map.104 = (bf16[320,2048]{1,0:T(8,128)(2,1)S(1)}, bf16[320,2048]{1,0:T(8,128)(2,1)S(1)}, bf16[320,512]{1,0:T(8,128)(2,1)S(1)}, bf16[320,512]{1,0:T(8,128)...) custom-call(bf16[640,256]{1,0:T(8,128)(2,1)S(1)} %pad_maximum_fusion, ...), custom_call_target="tpu_custom_call", output_to_operand_aliasing={{5}: (6, {}), {6}: (7, {})} | custom-call | flops 1000 | bytes 16449536 | tf_op jit(solution)/shard_map/pallas_call | solution.py:93
  41.7 0.2 collective-permute-start.12
  42.0 0.4 collective-permute-start.13
  42.4 2.9 %collective-permute-done.13.refs_5_ = bf16[1280,256]{1,0:T(8,128)(2,1)S(1)} collective-permute-done((bf16[1280,256]{1,0:T(8,128)(2,1)S(1)}, bf16[1280,256]{1,0:T(8,128)(2,1)S(1)}, u32[]{:S(2)}, u32[]{:S(2)}) %collective-permute-start.13) | collective-permute-done | bytes 655392 | tf_op jit(solution)/shard_map/ppermute | solution.py:260
  45.3 3.1 %shard_map.105 = (bf16[160,2048]{1,0:T(8,128)(2,1)S(1)}, bf16[160,2048]{1,0:T(8,128)(2,1)S(1)}, bf16[160,512]{1,0:T(8,128)(2,1)S(1)}, bf16[160,512]{1,0:T(8,128)...) custom-call(bf16[320,256]{1,0:T(8,128)(2,1)S(1)} %collective-permute-don, ...), custom_call_target="tpu_custom_call" | custom-call | flops 1000 | bytes 10059776 | tf_op jit(solution)/shard_map/pallas_call | solution.py:93
  48.4 0.2 collective-permute-start.15
  48.5 0.2 fusion.6
  48.7 1.6 %collective-permute-start.14 = (bf16[480,256]{1,0:T(8,128)(2,1)S(1)}, bf16[480,256]{1,0:T(8,128)(2,1)S(1)}, u32[]{:S(2)}, u32[]{:S(2)}) collective-permute-start(bf16[480,256]{1,0:T(8,128)(2,1)S(1)} %get-tuple-element.192), channel_id=1, source_target_pairs={{0,8},{4,12},{8,0},{12,4},{16,24},{20,28},{24,16},{28,20},{1,9},{5... | collective-permute-start | bytes 737288 | tf_op jit(solution)/shard_map/ppermute | solution.py:260
  50.3 0.5 collective-permute-start.16
  50.8 1.5 %collective-permute-start.17 = (bf16[480,256]{1,0:T(8,128)(2,1)S(1)}, bf16[480,256]{1,0:T(8,128)(2,1)S(1)}, u32[]{:S(2)}, u32[]{:S(2)}) collective-permute-start(bf16[480,256]{1,0:T(8,128)(2,1)S(1)} %get-tuple-element.190), channel_id=1, source_target_pairs={{0,24},{4,28},{8,16},{12,20},{16,8},{20,12},{24,0},{28,4},{1,25},{... | collective-permute-start | bytes 737288 | tf_op jit(solution)/shard_map/ppermute | solution.py:260
  52.3 5.3 %collective-permute-done.14 = bf16[480,256]{1,0:T(8,128)(2,1)S(1)} collective-permute-done((bf16[480,256]{1,0:T(8,128)(2,1)S(1)}, bf16[480,256]{1,0:T(8,128)(2,1)S(1)}, u32[]{:S(2)}, u32[]{:S(2)}) %collective-permute-start.14) | collective-permute-done | bytes 245792 | tf_op jit(solution)/shard_map/ppermute | solution.py:260
  57.6 1.5 %collective-permute-start.18 = (bf16[160,256]{1,0:T(8,128)(2,1)S(1)}, bf16[160,256]{1,0:T(8,128)(2,1)S(1)}, u32[]{:S(2)}, u32[]{:S(2)}) collective-permute-start(bf16[160,256]{1,0:T(8,128)(2,1)S(1)} %get-tuple-element.195), channel_id=1, source_target_pairs={{0,8},{4,12},{8,0},{12,4},{16,24},{20,28},{24,16},{28,20},{1,9},{5... | collective-permute-start | bytes 245768 | tf_op jit(solution)/shard_map/ppermute | solution.py:260
  59.2 0.5 collective-permute-start.19
  59.7 1.5 %collective-permute-start.20 = (bf16[160,256]{1,0:T(8,128)(2,1)S(1)}, bf16[160,256]{1,0:T(8,128)(2,1)S(1)}, u32[]{:S(2)}, u32[]{:S(2)}) collective-permute-start(bf16[160,256]{1,0:T(8,128)(2,1)S(1)} %get-tuple-element.193), channel_id=1, source_target_pairs={{0,24},{4,28},{8,16},{12,20},{16,8},{20,12},{24,0},{28,4},{1,25},{... | collective-permute-start | bytes 245768 | tf_op jit(solution)/shard_map/ppermute | solution.py:260
  61.2 3.7 %shard_map.106 = bf16[2048,512]{1,0:T(8,128)(2,1)} custom-call(bf16[160,2048]{1,0:T(8,128)(2,1)S(1)} %get-tuple-element.160.a0, bf16[320,2048]{1,0:T(8,128)(2,1)S(1)} %get-tuple-element.161.a1, bf16[160,2048]{1,0:T(8,128)(2,1)S(1)} %get-tuple-element.162.a2, bf16[160,512]{1,0:T(8,128)(2,1)S(1)} %get-tuple-element.163.b0, ...), custom_call_target="tpu_custom_call" | custom-call | flops 1342177280 | bytes 5373952 | tf_op jit(solution)/shard_map/pallas_call | solution.py:93
  64.9 1.2 %collective-permute-done.16 = bf16[480,256]{1,0:T(8,128)(2,1)S(1)} collective-permute-done((bf16[480,256]{1,0:T(8,128)(2,1)S(1)}, bf16[480,256]{1,0:T(8,128)(2,1)S(1)}, u32[]{:S(2)}, u32[]{:S(2)}) %collective-permute-start.16) | collective-permute-done | bytes 245792 | tf_op jit(solution)/shard_map/ppermute | solution.py:260
  66.1 0.9 %collective-permute-done.19 = bf16[160,256]{1,0:T(8,128)(2,1)S(1)} collective-permute-done((bf16[160,256]{1,0:T(8,128)(2,1)S(1)}, bf16[160,256]{1,0:T(8,128)(2,1)S(1)}, u32[]{:S(2)}, u32[]{:S(2)}) %collective-permute-start.19) | collective-permute-done | bytes 81952 | tf_op jit(solution)/shard_map/ppermute | solution.py:260
  67.2 0.3 collective-permute-start.21
  67.5 2.8 %collective-permute-start.22 = (bf16[160,256]{1,0:T(8,128)(2,1)S(1)}, bf16[160,256]{1,0:T(8,128)(2,1)S(1)}, u32[]{:S(2)}, u32[]{:S(2)}) collective-permute-start(bf16[160,256]{1,0:T(8,128)(2,1)S(1)} %fusion.9), channel_id=1, source_target_pairs={{0,2},{1,3},{2,0},{3,1},{4,6},{5,7},{6,4},{7,5},{8,10},{9,11},{10,... | collective-permute-start | bytes 245768 | tf_op jit(solution)/shard_map/ppermute | solution.py:260
  70.3 1.6 %collective-permute-start.23 = (bf16[160,256]{1,0:T(8,128)(2,1)S(1)}, bf16[160,256]{1,0:T(8,128)(2,1)S(1)}, u32[]{:S(2)}, u32[]{:S(2)}) collective-permute-start(bf16[160,256]{1,0:T(8,128)(2,1)S(1)} %get-tuple-element.196), channel_id=1, source_target_pairs={{0,3},{1,2},{2,1},{3,0},{4,7},{5,6},{6,5},{7,4},{8,11},{9,10},{10,... | collective-permute-start | bytes 245768 | tf_op jit(solution)/shard_map/ppermute | solution.py:260
  71.9 3.7 %shard_map.107 = bf16[2048,512]{1,0:T(8,128)(2,1)} custom-call(bf16[160,2048]{1,0:T(8,128)(2,1)S(1)} %get-tuple-element.160.a0, bf16[320,2048]{1,0:T(8,128)(2,1)S(1)} %get-tuple-element.161.a1, bf16[160,2048]{1,0:T(8,128)(2,1)S(1)} %get-tuple-element.162.a2, bf16[160,512]{1,0:T(8,128)(2,1)S(1)} %get-tuple-element.172.b0, ...), custom_call_target="tpu_custom_call" | custom-call | flops 1342177280 | bytes 5373952 | tf_op jit(solution)/shard_map/pallas_call | solution.py:93
  75.7 1.1 %collective-permute-done.22.r2 = bf16[160,256]{1,0:T(8,128)(2,1)S(1)} collective-permute-done((bf16[160,256]{1,0:T(8,128)(2,1)S(1)}, bf16[160,256]{1,0:T(8,128)(2,1)S(1)}, u32[]{:S(2)}, u32[]{:S(2)}) %collective-permute-start.22) | collective-permute-done | bytes 81952 | tf_op jit(solution)/shard_map/ppermute | solution.py:260
  76.8 0.3 shard_map.108.refs_0_
  77.1 1.1 %collective-permute-start.24 = (bf16[256,256]{1,0:T(8,128)(2,1)S(1)}, bf16[256,256]{1,0:T(8,128)(2,1)S(1)}, u32[]{:S(2)}, u32[]{:S(2)}) collective-permute-start(bf16[256,256]{1,0:T(8,128)(2,1)S(1)} %shard_map.108.refs_0_), channel_id=1, source_target_pairs={{0,8},{4,12},{8,0},{12,4},{16,24},{20,28},{24,16},{28,20},{1,9},{5... | collective-permute-start | bytes 393224 | tf_op jit(solution)/shard_map/ppermute | solution.py:260
  78.2 0.9 %collective-permute-start.25 = (bf16[256,256]{1,0:T(8,128)(2,1)S(1)}, bf16[256,256]{1,0:T(8,128)(2,1)S(1)}, u32[]{:S(2)}, u32[]{:S(2)}) collective-permute-start(bf16[256,256]{1,0:T(8,128)(2,1)S(1)} %shard_map.108.refs_0_), channel_id=1, source_target_pairs={{0,16},{4,20},{8,24},{12,28},{16,0},{20,4},{24,8},{28,12},{1,17},{... | collective-permute-start | bytes 393224 | tf_op jit(solution)/shard_map/ppermute | solution.py:260
  79.2 1.5 %collective-permute-start.26 = (bf16[256,256]{1,0:T(8,128)(2,1)S(1)}, bf16[256,256]{1,0:T(8,128)(2,1)S(1)}, u32[]{:S(2)}, u32[]{:S(2)}) collective-permute-start(bf16[256,256]{1,0:T(8,128)(2,1)S(1)} %shard_map.108.refs_0_), channel_id=1, source_target_pairs={{0,24},{4,28},{8,16},{12,20},{16,8},{20,12},{24,0},{28,4},{1,25},{... | collective-permute-start | bytes 393224 | tf_op jit(solution)/shard_map/ppermute | solution.py:260
  80.7 3.7 %shard_map.109 = bf16[512,2048]{1,0:T(8,128)(2,1)} custom-call(bf16[160,512]{1,0:T(8,128)(2,1)S(1)} %get-tuple-element.178.a0, bf16[320,512]{1,0:T(8,128)(2,1)S(1)} %get-tuple-element.179.a1, bf16[160,512]{1,0:T(8,128)(2,1)S(1)} %get-tuple-element.180.a2, bf16[160,2048]{1,0:T(8,128)(2,1)S(1)} %get-tuple-element.181.b0, ...), custom_call_target="tpu_custom_call" | custom-call | flops 1342177280 | bytes 5373952 | tf_op jit(solution)/shard_map/pallas_call | solution.py:93
  84.4 0.7 collective-permute-done.26.refs_3_
  85.2 1.9 %collective-permute-done.27.refs_4_ = bf16[1024,256]{1,0:T(8,128)(2,1)S(1)} collective-permute-done((bf16[1024,256]{1,0:T(8,128)(2,1)S(1)}, bf16[1024,256]{1,0:T(8,128)(2,1)S(1)}, u32[]{:S(2)}, u32[]{:S(2)}) %collective-permute-start.27) | collective-permute-done | bytes 524320 | tf_op jit(solution)/shard_map/ppermute | solution.py:260
  87.0 1.1 %shard_map.110 = bf16[256,2048]{1,0:T(8,128)(2,1)} custom-call(bf16[256,256]{1,0:T(8,128)(2,1)S(1)} %shard_map.108.refs_0_, bf16[256,256]{1,0:T(8,128)(2,1)S(1)} %collective-permute-done.24.refs_1_, bf16[256,256]{1,0:T(8,128)(2,1)S(1)} %collective-permute-done.25.refs_2_, bf16[256,256]{1,0:T(8,128)(2,1)S(1)} %collective-permute-done.26.refs_3_, ...), custom_call_target="tpu_custom_call" | custom-call | flops 1000 | bytes 2097152 | tf_op jit(solution)/shard_map/pallas_call | solution.py:93
  (39 shorter events, 0.7 us)
Async XLA Ops:
  2.3 11.4 %collective-permute-start = (bf16[320,256]{1,0:T(8,128)(2,1)S(1)}, bf16[320,256]{1,0:T(8,128)(2,1)S(1)}, u32[]{:S(2)}, u32[]{:S(2)}) collective-permute-start(bf16[320,256]{1,0:T(8,128)(2,1)S(1)} %get-tuple-element.98), channel_id=1, source_target_pairs={{0,1},{1,0},{2,3},{3,2},{4,5},{5,4},{6,7},{7,6},{8,9},{9,8},{10,11... | collective-permute-start | bytes 491528 | tf_op jit(solution)/shard_map/ppermute | solution.py:260
  5.4 10.0 %collective-permute-start.1 = (bf16[320,256]{1,0:T(8,128)(2,1)S(1)}, bf16[320,256]{1,0:T(8,128)(2,1)S(1)}, u32[]{:S(2)}, u32[]{:S(2)}) collective-permute-start(bf16[320,256]{1,0:T(8,128)(2,1)S(1)} %get-tuple-element.99), channel_id=1, source_target_pairs={{0,3},{1,2},{2,1},{3,0},{4,7},{5,6},{6,5},{7,4},{8,11},{9,10},{10,... | collective-permute-start | bytes 491528 | tf_op jit(solution)/shard_map/ppermute | solution.py:260
  15.5 11.1 %collective-permute-start.2 = (bf16[640,256]{1,0:T(8,128)(2,1)S(1)}, bf16[640,256]{1,0:T(8,128)(2,1)S(1)}, u32[]{:S(2)}, u32[]{:S(2)}) collective-permute-start(bf16[640,256]{1,0:T(8,128)(2,1)S(1)} %pad_maximum_fusion.1.refs_0_), channel_id=1, source_target_pairs={{0,8},{4,12},{8,0},{12,4},{16,24},{20,28},{24,16},{28,20},{1,9},{5... | collective-permute-start | bytes 983048 | tf_op jit(solution)/shard_map/ppermute | solution.py:260
  17.0 9.5 %collective-permute-start.3 = (bf16[640,256]{1,0:T(8,128)(2,1)S(1)}, bf16[640,256]{1,0:T(8,128)(2,1)S(1)}, u32[]{:S(2)}, u32[]{:S(2)}) collective-permute-start(bf16[640,256]{1,0:T(8,128)(2,1)S(1)} %pad_maximum_fusion.1.refs_0_), channel_id=1, source_target_pairs={{0,16},{4,20},{8,24},{12,28},{16,0},{20,4},{24,8},{28,12},{1,17},{... | collective-permute-start | bytes 983048 | tf_op jit(solution)/shard_map/ppermute | solution.py:260
  18.5 8.0 %collective-permute-start.4 = (bf16[320,256]{1,0:T(8,128)(2,1)S(1)}, bf16[320,256]{1,0:T(8,128)(2,1)S(1)}, u32[]{:S(2)}, u32[]{:S(2)}) collective-permute-start(bf16[320,256]{1,0:T(8,128)(2,1)S(1)} %get-tuple-element.123), channel_id=1, source_target_pairs={{0,2},{1,3},{2,0},{3,1},{4,6},{5,7},{6,4},{7,5},{8,10},{9,11},{10,... | collective-permute-start | bytes 491528 | tf_op jit(solution)/shard_map/ppermute | solution.py:260
  26.5 8.0 %collective-permute-start.7 = (bf16[320,256]{1,0:T(8,128)(2,1)S(1)}, bf16[320,256]{1,0:T(8,128)(2,1)S(1)}, u32[]{:S(2)}, u32[]{:S(2)}) collective-permute-start(bf16[320,256]{1,0:T(8,128)(2,1)S(1)} %collective-permute-done.4.refs_0_), channel_id=1, source_target_pairs={{0,8},{4,12},{8,0},{12,4},{16,24},{20,28},{24,16},{28,20},{1,9},{5... | collective-permute-start | bytes 491528 | tf_op jit(solution)/shard_map/ppermute | solution.py:260
  27.1 7.5 %collective-permute-start.8 = (bf16[320,256]{1,0:T(8,128)(2,1)S(1)}, bf16[320,256]{1,0:T(8,128)(2,1)S(1)}, u32[]{:S(2)}, u32[]{:S(2)}) collective-permute-start(bf16[320,256]{1,0:T(8,128)(2,1)S(1)} %collective-permute-done.4.refs_0_), channel_id=1, source_target_pairs={{0,16},{4,20},{8,24},{12,28},{16,0},{20,4},{24,8},{28,12},{1,17},{... | collective-permute-start | bytes 491528 | tf_op jit(solution)/shard_map/ppermute | solution.py:260
  27.6 6.6 %collective-permute-start.5 = (bf16[320,256]{1,0:T(8,128)(2,1)S(1)}, bf16[320,256]{1,0:T(8,128)(2,1)S(1)}, u32[]{:S(2)}, u32[]{:S(2)}) collective-permute-start(bf16[320,256]{1,0:T(8,128)(2,1)S(1)} %slice.85), channel_id=1, source_target_pairs={{0,16},{4,20},{8,24},{12,28},{16,0},{20,4},{24,8},{28,12},{1,17},{... | collective-permute-start | bytes 491528 | tf_op jit(solution)/shard_map/ppermute | solution.py:260
  29.2 5.4 %collective-permute-start.6 = (bf16[320,256]{1,0:T(8,128)(2,1)S(1)}, bf16[320,256]{1,0:T(8,128)(2,1)S(1)}, u32[]{:S(2)}, u32[]{:S(2)}) collective-permute-start(bf16[320,256]{1,0:T(8,128)(2,1)S(1)} %slice.86), channel_id=1, source_target_pairs={{0,8},{4,12},{8,0},{12,4},{16,24},{20,28},{24,16},{28,20},{1,9},{5... | collective-permute-start | bytes 491528 | tf_op jit(solution)/shard_map/ppermute | solution.py:260
  34.6 3.1 %collective-permute-start.11 = (bf16[2560,256]{1,0:T(8,128)(2,1)S(1)}, bf16[2560,256]{1,0:T(8,128)(2,1)S(1)}, u32[]{:S(2)}, u32[]{:S(2)}) collective-permute-start(bf16[2560,256]{1,0:T(8,128)(2,1)S(1)} %constant_dynamic-update-slice_fusion), channel_id=1, source_target_pairs={{0,4},{4,0},{8,12},{12,8},{16,20},{20,16},{24,28},{28,24},{1,5},{5... | collective-permute-start | bytes 3932168 | tf_op jit(solution)/shard_map/ppermute | solution.py:260
  34.7 7.0 %collective-permute-start.9 = (bf16[160,256]{1,0:T(8,128)(2,1)S(1)}, bf16[160,256]{1,0:T(8,128)(2,1)S(1)}, u32[]{:S(2)}, u32[]{:S(2)}) collective-permute-start(bf16[160,256]{1,0:T(8,128)(2,1)S(1)} %slice.87), channel_id=1, source_target_pairs={{0,16},{4,20},{8,24},{12,28},{16,0},{20,4},{24,8},{28,12},{1,17},{... | collective-permute-start | bytes 245768 | tf_op jit(solution)/shard_map/ppermute | solution.py:260
  35.3 6.4 %collective-permute-start.10 = (bf16[160,256]{1,0:T(8,128)(2,1)S(1)}, bf16[160,256]{1,0:T(8,128)(2,1)S(1)}, u32[]{:S(2)}, u32[]{:S(2)}) collective-permute-start(bf16[160,256]{1,0:T(8,128)(2,1)S(1)} %slice.88), channel_id=1, source_target_pairs={{0,8},{4,12},{8,0},{12,4},{16,24},{20,28},{24,16},{28,20},{1,9},{5... | collective-permute-start | bytes 245768 | tf_op jit(solution)/shard_map/ppermute | solution.py:260
  41.7 3.6 %collective-permute-start.12 = (bf16[4,480,256]{2,1,0:T(8,128)(2,1)S(1)}, bf16[4,480,256]{2,1,0:T(8,128)(2,1)S(1)}, u32[]{:S(2)}, u32[]{:S(2)}) collective-permute-start(bf16[4,480,256]{2,1,0:T(8,128)(2,1)S(1)} %get-tuple-element.145), channel_id=1, source_target_pairs={{0,4},{4,0},{8,12},{12,8},{16,20},{20,16},{24,28},{28,24},{1,5},{5... | collective-permute-start | bytes 2949128 | tf_op jit(solution)/shard_map/ppermute | solution.py:260
  42.0 3.3 %collective-permute-start.13 = (bf16[1280,256]{1,0:T(8,128)(2,1)S(1)}, bf16[1280,256]{1,0:T(8,128)(2,1)S(1)}, u32[]{:S(2)}, u32[]{:S(2)}) collective-permute-start(bf16[1280,256]{1,0:T(8,128)(2,1)S(1)} %constant_dynamic-update-slice_fusion.5), channel_id=1, source_target_pairs={{0,4},{4,0},{8,12},{12,8},{16,20},{20,16},{24,28},{28,24},{1,5},{5... | collective-permute-start | bytes 1966088 | tf_op jit(solution)/shard_map/ppermute | solution.py:260
  48.4 9.2 %collective-permute-start.15 = (bf16[4,160,256]{2,1,0:T(8,128)(2,1)S(1)}, bf16[4,160,256]{2,1,0:T(8,128)(2,1)S(1)}, u32[]{:S(2)}, u32[]{:S(2)}) collective-permute-start(bf16[4,160,256]{2,1,0:T(8,128)(2,1)S(1)} %get-tuple-element.150), channel_id=1, source_target_pairs={{0,4},{4,0},{8,12},{12,8},{16,20},{20,16},{24,28},{28,24},{1,5},{5... | collective-permute-start | bytes 983048 | tf_op jit(solution)/shard_map/ppermute | solution.py:260
  48.7 8.9 %collective-permute-start.14 = (bf16[480,256]{1,0:T(8,128)(2,1)S(1)}, bf16[480,256]{1,0:T(8,128)(2,1)S(1)}, u32[]{:S(2)}, u32[]{:S(2)}) collective-permute-start(bf16[480,256]{1,0:T(8,128)(2,1)S(1)} %get-tuple-element.192), channel_id=1, source_target_pairs={{0,8},{4,12},{8,0},{12,4},{16,24},{20,28},{24,16},{28,20},{1,9},{5... | collective-permute-start | bytes 737288 | tf_op jit(solution)/shard_map/ppermute | solution.py:260
  50.3 15.8 %collective-permute-start.16 = (bf16[480,256]{1,0:T(8,128)(2,1)S(1)}, bf16[480,256]{1,0:T(8,128)(2,1)S(1)}, u32[]{:S(2)}, u32[]{:S(2)}) collective-permute-start(bf16[480,256]{1,0:T(8,128)(2,1)S(1)} %get-tuple-element.191), channel_id=1, source_target_pairs={{0,16},{4,20},{8,24},{12,28},{16,0},{20,4},{24,8},{28,12},{1,17},{... | collective-permute-start | bytes 737288 | tf_op jit(solution)/shard_map/ppermute | solution.py:260
  50.8 15.3 %collective-permute-start.17 = (bf16[480,256]{1,0:T(8,128)(2,1)S(1)}, bf16[480,256]{1,0:T(8,128)(2,1)S(1)}, u32[]{:S(2)}, u32[]{:S(2)}) collective-permute-start(bf16[480,256]{1,0:T(8,128)(2,1)S(1)} %get-tuple-element.190), channel_id=1, source_target_pairs={{0,24},{4,28},{8,16},{12,20},{16,8},{20,12},{24,0},{28,4},{1,25},{... | collective-permute-start | bytes 737288 | tf_op jit(solution)/shard_map/ppermute | solution.py:260
  57.6 8.5 %collective-permute-start.18 = (bf16[160,256]{1,0:T(8,128)(2,1)S(1)}, bf16[160,256]{1,0:T(8,128)(2,1)S(1)}, u32[]{:S(2)}, u32[]{:S(2)}) collective-permute-start(bf16[160,256]{1,0:T(8,128)(2,1)S(1)} %get-tuple-element.195), channel_id=1, source_target_pairs={{0,8},{4,12},{8,0},{12,4},{16,24},{20,28},{24,16},{28,20},{1,9},{5... | collective-permute-start | bytes 245768 | tf_op jit(solution)/shard_map/ppermute | solution.py:260
  59.2 7.8 %collective-permute-start.19 = (bf16[160,256]{1,0:T(8,128)(2,1)S(1)}, bf16[160,256]{1,0:T(8,128)(2,1)S(1)}, u32[]{:S(2)}, u32[]{:S(2)}) collective-permute-start(bf16[160,256]{1,0:T(8,128)(2,1)S(1)} %get-tuple-element.194), channel_id=1, source_target_pairs={{0,16},{4,20},{8,24},{12,28},{16,0},{20,4},{24,8},{28,12},{1,17},{... | collective-permute-start | bytes 245768 | tf_op jit(solution)/shard_map/ppermute | solution.py:260
  59.7 7.3 %collective-permute-start.20 = (bf16[160,256]{1,0:T(8,128)(2,1)S(1)}, bf16[160,256]{1,0:T(8,128)(2,1)S(1)}, u32[]{:S(2)}, u32[]{:S(2)}) collective-permute-start(bf16[160,256]{1,0:T(8,128)(2,1)S(1)} %get-tuple-element.193), channel_id=1, source_target_pairs={{0,24},{4,28},{8,16},{12,20},{16,8},{20,12},{24,0},{28,4},{1,25},{... | collective-permute-start | bytes 245768 | tf_op jit(solution)/shard_map/ppermute | solution.py:260
  67.2 8.5 %collective-permute-start.21 = (bf16[160,256]{1,0:T(8,128)(2,1)S(1)}, bf16[160,256]{1,0:T(8,128)(2,1)S(1)}, u32[]{:S(2)}, u32[]{:S(2)}) collective-permute-start(bf16[160,256]{1,0:T(8,128)(2,1)S(1)} %get-tuple-element.197), channel_id=1, source_target_pairs={{0,1},{1,0},{2,3},{3,2},{4,5},{5,4},{6,7},{7,6},{8,9},{9,8},{10,11... | collective-permute-start | bytes 245768 | tf_op jit(solution)/shard_map/ppermute | solution.py:260
  67.5 9.3 %collective-permute-start.22 = (bf16[160,256]{1,0:T(8,128)(2,1)S(1)}, bf16[160,256]{1,0:T(8,128)(2,1)S(1)}, u32[]{:S(2)}, u32[]{:S(2)}) collective-permute-start(bf16[160,256]{1,0:T(8,128)(2,1)S(1)} %fusion.9), channel_id=1, source_target_pairs={{0,2},{1,3},{2,0},{3,1},{4,6},{5,7},{6,4},{7,5},{8,10},{9,11},{10,... | collective-permute-start | bytes 245768 | tf_op jit(solution)/shard_map/ppermute | solution.py:260
  70.3 6.4 %collective-permute-start.23 = (bf16[160,256]{1,0:T(8,128)(2,1)S(1)}, bf16[160,256]{1,0:T(8,128)(2,1)S(1)}, u32[]{:S(2)}, u32[]{:S(2)}) collective-permute-start(bf16[160,256]{1,0:T(8,128)(2,1)S(1)} %get-tuple-element.196), channel_id=1, source_target_pairs={{0,3},{1,2},{2,1},{3,0},{4,7},{5,6},{6,5},{7,4},{8,11},{9,10},{10,... | collective-permute-start | bytes 245768 | tf_op jit(solution)/shard_map/ppermute | solution.py:260
  77.1 7.3 %collective-permute-start.24 = (bf16[256,256]{1,0:T(8,128)(2,1)S(1)}, bf16[256,256]{1,0:T(8,128)(2,1)S(1)}, u32[]{:S(2)}, u32[]{:S(2)}) collective-permute-start(bf16[256,256]{1,0:T(8,128)(2,1)S(1)} %shard_map.108.refs_0_), channel_id=1, source_target_pairs={{0,8},{4,12},{8,0},{12,4},{16,24},{20,28},{24,16},{28,20},{1,9},{5... | collective-permute-start | bytes 393224 | tf_op jit(solution)/shard_map/ppermute | solution.py:260
  78.2 6.1 %collective-permute-start.25 = (bf16[256,256]{1,0:T(8,128)(2,1)S(1)}, bf16[256,256]{1,0:T(8,128)(2,1)S(1)}, u32[]{:S(2)}, u32[]{:S(2)}) collective-permute-start(bf16[256,256]{1,0:T(8,128)(2,1)S(1)} %shard_map.108.refs_0_), channel_id=1, source_target_pairs={{0,16},{4,20},{8,24},{12,28},{16,0},{20,4},{24,8},{28,12},{1,17},{... | collective-permute-start | bytes 393224 | tf_op jit(solution)/shard_map/ppermute | solution.py:260
  79.2 5.9 %collective-permute-start.26 = (bf16[256,256]{1,0:T(8,128)(2,1)S(1)}, bf16[256,256]{1,0:T(8,128)(2,1)S(1)}, u32[]{:S(2)}, u32[]{:S(2)}) collective-permute-start(bf16[256,256]{1,0:T(8,128)(2,1)S(1)} %shard_map.108.refs_0_), channel_id=1, source_target_pairs={{0,24},{4,28},{8,16},{12,20},{16,8},{20,12},{24,0},{28,4},{1,25},{... | collective-permute-start | bytes 393224 | tf_op jit(solution)/shard_map/ppermute | solution.py:260
  85.1 2.0 %collective-permute-start.27 = (bf16[1024,256]{1,0:T(8,128)(2,1)S(1)}, bf16[1024,256]{1,0:T(8,128)(2,1)S(1)}, u32[]{:S(2)}, u32[]{:S(2)}) collective-permute-start(bf16[1024,256]{1,0:T(8,128)(2,1)S(1)} %pad_maximum_fusion), channel_id=1, source_target_pairs={{0,4},{4,0},{8,12},{12,8},{16,20},{20,16},{24,28},{28,24},{1,5},{5... | collective-permute-start | bytes 1572872 | tf_op jit(solution)/shard_map/ppermute | solution.py:260

commit v3 on v2

--- a/solution.py
+++ b/solution.py
@@ -87,7 +87,7 @@
 HBM = pltpu.MemorySpace.HBM
 
 
-def call(body, outs, operands, flops, limit, scratch=(), far=0, aliases=None):
+def call(body, outs, operands, flops, limit, scratch=(), far=0, aliases=None, out_space=VMEM):
     nbytes = sum(a.size * a.dtype.itemsize for a in operands)
     nbytes += sum(o.size * o.dtype.itemsize for o in outs)
     return pl.pallas_call(
@@ -95,7 +95,7 @@
         out_shape=outs,
         in_specs=[pl.BlockSpec(memory_space=HBM)] * far
         + [pl.BlockSpec(memory_space=VMEM)] * (len(operands) - far),
-        out_specs=[pl.BlockSpec(memory_space=VMEM)] * len(outs),
+        out_specs=[pl.BlockSpec(memory_space=out_space)] * len(outs),
         scratch_shapes=list(scratch),
         input_output_aliases=aliases or {},
         compiler_params=pltpu.CompilerParams(vmem_limit_bytes=limit << 20),
@@ -162,31 +162,41 @@
         ref[capacity:] = jnp.dot(pick, y_part, preferred_element_type=F32).astype(BF16)
 
 
-def expert_math(
-    share, start, x_all, y_all, w_gate, w_up, w_down, hidden, gate_grad, up_grad, even, odd,
-    ready=(lambda: None,) * 3,
-):
+def block_order():
+    core = jnp.bitwise_and(lax.axis_index("dp"), 1)
+    first = 2 + 2 * core
+    second = 4 - 2 * core
+    return (0, first, second, 6), (1, second + 1, first + 1, 7)
+
+
+def expert_math(share, rows, spot, shared, terms, weights, ready=(lambda: None,) * 3):
+    x_all, y_all, hidden, gate_grad, up_grad = shared
+    even, odd = terms
+    w_gate, w_up, w_down = weights
     block = lax.axis_index("dp")
-    rows = x_all.shape[0]
     ready[0]()
-    pre_gate = jnp.dot(x_all[...], w_gate[...], preferred_element_type=F32)
+    pre_gate = jnp.dot(x_all[rows], w_gate[...], preferred_element_type=F32)
     ready[1]()
-    pre_up = jnp.dot(x_all[...], w_up[...], preferred_element_type=F32)
+    pre_up = jnp.dot(x_all[rows], w_up[...], preferred_element_type=F32)
     ready[2]()
-    hidden_grad = lax.dot_general(y_all[...], w_down[...], LAST, preferred_element_type=F32)
+    hidden_grad = lax.dot_general(y_all[rows], w_down[...], LAST, preferred_element_type=F32)
     activated, slope = silu_parts(pre_gate)
-    hidden[...] = (activated * pre_up).astype(BF16)
-    gate_grad[...] = (hidden_grad * pre_up * slope).astype(BF16)
-    up_grad[...] = (hidden_grad * activated).astype(BF16)
-    for k in range(8):
-        piece = cols(jnp.bitwise_xor(block, k), share)
-        term = lax.dot_general(gate_grad[...], w_gate[piece, :], LAST, preferred_element_type=F32)
-        term += lax.dot_general(up_grad[...], w_up[piece, :], LAST, preferred_element_type=F32)
-        (odd if k % 2 else even)[k // 2, start : start + rows] = term.astype(BF16)
+    hidden[rows] = (activated * pre_up).astype(BF16)
+    gate_part = (hidden_grad * pre_up * slope).astype(BF16)
+    up_part = (hidden_grad * activated).astype(BF16)
+    gate_grad[rows] = gate_part
+    up_grad[rows] = up_part
+    mine, across = block_order()
+    for out, order in ((odd, across), (even, mine)):
+        for j, k in enumerate(order):
+            piece = cols(jnp.bitwise_xor(block, k), share)
+            term = lax.dot_general(gate_part, w_gate[piece, :], LAST, preferred_element_type=F32)
+            term += lax.dot_general(up_part, w_up[piece, :], LAST, preferred_element_type=F32)
+            out[j, spot] = term.astype(BF16)
 
 
 def own_kernel(
-    share, start, prob_far, tok_far, grad_far, gate_far, up_far, down_far, assign,
+    share, spot, prob_far, tok_far, grad_far, gate_far, up_far, down_far, assign,
     x_all, y_all, hidden, gate_grad, up_grad, even, odd, w_gate, w_up, w_down,
     prob, tok, grad, sems,
 ):
@@ -199,40 +209,50 @@
         (up_far, w_up),
         (down_far, w_down),
     )
-    own = assign[: x_all.shape[0]]
+    own = assign[: spot.stop - spot.start]
     tok_copy.wait()
-    x_all[...] = jnp.dot(own, tok[...], preferred_element_type=F32).astype(BF16)
+    x_all[spot] = jnp.dot(own, tok[...], preferred_element_type=F32).astype(BF16)
     prob_copy.wait()
     grad_copy.wait()
     scaled = (column(prob[...]) * grad[...].astype(F32)).astype(BF16)
-    y_all[...] = jnp.dot(own, scaled, preferred_element_type=F32).astype(BF16)
+    y_all[spot] = jnp.dot(own, scaled, preferred_element_type=F32).astype(BF16)
     expert_math(
-        share, start, x_all, y_all, w_gate, w_up, w_down, hidden, gate_grad, up_grad, even, odd,
-        [copy.wait for copy in weight_copies],
-    )
-
-
-def chunk_kernel(share, extra, *refs):
-    block_ref, by_two, by_four, first, second, across = refs[:6]
-    rest = refs[6 + extra :]
-    w_gate, w_up, w_down, x_all, y_all = rest[:5]
+        share, spot, spot, (x_all, y_all, hidden, gate_grad, up_grad), (even, odd),
+        (w_gate, w_up, w_down), [copy.wait for copy in weight_copies],
+    )
+
+
+def chunk_kernel(share, rows, spot, pieces, extra, *refs):
+    blocks = list(refs[:4])
+    for ref in refs[4 : 4 + pieces]:
+        blocks += parts_of(ref, 4 // pieces)
+    rest = refs[4 + pieces :]
+    weights = rest[:3]
+    outs = rest[3 + extra :]
+    x_all, y_all = outs[:2]
     block = lax.axis_index("dp")
-    half = block_ref.shape[0] // 2
-    near = [halves_of(ref) for ref in parts_of(across, 4)]
-    mine = [halves_of(block_ref), halves_of(by_two), halves_of(by_four), (first, second)]
-    for k in range(8):
-        x_part, y_part = (near if k % 2 else mine)[k // 2]
+    mine, across = block_order()
+    for k, ref in zip(mine + across, blocks):
+        x_part, y_part = halves_of(ref)
         piece = cols(jnp.bitwise_xor(block, k), share)
-        x_all[:, piece] = x_part[...]
-        y_all[:, piece] = y_part[...]
-    expert_math(share, 0, x_all, y_all, w_gate, w_up, w_down, *rest[5:])
-
-
-def wgrad_kernel(a0, a1, a2, b0, b1, b2, out):
-    total = lax.dot_general(a0[...], b0[...], FIRST, preferred_element_type=F32)
-    total += lax.dot_general(a1[...], b1[...], FIRST, preferred_element_type=F32)
-    total += lax.dot_general(a2[...], b2[...], FIRST, preferred_element_type=F32)
-    out[...] = total.astype(BF16)
+        x_all[rows, piece] = x_part[...]
+        y_all[rows, piece] = y_part[...]
+    expert_math(share, rows, spot, outs[:5], outs[5:7], weights)
+
+
+def wgrad_kernel(left, right, out, tile, sems):
+    blocks = tile.shape[0]
+    rows = tile.shape[1]
+    copies = []
+    for j in range(blocks):
+        part = left[:, j * rows : (j + 1) * rows]
+        total = lax.dot_general(part, right[...], FIRST, preferred_element_type=F32)
+        tile[j] = total.astype(BF16)
+        copy = pltpu.make_async_copy(tile.at[j], out.at[pl.ds(j * rows, rows)], sems.at[j])
+        copy.start()
+        copies.append(copy)
+    for copy in copies:
+        copy.wait()
 
 
 def combine_kernel(assign, r0, r1, r2, r3, out, rows):
@@ -243,12 +263,13 @@
 
 
 def place_kernel(share, *refs):
-    out = refs[-1]
+    out, sems = refs[-2:]
     block = lax.axis_index("dp")
-    near = parts_of(refs[4], 4)
-    for k in range(8):
-        piece = cols(jnp.bitwise_xor(block, k), share)
-        out[:, piece] = (near if k % 2 else refs)[k // 2][...]
+    mine, across = block_order()
+    pieces = [cols(jnp.bitwise_xor(block, k), share) for k in mine + across]
+    blocks = list(refs[:4]) + parts_of(refs[4], 4)
+    for copy in start_copies(sems, *[(b, out.at[:, p]) for b, p in zip(blocks, pieces)]):
+        copy.wait()
 
 
 def fence(*arrays):
@@ -270,24 +291,20 @@
     return [ref.at[pl.ds(j * rows, rows)] for j in range(count)]
 
 
+def swap_first(array):
+    return lax.ppermute(array, "dp", [(i, i ^ (4 if i % 2 else 2)) for i in range(8)])
+
+
+def swap_second(array):
+    return lax.ppermute(array, "dp", [(i, i ^ (2 if i % 2 else 4)) for i in range(8)])
+
+
 def core_pairs(even, other):
     return [(even[j].astype(F32) + other[j].astype(F32)).astype(BF16) for j in range(4)]
 
 
 def total_of(parts):
     return sum(part.astype(F32) for part in parts).astype(BF16)
-
-
-def expert_outs(rows, width, hidden, share, all_rows=None):
-    return [
-        shape(rows, width),
-        shape(rows, width),
-        shape(rows, hidden),
-        shape(rows, hidden),
-        shape(rows, hidden),
-        shape(4, all_rows or rows, share),
-        shape(4, all_rows or rows, share),
-    ]
 
 
 def per_device_blocks(tokens, grad_out, expert_ids, gate_prob, w_gate, w_up, w_down):
@@ -313,10 +330,16 @@
     )
     got1 = swap(send1, "expert", 1)
     got3 = swap(send3, "expert", 3)
+    total_rows = experts * capacity
+    chunk_a = slice(0, 2 * capacity)
+    chunk_own = slice(2 * capacity, 3 * capacity)
+    chunk_b = slice(3 * capacity, 4 * capacity)
+    shared = [shape(total_rows, width)] * 2 + [shape(total_rows, hidden_part)] * 3
+    terms_a = [shape(4, 3 * capacity, share)] * 2
+    terms_b = [shape(4, capacity, share)] * 2
     own_out = call(
-        functools.partial(own_kernel, share, 2 * capacity),
-        expert_outs(capacity, width, hidden_part, share, 3 * capacity)
-        + [shape(*w.shape) for w in weights],
+        functools.partial(own_kernel, share, chunk_own),
+        shared + terms_a + [shape(*w.shape) for w in weights],
         (prob, tokens, grad_out) + weights + (assign,),
         SMALL,
         20,
@@ -333,73 +356,74 @@
     block_a = jnp.concatenate(
         [got1[:capacity], got3[:capacity], got1[capacity:], got3[capacity:]], axis=0
     )
-    half_a, half_b = 2 * capacity, capacity
-    two_a = swap(block_a, "dp", 2)
-    four_a = swap(block_a, "dp", 4)
-    block_a, two_a, four_a, block_b = fence(block_a, two_a, four_a, block_b)
-
-    first_a = swap(two_a[:half_a], "dp", 4)
-    second_a = swap(four_a[half_a:], "dp", 2)
-    two_b = swap(block_b, "dp", 2)
-    four_b = swap(block_b, "dp", 4)
-    first_a, second_a, two_b, four_b = fence(first_a, second_a, two_b, four_b)
-
-    across_a = swap(jnp.concatenate([block_a, two_a, four_a, first_a, second_a]), "dp", 1)
-    first_b = swap(two_b[:half_b], "dp", 4)
-    second_b = swap(four_b[half_b:], "dp", 2)
+    first_a = swap_first(block_a)
+    second_a = swap_second(block_a)
+    first_a, block_b = fence(first_a, block_b)
+    third_a = swap_second(first_a)
+    first_b = swap_first(block_b)
+    second_b = swap_second(block_b)
+    second_a, third_a, first_b = fence(second_a, third_a, first_b)
+
+    across_a = swap(jnp.concatenate([block_a, first_a, second_a, third_a]), "dp", 1)
+    third_b = swap_second(first_b)
+    early_b = swap(jnp.concatenate([block_b, first_b]), "dp", 1)
     out_a = call(
-        functools.partial(chunk_kernel, share, 2),
-        expert_outs(2 * capacity, width, hidden_part, share, 3 * capacity),
-        (block_a, two_a, four_a, first_a, second_a, across_a, own_out[5], own_out[6]) + weights,
+        functools.partial(chunk_kernel, share, chunk_a, chunk_a, 1, 7),
+        shared + terms_a,
+        (block_a, first_a, second_a, third_a, across_a) + weights + tuple(own_out[:7]),
         SMALL,
         16,
-        aliases={6: 5, 7: 6},
-    )
-    first_b, second_b, *out_a = fence(first_b, second_b, *out_a)
-
+        aliases={8 + j: j for j in range(7)},
+    )
+    second_b, third_b, early_b, *out_a = fence(second_b, third_b, early_b, *out_a)
+
+    later_b, *out_a = fence(swap(jnp.concatenate([second_b, third_b]), "dp", 1), *out_a)
     other_a = swap(out_a[6], "dp", 1)
-    across_b = swap(jnp.concatenate([block_b, two_b, four_b, first_b, second_b]), "dp", 1)
-    other_a, across_b = fence(other_a, across_b)
-
-    pairs_a = core_pairs(out_a[5], other_a)
-    sums_a = [swap(pairs_a[j], "dp", 2 * j) for j in range(1, 4)]
     out_b = call(
-        functools.partial(chunk_kernel, share, 0),
-        expert_outs(capacity, width, hidden_part, share),
-        (block_b, two_b, four_b, first_b, second_b, across_b) + weights,
+        functools.partial(chunk_kernel, share, chunk_b, slice(0, capacity), 2, 5),
+        shared + terms_b,
+        (block_b, first_b, second_b, third_b, early_b, later_b) + weights + tuple(out_a[:5]),
         SMALL,
         16,
-    )
-    out_b = fence(*out_b)
-    sums_a[0], *rest = fence(sums_a[0], swap(out_b[6], "dp", 1), *out_b)
-    other_b, out_b = rest[0], rest[1:]
-
-    parts = (own_out, out_a, out_b)
-    rows_all = experts * capacity
-
-    def wgrad(left, right, rows, width_out):
+        aliases={9 + j: j for j in range(5)},
+    )
+    other_a, *out_b = fence(other_a, *out_b)
+    x_all, y_all, hidden, gate_grad, up_grad = out_b[:5]
+    (other_b,) = fence(swap(out_b[6], "dp", 1))
+
+    def wgrad(left, right):
+        blocks = 4
+        scratch = [
+            pltpu.VMEM((blocks, left.shape[1] // blocks, right.shape[1]), BF16),
+            pltpu.SemaphoreType.DMA((blocks,)),
+        ]
         (out,) = call(
             wgrad_kernel,
-            [shape(rows, width_out)],
-            [o[left] for o in parts] + [o[right] for o in parts],
-            2 * rows_all * rows * width_out,
+            [shape(left.shape[1], right.shape[1])],
+            (left, right),
+            SMALL,
             16,
+            scratch,
+            out_space=HBM,
         )
         return out
 
+    pairs_a = core_pairs(out_a[5], other_a)
     pairs_b = core_pairs(out_b[5], other_b)
-    sums_b = [swap(pairs_b[j], "dp", 2 * j) for j in range(1, 4)]
-    gate_wgrad = wgrad(0, 3, width, hidden_part)
-    *rest, gate_wgrad = fence(*sums_a, *sums_b, gate_wgrad)
-    sums_a, sums_b = rest[:3], rest[3:]
-
-    summed_a = total_of([pairs_a[0]] + sums_a)
-    ret0 = summed_a[2 * capacity :]
-    ret1 = swap(summed_a[:capacity], "expert", 1)
-    ret3 = swap(summed_a[capacity : 2 * capacity], "expert", 3)
-    ret2 = swap(total_of([pairs_b[0]] + sums_b), "expert", 2)
-    up_wgrad = wgrad(0, 4, width, hidden_part)
-    ret1, ret2, ret3, up_wgrad = fence(ret1, ret2, ret3, up_wgrad)
+    pairs = [jnp.concatenate([pairs_a[j], pairs_b[j]]) for j in range(4)]
+    relay = swap_second(pairs[3])
+    late = swap_second(pairs[2])
+    (relay,) = fence(relay)
+    last = swap_first(total_of([pairs[1], relay]))
+    up_wgrad = wgrad(x_all, up_grad)
+    last, late, up_wgrad, x_all = fence(last, late, up_wgrad, x_all)
+    summed = total_of([pairs[0], last, late])
+    ret0 = summed[chunk_own]
+    ret3 = swap(summed[capacity : 2 * capacity], "expert", 3)
+    ret1 = swap(summed[:capacity], "expert", 1)
+    ret2 = swap(summed[chunk_b], "expert", 2)
+    gate_wgrad = wgrad(x_all, gate_grad)
+    ret1, ret2, ret3, gate_wgrad = fence(ret1, ret2, ret3, gate_wgrad)
     (token_cols,) = call(
         combine_kernel,
         [shape(count, share)],
@@ -408,18 +432,20 @@
         8,
         [pltpu.VMEM((experts * capacity, share), BF16)],
     )
-    down_wgrad = wgrad(2, 1, hidden_part, width)
-    six = swap(token_cols, "dp", 6)
-    two = swap(token_cols, "dp", 2)
-    four = swap(token_cols, "dp", 4)
-    two, four, six, down_wgrad = fence(two, four, six, down_wgrad)
-    across = swap(jnp.concatenate([token_cols, two, four, six]), "dp", 1)
+    sixth = swap(token_cols, "dp", 6)
+    first = swap_first(token_cols)
+    second = swap_second(token_cols)
+    down_wgrad = wgrad(hidden, y_all)
+    first, second, sixth, down_wgrad = fence(first, second, sixth, down_wgrad)
+    across = swap(jnp.concatenate([token_cols, first, second, sixth]), "dp", 1)
     (grad_tokens,) = call(
         functools.partial(place_kernel, share),
         [shape(count, width)],
-        (token_cols, two, four, six, across),
+        (token_cols, first, second, sixth, across),
         SMALL,
         8,
+        [pltpu.SemaphoreType.DMA((8,))],
+        out_space=HBM,
     )
     return (grad_tokens, gate_wgrad[None], up_wgrad[None], down_wgrad[None])
 

time: 88.3 us -> 84.9 us (0.961)
  starting transfers between devices: 33 us -> 28.5 us
  waiting for transfers between devices: 26.5 us -> 30.3 us
  Pallas kernels: 27.1 us -> 24.1 us
    ppermute x28 -> x13, starting transfers between devices: 33 us -> 13.6 us  [swap(): return lax.ppermute(array, axis, [(i, i ^ distance) for i in range(size)])]
    ppermute x0 -> x11, starting transfers between devices: none -> 14.8 us  [the longest x7 9.41 us: swap_second(): lax.ppermute(array, 'dp', [(i, i ^ (2 if i % 2 else 4)) for i in range(8)])]
    ppermute x0 -> x11, waiting for transfers between devices: none -> 14.7 us  [the longest x7 7.85 us: swap_second(): lax.ppermute(array, 'dp', [(i, i ^ (2 if i % 2 else 4)) for i in range(8)])]
    ppermute x28 -> x13, waiting for transfers between devices: 26.5 us -> 15.6 us  [swap(): return lax.ppermute(array, axis, [(i, i ^ distance) for i in range(size)])]
    pallas_call x9, Pallas kernels: 27.1 us -> 24.1 us  [call(): pl.pallas_call(body, out_shape=outs, in_specs=[pl.BlockSpec(memory_space=...]
  transfers between devices with their start and end apart: 28 -> 24, of which waited for: 12 -> 16; matrix products, arithmetic and copies ran while one was open for 1% -> 0% of each run, Pallas kernels for 24% -> 25%
where the time goes in v3:
time: 84.9 us; the launch traced here: 84.7 us
  waiting for transfers between devices  30.3 us (36%)
  starting transfers between devices  28.5 us (34%)
  Pallas kernels  24.1 us (28%)
  between operations  1.03 us (1%)
    pallas_call x9, Pallas kernels, call(): pl.pallas_call(body, out_shape=outs, in_specs=[pl.BlockSpec(memory_space=...  24.1 us
    ppermute x13, waiting for transfers between devices, swap(): return lax.ppermute(array, axis, [(i, i ^ distance) for i in range(size)])  15.6 us
    ppermute x13, starting transfers between devices, swap(): return lax.ppermute(array, axis, [(i, i ^ distance) for i in range(size)])  13.6 us
    ppermute x7, starting transfers between devices, swap_second(): lax.ppermute(array, 'dp', [(i, i ^ (2 if i % 2 else 4)) for i in range(8)])  9.41 us
    ppermute x7, waiting for transfers between devices, swap_second(): lax.ppermute(array, 'dp', [(i, i ^ (2 if i % 2 else 4)) for i in range(8)])  7.85 us
    ppermute x4, waiting for transfers between devices, swap_first(): lax.ppermute(array, 'dp', [(i, i ^ (4 if i % 2 else 2)) for i in range(8)])  6.89 us
    ppermute x4, starting transfers between devices, swap_first(): lax.ppermute(array, 'dp', [(i, i ^ (4 if i % 2 else 2)) for i in range(8)])  5.44 us
  transfers between devices with their start and end apart: 24, of which 16 were waited for; matrix products, arithmetic and copies ran while one was open for 0% of the time, Pallas kernels for 25%

profile of v3, /device:TPU:0, one launch (start us, length us, event | category | flops | bytes accessed | tf_op | source)
XLA Modules:
  0.0 84.7 jit_solution(11056147758048836272)
XLA Ops:
  0.6 1.7 %shard_map.102 = (bf16[320,256]{1,0:T(8,128)(2,1)S(1)}, bf16[320,256]{1,0:T(8,128)(2,1)S(1)}, bf16[320,256]{1,0:T(8,128)(2,1)S(1)}, bf16[640,256]{1,0:T(8,128)(2,1)S(1)}) custom-call(s32[1,256]{1,0:T(1,128)} %bitcast.32, f32[1,256]{1,0:T(1,128)} %bitcast.30, bf16[256,2048]{1,0:T(8,128)(2,1)} %tok_far.1, bf16[256,2048]{1,0:T(8,128)(2,1)} %grad_far.1), custom_call_target="tpu_custom_call" | custom-call | flops 1000 | bytes 2918400 | tf_op jit(solution)/shard_map/pallas_call | solution.py:93
  2.3 3.1 %collective-permute-start = (bf16[320,256]{1,0:T(8,128)(2,1)S(1)}, bf16[320,256]{1,0:T(8,128)(2,1)S(1)}, u32[]{:S(2)}, u32[]{:S(2)}) collective-permute-start(bf16[320,256]{1,0:T(8,128)(2,1)S(1)} %get-tuple-element.99), channel_id=1, source_target_pairs={{0,1},{1,0},{2,3},{3,2},{4,5},{5,4},{6,7},{7,6},{8,9},{9,8},{10,11... | collective-permute-start | bytes 491528 | tf_op jit(solution)/shard_map/ppermute | solution.py:281
  5.4 2.5 %collective-permute-start.1 = (bf16[320,256]{1,0:T(8,128)(2,1)S(1)}, bf16[320,256]{1,0:T(8,128)(2,1)S(1)}, u32[]{:S(2)}, u32[]{:S(2)}) collective-permute-start(bf16[320,256]{1,0:T(8,128)(2,1)S(1)} %get-tuple-element.100), channel_id=1, source_target_pairs={{0,3},{1,2},{2,1},{3,0},{4,7},{5,6},{6,5},{7,4},{8,11},{9,10},{10,... | collective-permute-start | bytes 491528 | tf_op jit(solution)/shard_map/ppermute | solution.py:281
  7.9 5.8 %shard_map.103 = (bf16[640,2048]{1,0:T(8,128)(2,1)S(1)}, bf16[640,2048]{1,0:T(8,128)(2,1)S(1)}, bf16[640,512]{1,0:T(8,128)(2,1)S(1)}, bf16[640,512]{1,0:T(8,128)...) custom-call(f32[1,256]{1,0:T(1,128)} %bitcast.31, ...), custom_call_target="tpu_custom_call" | custom-call | flops 1000 | bytes 24183808 | tf_op jit(solution)/shard_map/pallas_call | solution.py:93
  13.7 1.7 %collective-permute-done.1 = bf16[320,256]{1,0:T(8,128)(2,1)S(1)} collective-permute-done((bf16[320,256]{1,0:T(8,128)(2,1)S(1)}, bf16[320,256]{1,0:T(8,128)(2,1)S(1)}, u32[]{:S(2)}, u32[]{:S(2)}) %collective-permute-start.1) | collective-permute-done | bytes 163872 | tf_op jit(solution)/shard_map/ppermute | solution.py:281
  15.5 1.6 %collective-permute-start.2 = (bf16[640,256]{1,0:T(8,128)(2,1)S(1)}, bf16[640,256]{1,0:T(8,128)(2,1)S(1)}, u32[]{:S(2)}, u32[]{:S(2)}) collective-permute-start(bf16[640,256]{1,0:T(8,128)(2,1)S(1)} %pad_maximum_fusion.1.refs_0_), channel_id=1, source_target_pairs={{0,8},{4,20},{8,0},{12,28},{16,24},{20,4},{24,16},{28,12},{1,9},{5... | collective-permute-start | bytes 983048 | tf_op jit(solution)/shard_map/ppermute | solution.py:295
  17.1 1.8 %collective-permute-start.3 = (bf16[320,256]{1,0:T(8,128)(2,1)S(1)}, bf16[320,256]{1,0:T(8,128)(2,1)S(1)}, u32[]{:S(2)}, u32[]{:S(2)}) collective-permute-start(bf16[320,256]{1,0:T(8,128)(2,1)S(1)} %get-tuple-element.124), channel_id=1, source_target_pairs={{0,2},{1,3},{2,0},{3,1},{4,6},{5,7},{6,4},{7,5},{8,10},{9,11},{10,... | collective-permute-start | bytes 491528 | tf_op jit(solution)/shard_map/ppermute | solution.py:281
  18.8 1.5 %collective-permute-start.5 = (bf16[640,256]{1,0:T(8,128)(2,1)S(1)}, bf16[640,256]{1,0:T(8,128)(2,1)S(1)}, u32[]{:S(2)}, u32[]{:S(2)}) collective-permute-start(bf16[640,256]{1,0:T(8,128)(2,1)S(1)} %pad_maximum_fusion.1.refs_0_), channel_id=1, source_target_pairs={{0,16},{4,12},{8,24},{12,4},{16,0},{20,28},{24,8},{28,20},{1,17},{... | collective-permute-start | bytes 983048 | tf_op jit(solution)/shard_map/ppermute | solution.py:299
  20.3 4.7 %collective-permute-done.3.refs_0_ = bf16[320,256]{1,0:T(8,128)(2,1)S(1)} collective-permute-done((bf16[320,256]{1,0:T(8,128)(2,1)S(1)}, bf16[320,256]{1,0:T(8,128)(2,1)S(1)}, u32[]{:S(2)}, u32[]{:S(2)}) %collective-permute-start.3) | collective-permute-done | bytes 163872 | tf_op jit(solution)/shard_map/ppermute | solution.py:281
  25.0 0.5 collective-permute-done.2.refs_1_
  25.6 2.0 %collective-permute-start.6 = (bf16[640,256]{1,0:T(8,128)(2,1)S(1)}, bf16[640,256]{1,0:T(8,128)(2,1)S(1)}, u32[]{:S(2)}, u32[]{:S(2)}) collective-permute-start(bf16[640,256]{1,0:T(8,128)(2,1)S(1)} %collective-permute-done.2.refs_1_), channel_id=1, source_target_pairs={{0,16},{4,12},{8,24},{12,4},{16,0},{20,28},{24,8},{28,20},{1,17},{... | collective-permute-start | bytes 983048 | tf_op jit(solution)/shard_map/ppermute | solution.py:299
  27.6 1.5 %collective-permute-start.7 = (bf16[320,256]{1,0:T(8,128)(2,1)S(1)}, bf16[320,256]{1,0:T(8,128)(2,1)S(1)}, u32[]{:S(2)}, u32[]{:S(2)}) collective-permute-start(bf16[320,256]{1,0:T(8,128)(2,1)S(1)} %collective-permute-done.3.refs_0_), channel_id=1, source_target_pairs={{0,8},{4,20},{8,0},{12,28},{16,24},{20,4},{24,16},{28,12},{1,9},{5... | collective-permute-start | bytes 491528 | tf_op jit(solution)/shard_map/ppermute | solution.py:295
  29.1 3.8 %collective-permute-done.7.refs_1_ = bf16[320,256]{1,0:T(8,128)(2,1)S(1)} collective-permute-done((bf16[320,256]{1,0:T(8,128)(2,1)S(1)}, bf16[320,256]{1,0:T(8,128)(2,1)S(1)}, u32[]{:S(2)}, u32[]{:S(2)}) %collective-permute-start.7) | collective-permute-done | bytes 163872 | tf_op jit(solution)/shard_map/ppermute | solution.py:295
  32.9 0.5 collective-permute-done.6.refs_3_
  33.6 0.6 collective-permute-start.9
  34.1 1.3 %collective-permute-start.4 = (bf16[320,256]{1,0:T(8,128)(2,1)S(1)}, bf16[320,256]{1,0:T(8,128)(2,1)S(1)}, u32[]{:S(2)}, u32[]{:S(2)}) collective-permute-start(bf16[320,256]{1,0:T(8,128)(2,1)S(1)} %collective-permute-done.3.refs_0_), channel_id=1, source_target_pairs={{0,16},{4,12},{8,24},{12,4},{16,0},{20,28},{24,8},{28,20},{1,17},{... | collective-permute-start | bytes 491528 | tf_op jit(solution)/shard_map/ppermute | solution.py:299
  35.4 0.8 collective-permute-start.8
  36.1 0.4 collective-permute-done.10.refs_4_
  36.6 4.0 %shard_map.104 = (bf16[640,2048]{1,0:T(8,128)(2,1)S(1)}, bf16[640,2048]{1,0:T(8,128)(2,1)S(1)}, bf16[640,512]{1,0:T(8,128)(2,1)S(1)}, bf16[640,512]{1,0:T(8,128)...) custom-call(bf16[640,256]{1,0:T(8,128)(2,1)S(1)} %pad_maximum_fusion, ...), custom_call_target="tpu_custom_call", output_to_operand_aliasing={{0}: (8, {}), {1}: (9, {}), {2}: (10, {}), {3}: (11, {}), {... | custom-call | flops 1000 | bytes 27262976 | tf_op jit(solution)/shard_map/pallas_call | solution.py:93
  40.6 0.6 collective-permute-done.8.refs_3_
  41.3 1.6 %collective-permute-done.11.refs_5_ = bf16[640,256]{1,0:T(8,128)(2,1)S(1)} collective-permute-done((bf16[640,256]{1,0:T(8,128)(2,1)S(1)}, bf16[640,256]{1,0:T(8,128)(2,1)S(1)}, u32[]{:S(2)}, u32[]{:S(2)}) %collective-permute-start.11) | collective-permute-done | bytes 327712 | tf_op jit(solution)/shard_map/ppermute | solution.py:281
  42.9 0.1 collective-permute-start.12
  43.1 3.1 %shard_map.105 = (bf16[640,2048]{1,0:T(8,128)(2,1)S(1)}, bf16[640,2048]{1,0:T(8,128)(2,1)S(1)}, bf16[640,512]{1,0:T(8,128)(2,1)S(1)}, bf16[640,512]{1,0:T(8,128)...) custom-call(bf16[320,256]{1,0:T(8,128)(2,1)S(1)} %collective-permute, ...), custom_call_target="tpu_custom_call", output_to_operand_aliasing={{0}: (9, {}), {1}: (10, {}), {2}: (11, {}), {3}: (12, {}), ... | custom-call | flops 1000 | bytes 22675456 | tf_op jit(solution)/shard_map/pallas_call | solution.py:93
  46.2 0.4 collective-permute-start.13
  46.6 0.2 fusion
  46.8 1.0 %collective-permute-done.13 = bf16[4,160,256]{2,1,0:T(8,128)(2,1)S(1)} collective-permute-done((bf16[4,160,256]{2,1,0:T(8,128)(2,1)S(1)}, bf16[4,160,256]{2,1,0:T(8,128)(2,1)S(1)}, u32[]{:S(2)}, u32[]{:S(2)}) %collective-permute-start.13) | collective-permute-done | bytes 327712 | tf_op jit(solution)/shard_map/ppermute | solution.py:281
  48.0 1.3 %collective-permute-start.14 = (bf16[640,256]{1,0:T(8,128)(2,1)S(1)}, bf16[640,256]{1,0:T(8,128)(2,1)S(1)}, u32[]{:S(2)}, u32[]{:S(2)}) collective-permute-start(bf16[640,256]{1,0:T(8,128)(2,1)S(1)} %pad_maximum_fusion.4), channel_id=1, source_target_pairs={{0,16},{4,12},{8,24},{12,4},{16,0},{20,28},{24,8},{28,20},{1,17},{... | collective-permute-start | bytes 983048 | tf_op jit(solution)/shard_map/ppermute | solution.py:299
  49.3 0.8 collective-permute-start.16
  50.2 5.0 %collective-permute-done.14 = bf16[640,256]{1,0:T(8,128)(2,1)S(1)} collective-permute-done((bf16[640,256]{1,0:T(8,128)(2,1)S(1)}, bf16[640,256]{1,0:T(8,128)(2,1)S(1)}, u32[]{:S(2)}, u32[]{:S(2)}) %collective-permute-start.14) | collective-permute-done | bytes 327712 | tf_op jit(solution)/shard_map/ppermute | solution.py:299
  55.2 1.1 %collective-permute-start.15 = (bf16[640,256]{1,0:T(8,128)(2,1)S(1)}, bf16[640,256]{1,0:T(8,128)(2,1)S(1)}, u32[]{:S(2)}, u32[]{:S(2)}) collective-permute-start(bf16[640,256]{1,0:T(8,128)(2,1)S(1)} %add_convert_fusion.1), channel_id=1, source_target_pairs={{0,8},{4,20},{8,0},{12,28},{16,24},{20,4},{24,16},{28,12},{1,9},{5... | collective-permute-start | bytes 983048 | tf_op jit(solution)/shard_map/ppermute | solution.py:295
  56.3 2.7 %shard_map.106 = bf16[2048,512]{1,0:T(8,128)(2,1)} custom-call(bf16[640,2048]{1,0:T(8,128)(2,1)S(1)} %get-tuple-element.179.left, bf16[640,512]{1,0:T(8,128)(2,1)S(1)} %get-tuple-element.176.right), custom_call_target="tpu_custom_call" | custom-call | flops 1000 | bytes 5373952 | tf_op jit(solution)/shard_map/pallas_call | solution.py:93
  58.9 0.9 %collective-permute-done.16 = bf16[640,256]{1,0:T(8,128)(2,1)S(1)} collective-permute-done((bf16[640,256]{1,0:T(8,128)(2,1)S(1)}, bf16[640,256]{1,0:T(8,128)(2,1)S(1)}, u32[]{:S(2)}, u32[]{:S(2)}) %collective-permute-start.16) | collective-permute-done | bytes 327712 | tf_op jit(solution)/shard_map/ppermute | solution.py:299
  59.8 2.5 %collective-permute-done.15 = bf16[640,256]{1,0:T(8,128)(2,1)S(1)} collective-permute-done((bf16[640,256]{1,0:T(8,128)(2,1)S(1)}, bf16[640,256]{1,0:T(8,128)(2,1)S(1)}, u32[]{:S(2)}, u32[]{:S(2)}) %collective-permute-start.15) | collective-permute-done | bytes 327712 | tf_op jit(solution)/shard_map/ppermute | solution.py:295
  62.3 0.1 add_convert_fusion
  62.5 0.2 collective-permute-start.17
  62.7 2.3 %collective-permute-start.18 = (bf16[160,256]{1,0:T(8,128)(2,1)S(1)}, bf16[160,256]{1,0:T(8,128)(2,1)S(1)}, u32[]{:S(2)}, u32[]{:S(2)}) collective-permute-start(bf16[160,256]{1,0:T(8,128)(2,1)S(1)} %get-tuple-element.201), channel_id=1, source_target_pairs={{0,2},{1,3},{2,0},{3,1},{4,6},{5,7},{6,4},{7,5},{8,10},{9,11},{10,... | collective-permute-start | bytes 245768 | tf_op jit(solution)/shard_map/ppermute | solution.py:281
  65.0 1.9 %collective-permute-start.19 = (bf16[160,256]{1,0:T(8,128)(2,1)S(1)}, bf16[160,256]{1,0:T(8,128)(2,1)S(1)}, u32[]{:S(2)}, u32[]{:S(2)}) collective-permute-start(bf16[160,256]{1,0:T(8,128)(2,1)S(1)} %get-tuple-element.200), channel_id=1, source_target_pairs={{0,3},{1,2},{2,1},{3,0},{4,7},{5,6},{6,5},{7,4},{8,11},{9,10},{10,... | collective-permute-start | bytes 245768 | tf_op jit(solution)/shard_map/ppermute | solution.py:281
  67.0 2.9 %shard_map.107 = bf16[2048,512]{1,0:T(8,128)(2,1)} custom-call(bf16[640,2048]{1,0:T(8,128)(2,1)S(1)} %get-tuple-element.179.left, bf16[640,512]{1,0:T(8,128)(2,1)S(1)} %get-tuple-element.180.right), custom_call_target="tpu_custom_call" | custom-call | flops 1000 | bytes 5373952 | tf_op jit(solution)/shard_map/pallas_call | solution.py:93
  69.8 2.5 %collective-permute-done.18.r2 = bf16[160,256]{1,0:T(8,128)(2,1)S(1)} collective-permute-done((bf16[160,256]{1,0:T(8,128)(2,1)S(1)}, bf16[160,256]{1,0:T(8,128)(2,1)S(1)}, u32[]{:S(2)}, u32[]{:S(2)}) %collective-permute-start.18) | collective-permute-done | bytes 81952 | tf_op jit(solution)/shard_map/ppermute | solution.py:281
  72.3 0.3 shard_map.108.refs_0_
  72.6 1.3 %collective-permute-start.20 = (bf16[256,256]{1,0:T(8,128)(2,1)S(1)}, bf16[256,256]{1,0:T(8,128)(2,1)S(1)}, u32[]{:S(2)}, u32[]{:S(2)}) collective-permute-start(bf16[256,256]{1,0:T(8,128)(2,1)S(1)} %shard_map.108.refs_0_), channel_id=1, source_target_pairs={{0,8},{4,20},{8,0},{12,28},{16,24},{20,4},{24,16},{28,12},{1,9},{5... | collective-permute-start | bytes 393224 | tf_op jit(solution)/shard_map/ppermute | solution.py:295
  73.9 1.7 %collective-permute-start.21 = (bf16[256,256]{1,0:T(8,128)(2,1)S(1)}, bf16[256,256]{1,0:T(8,128)(2,1)S(1)}, u32[]{:S(2)}, u32[]{:S(2)}) collective-permute-start(bf16[256,256]{1,0:T(8,128)(2,1)S(1)} %shard_map.108.refs_0_), channel_id=1, source_target_pairs={{0,16},{4,12},{8,24},{12,4},{16,0},{20,28},{24,8},{28,20},{1,17},{... | collective-permute-start | bytes 393224 | tf_op jit(solution)/shard_map/ppermute | solution.py:299
  75.7 0.5 collective-permute-start.22
  76.2 2.7 %shard_map.109 = bf16[512,2048]{1,0:T(8,128)(2,1)} custom-call(bf16[640,512]{1,0:T(8,128)(2,1)S(1)} %get-tuple-element.184.left, bf16[640,2048]{1,0:T(8,128)(2,1)S(1)} %get-tuple-element.185.right), custom_call_target="tpu_custom_call" | custom-call | flops 1000 | bytes 5373952 | tf_op jit(solution)/shard_map/pallas_call | solution.py:93
  78.8 0.9 %collective-permute-done.21.refs_2_ = bf16[256,256]{1,0:T(8,128)(2,1)S(1)} collective-permute-done((bf16[256,256]{1,0:T(8,128)(2,1)S(1)}, bf16[256,256]{1,0:T(8,128)(2,1)S(1)}, u32[]{:S(2)}, u32[]{:S(2)}) %collective-permute-start.21) | collective-permute-done | bytes 131104 | tf_op jit(solution)/shard_map/ppermute | solution.py:299
  79.8 1.8 %collective-permute-done.22.refs_3_ = bf16[256,256]{1,0:T(8,128)(2,1)S(1)} collective-permute-done((bf16[256,256]{1,0:T(8,128)(2,1)S(1)}, bf16[256,256]{1,0:T(8,128)(2,1)S(1)}, u32[]{:S(2)}, u32[]{:S(2)}) %collective-permute-start.22) | collective-permute-done | bytes 131104 | tf_op jit(solution)/shard_map/ppermute | solution.py:281
  81.6 1.9 %collective-permute-done.23.refs_4_ = bf16[1024,256]{1,0:T(8,128)(2,1)S(1)} collective-permute-done((bf16[1024,256]{1,0:T(8,128)(2,1)S(1)}, bf16[1024,256]{1,0:T(8,128)(2,1)S(1)}, u32[]{:S(2)}, u32[]{:S(2)}) %collective-permute-start.23) | collective-permute-done | bytes 524320 | tf_op jit(solution)/shard_map/ppermute | solution.py:281
  83.5 1.0 %shard_map.110 = bf16[256,2048]{1,0:T(8,128)(2,1)} custom-call(bf16[256,256]{1,0:T(8,128)(2,1)S(1)} %shard_map.108.refs_0_, bf16[256,256]{1,0:T(8,128)(2,1)S(1)} %collective-permute-done.20.refs_1_, bf16[256,256]{1,0:T(8,128)(2,1)S(1)} %collective-permute-done.21.refs_2_, bf16[256,256]{1,0:T(8,128)(2,1)S(1)} %collective-permute-done.22.refs_3_, ...), custom_call_target="tpu_custom_call" | custom-call | flops 1000 | bytes 2097152 | tf_op jit(solution)/shard_map/pallas_call | solution.py:93
  (27 shorter events, 0.7 us)
Async XLA Ops:
  2.3 11.4 %collective-permute-start = (bf16[320,256]{1,0:T(8,128)(2,1)S(1)}, bf16[320,256]{1,0:T(8,128)(2,1)S(1)}, u32[]{:S(2)}, u32[]{:S(2)}) collective-permute-start(bf16[320,256]{1,0:T(8,128)(2,1)S(1)} %get-tuple-element.99), channel_id=1, source_target_pairs={{0,1},{1,0},{2,3},{3,2},{4,5},{5,4},{6,7},{7,6},{8,9},{9,8},{10,11... | collective-permute-start | bytes 491528 | tf_op jit(solution)/shard_map/ppermute | solution.py:281
  5.4 10.0 %collective-permute-start.1 = (bf16[320,256]{1,0:T(8,128)(2,1)S(1)}, bf16[320,256]{1,0:T(8,128)(2,1)S(1)}, u32[]{:S(2)}, u32[]{:S(2)}) collective-permute-start(bf16[320,256]{1,0:T(8,128)(2,1)S(1)} %get-tuple-element.100), channel_id=1, source_target_pairs={{0,3},{1,2},{2,1},{3,0},{4,7},{5,6},{6,5},{7,4},{8,11},{9,10},{10,... | collective-permute-start | bytes 491528 | tf_op jit(solution)/shard_map/ppermute | solution.py:281
  15.5 10.1 %collective-permute-start.2 = (bf16[640,256]{1,0:T(8,128)(2,1)S(1)}, bf16[640,256]{1,0:T(8,128)(2,1)S(1)}, u32[]{:S(2)}, u32[]{:S(2)}) collective-permute-start(bf16[640,256]{1,0:T(8,128)(2,1)S(1)} %pad_maximum_fusion.1.refs_0_), channel_id=1, source_target_pairs={{0,8},{4,20},{8,0},{12,28},{16,24},{20,4},{24,16},{28,12},{1,9},{5... | collective-permute-start | bytes 983048 | tf_op jit(solution)/shard_map/ppermute | solution.py:295
  17.1 8.0 %collective-permute-start.3 = (bf16[320,256]{1,0:T(8,128)(2,1)S(1)}, bf16[320,256]{1,0:T(8,128)(2,1)S(1)}, u32[]{:S(2)}, u32[]{:S(2)}) collective-permute-start(bf16[320,256]{1,0:T(8,128)(2,1)S(1)} %get-tuple-element.124), channel_id=1, source_target_pairs={{0,2},{1,3},{2,0},{3,1},{4,6},{5,7},{6,4},{7,5},{8,10},{9,11},{10,... | collective-permute-start | bytes 491528 | tf_op jit(solution)/shard_map/ppermute | solution.py:281
  18.8 10.3 %collective-permute-start.5 = (bf16[640,256]{1,0:T(8,128)(2,1)S(1)}, bf16[640,256]{1,0:T(8,128)(2,1)S(1)}, u32[]{:S(2)}, u32[]{:S(2)}) collective-permute-start(bf16[640,256]{1,0:T(8,128)(2,1)S(1)} %pad_maximum_fusion.1.refs_0_), channel_id=1, source_target_pairs={{0,16},{4,12},{8,24},{12,4},{16,0},{20,28},{24,8},{28,20},{1,17},{... | collective-permute-start | bytes 983048 | tf_op jit(solution)/shard_map/ppermute | solution.py:299
  25.6 7.8 %collective-permute-start.6 = (bf16[640,256]{1,0:T(8,128)(2,1)S(1)}, bf16[640,256]{1,0:T(8,128)(2,1)S(1)}, u32[]{:S(2)}, u32[]{:S(2)}) collective-permute-start(bf16[640,256]{1,0:T(8,128)(2,1)S(1)} %collective-permute-done.2.refs_1_), channel_id=1, source_target_pairs={{0,16},{4,12},{8,24},{12,4},{16,0},{20,28},{24,8},{28,20},{1,17},{... | collective-permute-start | bytes 983048 | tf_op jit(solution)/shard_map/ppermute | solution.py:299
  27.6 5.3 %collective-permute-start.7 = (bf16[320,256]{1,0:T(8,128)(2,1)S(1)}, bf16[320,256]{1,0:T(8,128)(2,1)S(1)}, u32[]{:S(2)}, u32[]{:S(2)}) collective-permute-start(bf16[320,256]{1,0:T(8,128)(2,1)S(1)} %collective-permute-done.3.refs_0_), channel_id=1, source_target_pairs={{0,8},{4,20},{8,0},{12,28},{16,24},{20,4},{24,16},{28,12},{1,9},{5... | collective-permute-start | bytes 491528 | tf_op jit(solution)/shard_map/ppermute | solution.py:295
  33.5 3.1 %collective-permute-start.10 = (bf16[2560,256]{1,0:T(8,128)(2,1)S(1)}, bf16[2560,256]{1,0:T(8,128)(2,1)S(1)}, u32[]{:S(2)}, u32[]{:S(2)}) collective-permute-start(bf16[2560,256]{1,0:T(8,128)(2,1)S(1)} %constant_dynamic-update-slice_fusion), channel_id=1, source_target_pairs={{0,4},{4,0},{8,12},{12,8},{16,20},{20,16},{24,28},{28,24},{1,5},{5... | collective-permute-start | bytes 3932168 | tf_op jit(solution)/shard_map/ppermute | solution.py:281
  33.6 7.6 %collective-permute-start.9 = (bf16[640,256]{1,0:T(8,128)(2,1)S(1)}, bf16[640,256]{1,0:T(8,128)(2,1)S(1)}, u32[]{:S(2)}, u32[]{:S(2)}) collective-permute-start(bf16[640,256]{1,0:T(8,128)(2,1)S(1)} %pad_maximum_fusion.2), channel_id=1, source_target_pairs={{0,4},{4,0},{8,12},{12,8},{16,20},{20,16},{24,28},{28,24},{1,5},{5... | collective-permute-start | bytes 983048 | tf_op jit(solution)/shard_map/ppermute | solution.py:281
  34.1 6.4 %collective-permute-start.4 = (bf16[320,256]{1,0:T(8,128)(2,1)S(1)}, bf16[320,256]{1,0:T(8,128)(2,1)S(1)}, u32[]{:S(2)}, u32[]{:S(2)}) collective-permute-start(bf16[320,256]{1,0:T(8,128)(2,1)S(1)} %collective-permute-done.3.refs_0_), channel_id=1, source_target_pairs={{0,16},{4,12},{8,24},{12,4},{16,0},{20,28},{24,8},{28,20},{1,17},{... | collective-permute-start | bytes 491528 | tf_op jit(solution)/shard_map/ppermute | solution.py:299
  35.4 5.8 %collective-permute-start.8 = (bf16[320,256]{1,0:T(8,128)(2,1)S(1)}, bf16[320,256]{1,0:T(8,128)(2,1)S(1)}, u32[]{:S(2)}, u32[]{:S(2)}) collective-permute-start(bf16[320,256]{1,0:T(8,128)(2,1)S(1)} %collective-permute-done.7.refs_1_), channel_id=1, source_target_pairs={{0,16},{4,12},{8,24},{12,4},{16,0},{20,28},{24,8},{28,20},{1,17},{... | collective-permute-start | bytes 491528 | tf_op jit(solution)/shard_map/ppermute | solution.py:299
  41.2 1.7 %collective-permute-start.11 = (bf16[640,256]{1,0:T(8,128)(2,1)S(1)}, bf16[640,256]{1,0:T(8,128)(2,1)S(1)}, u32[]{:S(2)}, u32[]{:S(2)}) collective-permute-start(bf16[640,256]{1,0:T(8,128)(2,1)S(1)} %pad_maximum_fusion.3), channel_id=1, source_target_pairs={{0,4},{4,0},{8,12},{12,8},{16,20},{20,16},{24,28},{28,24},{1,5},{5... | collective-permute-start | bytes 983048 | tf_op jit(solution)/shard_map/ppermute | solution.py:281
  42.9 3.2 %collective-permute-start.12 = (bf16[4,480,256]{2,1,0:T(8,128)(2,1)S(1)}, bf16[4,480,256]{2,1,0:T(8,128)(2,1)S(1)}, u32[]{:S(2)}, u32[]{:S(2)}) collective-permute-start(bf16[4,480,256]{2,1,0:T(8,128)(2,1)S(1)} %get-tuple-element.157), channel_id=1, source_target_pairs={{0,4},{4,0},{8,12},{12,8},{16,20},{20,16},{24,28},{28,24},{1,5},{5... | collective-permute-start | bytes 2949128 | tf_op jit(solution)/shard_map/ppermute | solution.py:281
  46.2 1.7 %collective-permute-start.13 = (bf16[4,160,256]{2,1,0:T(8,128)(2,1)S(1)}, bf16[4,160,256]{2,1,0:T(8,128)(2,1)S(1)}, u32[]{:S(2)}, u32[]{:S(2)}) collective-permute-start(bf16[4,160,256]{2,1,0:T(8,128)(2,1)S(1)} %get-tuple-element.174), channel_id=1, source_target_pairs={{0,4},{4,0},{8,12},{12,8},{16,20},{20,16},{24,28},{28,24},{1,5},{5... | collective-permute-start | bytes 983048 | tf_op jit(solution)/shard_map/ppermute | solution.py:281
  48.0 7.1 %collective-permute-start.14 = (bf16[640,256]{1,0:T(8,128)(2,1)S(1)}, bf16[640,256]{1,0:T(8,128)(2,1)S(1)}, u32[]{:S(2)}, u32[]{:S(2)}) collective-permute-start(bf16[640,256]{1,0:T(8,128)(2,1)S(1)} %pad_maximum_fusion.4), channel_id=1, source_target_pairs={{0,16},{4,12},{8,24},{12,4},{16,0},{20,28},{24,8},{28,20},{1,17},{... | collective-permute-start | bytes 983048 | tf_op jit(solution)/shard_map/ppermute | solution.py:299
  49.3 10.5 %collective-permute-start.16 = (bf16[640,256]{1,0:T(8,128)(2,1)S(1)}, bf16[640,256]{1,0:T(8,128)(2,1)S(1)}, u32[]{:S(2)}, u32[]{:S(2)}) collective-permute-start(bf16[640,256]{1,0:T(8,128)(2,1)S(1)} %pad_maximum_fusion.5), channel_id=1, source_target_pairs={{0,16},{4,12},{8,24},{12,4},{16,0},{20,28},{24,8},{28,20},{1,17},{... | collective-permute-start | bytes 983048 | tf_op jit(solution)/shard_map/ppermute | solution.py:299
  55.2 7.1 %collective-permute-start.15 = (bf16[640,256]{1,0:T(8,128)(2,1)S(1)}, bf16[640,256]{1,0:T(8,128)(2,1)S(1)}, u32[]{:S(2)}, u32[]{:S(2)}) collective-permute-start(bf16[640,256]{1,0:T(8,128)(2,1)S(1)} %add_convert_fusion.1), channel_id=1, source_target_pairs={{0,8},{4,20},{8,0},{12,28},{16,24},{20,4},{24,16},{28,12},{1,9},{5... | collective-permute-start | bytes 983048 | tf_op jit(solution)/shard_map/ppermute | solution.py:295
  62.5 7.3 %collective-permute-start.17 = (bf16[160,256]{1,0:T(8,128)(2,1)S(1)}, bf16[160,256]{1,0:T(8,128)(2,1)S(1)}, u32[]{:S(2)}, u32[]{:S(2)}) collective-permute-start(bf16[160,256]{1,0:T(8,128)(2,1)S(1)} %get-tuple-element.202), channel_id=1, source_target_pairs={{0,1},{1,0},{2,3},{3,2},{4,5},{5,4},{6,7},{7,6},{8,9},{9,8},{10,11... | collective-permute-start | bytes 245768 | tf_op jit(solution)/shard_map/ppermute | solution.py:281
  62.7 9.6 %collective-permute-start.18 = (bf16[160,256]{1,0:T(8,128)(2,1)S(1)}, bf16[160,256]{1,0:T(8,128)(2,1)S(1)}, u32[]{:S(2)}, u32[]{:S(2)}) collective-permute-start(bf16[160,256]{1,0:T(8,128)(2,1)S(1)} %get-tuple-element.201), channel_id=1, source_target_pairs={{0,2},{1,3},{2,0},{3,1},{4,6},{5,7},{6,4},{7,5},{8,10},{9,11},{10,... | collective-permute-start | bytes 245768 | tf_op jit(solution)/shard_map/ppermute | solution.py:281
  65.0 7.3 %collective-permute-start.19 = (bf16[160,256]{1,0:T(8,128)(2,1)S(1)}, bf16[160,256]{1,0:T(8,128)(2,1)S(1)}, u32[]{:S(2)}, u32[]{:S(2)}) collective-permute-start(bf16[160,256]{1,0:T(8,128)(2,1)S(1)} %get-tuple-element.200), channel_id=1, source_target_pairs={{0,3},{1,2},{2,1},{3,0},{4,7},{5,6},{6,5},{7,4},{8,11},{9,10},{10,... | collective-permute-start | bytes 245768 | tf_op jit(solution)/shard_map/ppermute | solution.py:281
  72.6 6.2 %collective-permute-start.20 = (bf16[256,256]{1,0:T(8,128)(2,1)S(1)}, bf16[256,256]{1,0:T(8,128)(2,1)S(1)}, u32[]{:S(2)}, u32[]{:S(2)}) collective-permute-start(bf16[256,256]{1,0:T(8,128)(2,1)S(1)} %shard_map.108.refs_0_), channel_id=1, source_target_pairs={{0,8},{4,20},{8,0},{12,28},{16,24},{20,4},{24,16},{28,12},{1,9},{5... | collective-permute-start | bytes 393224 | tf_op jit(solution)/shard_map/ppermute | solution.py:295
  73.9 5.8 %collective-permute-start.21 = (bf16[256,256]{1,0:T(8,128)(2,1)S(1)}, bf16[256,256]{1,0:T(8,128)(2,1)S(1)}, u32[]{:S(2)}, u32[]{:S(2)}) collective-permute-start(bf16[256,256]{1,0:T(8,128)(2,1)S(1)} %shard_map.108.refs_0_), channel_id=1, source_target_pairs={{0,16},{4,12},{8,24},{12,4},{16,0},{20,28},{24,8},{28,20},{1,17},{... | collective-permute-start | bytes 393224 | tf_op jit(solution)/shard_map/ppermute | solution.py:299
  75.7 5.9 %collective-permute-start.22 = (bf16[256,256]{1,0:T(8,128)(2,1)S(1)}, bf16[256,256]{1,0:T(8,128)(2,1)S(1)}, u32[]{:S(2)}, u32[]{:S(2)}) collective-permute-start(bf16[256,256]{1,0:T(8,128)(2,1)S(1)} %shard_map.108.refs_0_), channel_id=1, source_target_pairs={{0,24},{4,28},{8,16},{12,20},{16,8},{20,12},{24,0},{28,4},{1,25},{... | collective-permute-start | bytes 393224 | tf_op jit(solution)/shard_map/ppermute | solution.py:281
  81.6 2.0 %collective-permute-start.23 = (bf16[1024,256]{1,0:T(8,128)(2,1)S(1)}, bf16[1024,256]{1,0:T(8,128)(2,1)S(1)}, u32[]{:S(2)}, u32[]{:S(2)}) collective-permute-start(bf16[1024,256]{1,0:T(8,128)(2,1)S(1)} %pad_maximum_fusion), channel_id=1, source_target_pairs={{0,4},{4,0},{8,12},{12,8},{16,20},{20,16},{24,28},{28,24},{1,5},{5... | collective-permute-start | bytes 1572872 | tf_op jit(solution)/shard_map/ppermute | solution.py:281

commit v4 on v3

--- a/solution.py
+++ b/solution.py
@@ -169,30 +169,85 @@
     return (0, first, second, 6), (1, second + 1, first + 1, 7)
 
 
+def forward_sums(parts, weights, ready=(lambda: None,) * 3):
+    sums = []
+    for weight, wait in zip(weights, ready):
+        wait()
+        total = 0.0
+        for x_part, y_part, piece in parts:
+            if weight is weights[2]:
+                total += lax.dot_general(
+                    y_part, weight[:, piece], LAST, preferred_element_type=F32
+                )
+            else:
+                total += jnp.dot(x_part, weight[piece, :], preferred_element_type=F32)
+        sums.append(total)
+    return sums
+
+
+def gradients(sums, hidden, gate_grad, up_grad, rows):
+    pre_gate, pre_up, hidden_grad = sums
+    activated, slope = silu_parts(pre_gate)
+    hidden[rows] = (activated * pre_up).astype(BF16)
+    gate_grad[rows] = (hidden_grad * pre_up * slope).astype(BF16)
+    up_grad[rows] = (hidden_grad * activated).astype(BF16)
+
+
+def input_terms(share, order, gate_part, up_part, w_gate, w_up, out, spot):
+    block = lax.axis_index("dp")
+    for j, k in enumerate(order):
+        piece = cols(jnp.bitwise_xor(block, k), share)
+        term = lax.dot_general(gate_part, w_gate[piece, :], LAST, preferred_element_type=F32)
+        term += lax.dot_general(up_part, w_up[piece, :], LAST, preferred_element_type=F32)
+        out[j, spot] = term.astype(BF16)
+
+
 def expert_math(share, rows, spot, shared, terms, weights, ready=(lambda: None,) * 3):
     x_all, y_all, hidden, gate_grad, up_grad = shared
-    even, odd = terms
-    w_gate, w_up, w_down = weights
+    sums = forward_sums([(x_all[rows], y_all[rows], slice(None))], weights, ready)
+    gradients(sums, hidden, gate_grad, up_grad, rows)
+    mine, across = block_order()
+    for out, order in zip(terms, (mine, across)):
+        input_terms(share, order, gate_grad[rows], up_grad[rows], weights[0], weights[1], out, spot)
+
+
+def early_kernel(share, *refs):
+    blocks = list(refs[:4]) + parts_of(refs[4], 2)
+    weights, outs = refs[5:8], refs[8:]
     block = lax.axis_index("dp")
-    ready[0]()
-    pre_gate = jnp.dot(x_all[rows], w_gate[...], preferred_element_type=F32)
-    ready[1]()
-    pre_up = jnp.dot(x_all[rows], w_up[...], preferred_element_type=F32)
-    ready[2]()
-    hidden_grad = lax.dot_general(y_all[rows], w_down[...], LAST, preferred_element_type=F32)
-    activated, slope = silu_parts(pre_gate)
-    hidden[rows] = (activated * pre_up).astype(BF16)
-    gate_part = (hidden_grad * pre_up * slope).astype(BF16)
-    up_part = (hidden_grad * activated).astype(BF16)
-    gate_grad[rows] = gate_part
-    up_grad[rows] = up_part
     mine, across = block_order()
-    for out, order in ((odd, across), (even, mine)):
-        for j, k in enumerate(order):
-            piece = cols(jnp.bitwise_xor(block, k), share)
-            term = lax.dot_general(gate_part, w_gate[piece, :], LAST, preferred_element_type=F32)
-            term += lax.dot_general(up_part, w_up[piece, :], LAST, preferred_element_type=F32)
-            out[j, spot] = term.astype(BF16)
+    parts = []
+    for k, ref in zip(mine + across[:2], blocks):
+        x_part, y_part = halves_of(ref)
+        parts.append((x_part[...], y_part[...], cols(jnp.bitwise_xor(block, k), share)))
+    for out, total in zip(outs, forward_sums(parts, weights)):
+        out[...] = total
+
+
+def late_kernel(share, rows, *refs):
+    blocks = list(refs[:4]) + parts_of(refs[4], 2) + parts_of(refs[5], 2)
+    early, weights = refs[6:9], refs[9:12]
+    x_all, y_all, hidden, gate_grad, up_grad, odd = refs[17:]
+    block = lax.axis_index("dp")
+    mine, across = block_order()
+    parts = []
+    for k, ref in zip(mine + across, blocks):
+        x_part, y_part = halves_of(ref)
+        piece = cols(jnp.bitwise_xor(block, k), share)
+        x_all[rows, piece] = x_part[...]
+        y_all[rows, piece] = y_part[...]
+        parts.append((x_part, y_part, piece))
+    parts = [(x_part[...], y_part[...], piece) for x_part, y_part, piece in parts[6:]]
+    sums = [total + part[...] for total, part in zip(forward_sums(parts, weights), early)]
+    gradients(sums, hidden, gate_grad, up_grad, rows)
+    input_terms(
+        share, across, gate_grad[rows], up_grad[rows], weights[0], weights[1], odd, slice(None)
+    )
+
+
+def even_kernel(share, rows, gate_grad, up_grad, w_gate, w_up, even):
+    mine, _ = block_order()
+    input_terms(share, mine, gate_grad[rows], up_grad[rows], w_gate, w_up, even, slice(None))
 
 
 def own_kernel(
@@ -377,19 +432,38 @@
     )
     second_b, third_b, early_b, *out_a = fence(second_b, third_b, early_b, *out_a)
 
-    later_b, *out_a = fence(swap(jnp.concatenate([second_b, third_b]), "dp", 1), *out_a)
+    partial = call(
+        functools.partial(early_kernel, share),
+        [shape(capacity, hidden_part, dtype=F32)] * 3,
+        (block_b, first_b, second_b, third_b, early_b) + weights,
+        SMALL,
+        16,
+    )
+    later_b = swap(jnp.concatenate([second_b, third_b]), "dp", 1)
+    later_b, *out_a = fence(later_b, *out_a, *partial)
+    out_a, partial = out_a[:7], tuple(out_a[7:])
     other_a = swap(out_a[6], "dp", 1)
     out_b = call(
-        functools.partial(chunk_kernel, share, chunk_b, slice(0, capacity), 2, 5),
-        shared + terms_b,
-        (block_b, first_b, second_b, third_b, early_b, later_b) + weights + tuple(out_a[:5]),
+        functools.partial(late_kernel, share, chunk_b),
+        shared + terms_b[:1],
+        (block_b, first_b, second_b, third_b, early_b, later_b)
+        + partial
+        + weights
+        + tuple(out_a[:5]),
         SMALL,
         16,
-        aliases={9 + j: j for j in range(5)},
+        aliases={12 + j: j for j in range(5)},
     )
     other_a, *out_b = fence(other_a, *out_b)
-    x_all, y_all, hidden, gate_grad, up_grad = out_b[:5]
-    (other_b,) = fence(swap(out_b[6], "dp", 1))
+    x_all, y_all, hidden, gate_grad, up_grad, odd_b = out_b
+    (even_b,) = call(
+        functools.partial(even_kernel, share, chunk_b),
+        terms_b[:1],
+        (gate_grad, up_grad) + weights[:2],
+        SMALL,
+        16,
+    )
+    other_b, even_b = fence(swap(odd_b, "dp", 1), even_b)
 
     def wgrad(left, right):
         blocks = 4
@@ -409,7 +483,7 @@
         return out
 
     pairs_a = core_pairs(out_a[5], other_a)
-    pairs_b = core_pairs(out_b[5], other_b)
+    pairs_b = core_pairs(even_b, other_b)
     pairs = [jnp.concatenate([pairs_a[j], pairs_b[j]]) for j in range(4)]
     relay = swap_second(pairs[3])
     late = swap_second(pairs[2])

time: 84.9 us -> 84.2 us (level)
    pallas_call x9 -> x11, Pallas kernels: 24.1 us -> 24.5 us  [call(): pl.pallas_call(body, out_shape=outs, in_specs=[pl.BlockSpec(memory_space=...]
  transfers between devices with their start and end apart: 24 -> 24, of which waited for: 16 -> 17; matrix products, arithmetic and copies ran while one was open for 0% -> 0% of each run, Pallas kernels for 25% -> 26%
where the time goes in v4:
time: 84.2 us; the launch traced here: 84 us
  waiting for transfers between devices  29.5 us (35%)
  starting transfers between devices  28.2 us (33%)
  Pallas kernels  24.5 us (29%)
  between operations  1.03 us (1%)
    pallas_call x11, Pallas kernels, call(): pl.pallas_call(body, out_shape=outs, in_specs=[pl.BlockSpec(memory_space=...  24.5 us
    ppermute x13, waiting for transfers between devices, swap(): return lax.ppermute(array, axis, [(i, i ^ distance) for i in range(size)])  14.7 us
    ppermute x13, starting transfers between devices, swap(): return lax.ppermute(array, axis, [(i, i ^ distance) for i in range(size)])  13.3 us
    ppermute x7, starting transfers between devices, swap_second(): lax.ppermute(array, 'dp', [(i, i ^ (2 if i % 2 else 4)) for i in range(8)])  9.4 us
    ppermute x7, waiting for transfers between devices, swap_second(): lax.ppermute(array, 'dp', [(i, i ^ (2 if i % 2 else 4)) for i in range(8)])  8.15 us
    ppermute x4, waiting for transfers between devices, swap_first(): lax.ppermute(array, 'dp', [(i, i ^ (4 if i % 2 else 2)) for i in range(8)])  6.64 us
    ppermute x4, starting transfers between devices, swap_first(): lax.ppermute(array, 'dp', [(i, i ^ (4 if i % 2 else 2)) for i in range(8)])  5.44 us
  transfers between devices with their start and end apart: 24, of which 17 were waited for; matrix products, arithmetic and copies ran while one was open for 0% of the time, Pallas kernels for 26%

profile of v4, /device:TPU:0, one launch (start us, length us, event | category | flops | bytes accessed | tf_op | source)
XLA Modules:
  0.0 84.0 jit_solution(10539809908364723224)
XLA Ops:
  0.6 1.7 %shard_map.102 = (bf16[320,256]{1,0:T(8,128)(2,1)S(1)}, bf16[320,256]{1,0:T(8,128)(2,1)S(1)}, bf16[320,256]{1,0:T(8,128)(2,1)S(1)}, bf16[640,256]{1,0:T(8,128)(2,1)S(1)}) custom-call(s32[1,256]{1,0:T(1,128)} %bitcast.32, f32[1,256]{1,0:T(1,128)} %bitcast.30, bf16[256,2048]{1,0:T(8,128)(2,1)} %tok_far.1, bf16[256,2048]{1,0:T(8,128)(2,1)} %grad_far.1), custom_call_target="tpu_custom_call" | custom-call | flops 1000 | bytes 2918400 | tf_op jit(solution)/shard_map/pallas_call | solution.py:93
  2.3 3.1 %collective-permute-start = (bf16[320,256]{1,0:T(8,128)(2,1)S(1)}, bf16[320,256]{1,0:T(8,128)(2,1)S(1)}, u32[]{:S(2)}, u32[]{:S(2)}) collective-permute-start(bf16[320,256]{1,0:T(8,128)(2,1)S(1)} %get-tuple-element.105), channel_id=1, source_target_pairs={{0,1},{1,0},{2,3},{3,2},{4,5},{5,4},{6,7},{7,6},{8,9},{9,8},{10,11... | collective-permute-start | bytes 491528 | tf_op jit(solution)/shard_map/ppermute | solution.py:336
  5.4 2.5 %collective-permute-start.1 = (bf16[320,256]{1,0:T(8,128)(2,1)S(1)}, bf16[320,256]{1,0:T(8,128)(2,1)S(1)}, u32[]{:S(2)}, u32[]{:S(2)}) collective-permute-start(bf16[320,256]{1,0:T(8,128)(2,1)S(1)} %get-tuple-element.106), channel_id=1, source_target_pairs={{0,3},{1,2},{2,1},{3,0},{4,7},{5,6},{6,5},{7,4},{8,11},{9,10},{10,... | collective-permute-start | bytes 491528 | tf_op jit(solution)/shard_map/ppermute | solution.py:336
  7.9 5.8 %shard_map.103 = (bf16[640,2048]{1,0:T(8,128)(2,1)S(1)}, bf16[640,2048]{1,0:T(8,128)(2,1)S(1)}, bf16[640,512]{1,0:T(8,128)(2,1)S(1)}, bf16[640,512]{1,0:T(8,128)...) custom-call(f32[1,256]{1,0:T(1,128)} %bitcast.31, ...), custom_call_target="tpu_custom_call" | custom-call | flops 1000 | bytes 24183808 | tf_op jit(solution)/shard_map/pallas_call | solution.py:93
  13.7 1.7 %collective-permute-done.1 = bf16[320,256]{1,0:T(8,128)(2,1)S(1)} collective-permute-done((bf16[320,256]{1,0:T(8,128)(2,1)S(1)}, bf16[320,256]{1,0:T(8,128)(2,1)S(1)}, u32[]{:S(2)}, u32[]{:S(2)}) %collective-permute-start.1) | collective-permute-done | bytes 163872 | tf_op jit(solution)/shard_map/ppermute | solution.py:336
  15.5 1.6 %collective-permute-start.2 = (bf16[640,256]{1,0:T(8,128)(2,1)S(1)}, bf16[640,256]{1,0:T(8,128)(2,1)S(1)}, u32[]{:S(2)}, u32[]{:S(2)}) collective-permute-start(bf16[640,256]{1,0:T(8,128)(2,1)S(1)} %pad_maximum_fusion.1.refs_0_), channel_id=1, source_target_pairs={{0,8},{4,20},{8,0},{12,28},{16,24},{20,4},{24,16},{28,12},{1,9},{5... | collective-permute-start | bytes 983048 | tf_op jit(solution)/shard_map/ppermute | solution.py:350
  17.1 1.8 %collective-permute-start.3 = (bf16[320,256]{1,0:T(8,128)(2,1)S(1)}, bf16[320,256]{1,0:T(8,128)(2,1)S(1)}, u32[]{:S(2)}, u32[]{:S(2)}) collective-permute-start(bf16[320,256]{1,0:T(8,128)(2,1)S(1)} %get-tuple-element.130), channel_id=1, source_target_pairs={{0,2},{1,3},{2,0},{3,1},{4,6},{5,7},{6,4},{7,5},{8,10},{9,11},{10,... | collective-permute-start | bytes 491528 | tf_op jit(solution)/shard_map/ppermute | solution.py:336
  18.8 1.5 %collective-permute-start.5 = (bf16[640,256]{1,0:T(8,128)(2,1)S(1)}, bf16[640,256]{1,0:T(8,128)(2,1)S(1)}, u32[]{:S(2)}, u32[]{:S(2)}) collective-permute-start(bf16[640,256]{1,0:T(8,128)(2,1)S(1)} %pad_maximum_fusion.1.refs_0_), channel_id=1, source_target_pairs={{0,16},{4,12},{8,24},{12,4},{16,0},{20,28},{24,8},{28,20},{1,17},{... | collective-permute-start | bytes 983048 | tf_op jit(solution)/shard_map/ppermute | solution.py:354
  20.3 4.7 %collective-permute-done.3.refs_0_ = bf16[320,256]{1,0:T(8,128)(2,1)S(1)} collective-permute-done((bf16[320,256]{1,0:T(8,128)(2,1)S(1)}, bf16[320,256]{1,0:T(8,128)(2,1)S(1)}, u32[]{:S(2)}, u32[]{:S(2)}) %collective-permute-start.3) | collective-permute-done | bytes 163872 | tf_op jit(solution)/shard_map/ppermute | solution.py:336
  25.0 0.5 collective-permute-done.2.refs_1_
  25.6 2.0 %collective-permute-start.6 = (bf16[640,256]{1,0:T(8,128)(2,1)S(1)}, bf16[640,256]{1,0:T(8,128)(2,1)S(1)}, u32[]{:S(2)}, u32[]{:S(2)}) collective-permute-start(bf16[640,256]{1,0:T(8,128)(2,1)S(1)} %collective-permute-done.2.refs_1_), channel_id=1, source_target_pairs={{0,16},{4,12},{8,24},{12,4},{16,0},{20,28},{24,8},{28,20},{1,17},{... | collective-permute-start | bytes 983048 | tf_op jit(solution)/shard_map/ppermute | solution.py:354
  27.6 1.5 %collective-permute-start.7 = (bf16[320,256]{1,0:T(8,128)(2,1)S(1)}, bf16[320,256]{1,0:T(8,128)(2,1)S(1)}, u32[]{:S(2)}, u32[]{:S(2)}) collective-permute-start(bf16[320,256]{1,0:T(8,128)(2,1)S(1)} %collective-permute-done.3.refs_0_), channel_id=1, source_target_pairs={{0,8},{4,20},{8,0},{12,28},{16,24},{20,4},{24,16},{28,12},{1,9},{5... | collective-permute-start | bytes 491528 | tf_op jit(solution)/shard_map/ppermute | solution.py:350
  29.1 3.8 %collective-permute-done.7.refs_1_ = bf16[320,256]{1,0:T(8,128)(2,1)S(1)} collective-permute-done((bf16[320,256]{1,0:T(8,128)(2,1)S(1)}, bf16[320,256]{1,0:T(8,128)(2,1)S(1)}, u32[]{:S(2)}, u32[]{:S(2)}) %collective-permute-start.7) | collective-permute-done | bytes 163872 | tf_op jit(solution)/shard_map/ppermute | solution.py:350
  32.9 0.5 collective-permute-done.6.refs_3_
  33.6 0.6 collective-permute-start.9
  34.1 1.2 %collective-permute-start.4 = (bf16[320,256]{1,0:T(8,128)(2,1)S(1)}, bf16[320,256]{1,0:T(8,128)(2,1)S(1)}, u32[]{:S(2)}, u32[]{:S(2)}) collective-permute-start(bf16[320,256]{1,0:T(8,128)(2,1)S(1)} %collective-permute-done.3.refs_0_), channel_id=1, source_target_pairs={{0,16},{4,12},{8,24},{12,4},{16,0},{20,28},{24,8},{28,20},{1,17},{... | collective-permute-start | bytes 491528 | tf_op jit(solution)/shard_map/ppermute | solution.py:354
  35.4 0.8 collective-permute-start.8
  36.2 0.4 collective-permute-done.10.refs_4_
  36.6 4.0 %shard_map.104 = (bf16[640,2048]{1,0:T(8,128)(2,1)S(1)}, bf16[640,2048]{1,0:T(8,128)(2,1)S(1)}, bf16[640,512]{1,0:T(8,128)(2,1)S(1)}, bf16[640,512]{1,0:T(8,128)...) custom-call(bf16[640,256]{1,0:T(8,128)(2,1)S(1)} %pad_maximum_fusion, ...), custom_call_target="tpu_custom_call", output_to_operand_aliasing={{0}: (8, {}), {1}: (9, {}), {2}: (10, {}), {3}: (11, {}), {... | custom-call | flops 1000 | bytes 27262976 | tf_op jit(solution)/shard_map/pallas_call | solution.py:93
  40.6 0.6 collective-permute-done.8.refs_3_
  41.3 1.2 %shard_map.105 = (f32[160,512]{1,0:T(8,128)S(1)}, f32[160,512]{1,0:T(8,128)S(1)}, f32[160,512]{1,0:T(8,128)S(1)}) custom-call(bf16[320,256]{1,0:T(8,128)(2,1)S(1)} %collective-permute-done.3.refs_0_, bf16[320,256]{1,0:T(8,128)(2,1)S(1)} %collective-permute-done.7.refs_1_, bf16[320,256]{1,0:T(8,128)(2,1)S(1)} %collective-permute-done.4.refs_2_, ...), custom_call_target="tpu_custom_call" | custom-call | flops 1000 | bytes 8257536 | tf_op jit(solution)/shard_map/pallas_call | solution.py:93
  42.5 0.4 collective-permute-done.11.refs_5_
  43.1 1.5 %shard_map.106 = (bf16[640,2048]{1,0:T(8,128)(2,1)S(1)}, bf16[640,2048]{1,0:T(8,128)(2,1)S(1)}, bf16[640,512]{1,0:T(8,128)(2,1)S(1)}, bf16[640,512]{1,0:T(8,128)...) custom-call(bf16[320,256]{1,0:T(8,128)(2,1)S(1)} %collective-permute, ...), custom_call_target="tpu_custom_call", output_to_operand_aliasing={{0}: (12, {}), {1}: (13, {}), {2}: (14, {}), {3}: (15, {}),... | custom-call | flops 1000 | bytes 23330816 | tf_op jit(solution)/shard_map/pallas_call | solution.py:93
  44.5 1.0 %collective-permute-done.12 = bf16[4,480,256]{2,1,0:T(8,128)(2,1)S(1)} collective-permute-done((bf16[4,480,256]{2,1,0:T(8,128)(2,1)S(1)}, bf16[4,480,256]{2,1,0:T(8,128)(2,1)S(1)}, u32[]{:S(2)}, u32[]{:S(2)}) %collective-permute-start.12) | collective-permute-done | bytes 983072 | tf_op jit(solution)/shard_map/ppermute | solution.py:336
  45.6 0.8 shard_map.107
  46.5 0.2 fusion
  46.7 0.4 collective-permute-done.13
  47.2 1.3 %collective-permute-start.14 = (bf16[640,256]{1,0:T(8,128)(2,1)S(1)}, bf16[640,256]{1,0:T(8,128)(2,1)S(1)}, u32[]{:S(2)}, u32[]{:S(2)}) collective-permute-start(bf16[640,256]{1,0:T(8,128)(2,1)S(1)} %pad_maximum_fusion.4), channel_id=1, source_target_pairs={{0,16},{4,12},{8,24},{12,4},{16,0},{20,28},{24,8},{28,20},{1,17},{... | collective-permute-start | bytes 983048 | tf_op jit(solution)/shard_map/ppermute | solution.py:354
  48.6 0.8 %collective-permute-start.16 = (bf16[640,256]{1,0:T(8,128)(2,1)S(1)}, bf16[640,256]{1,0:T(8,128)(2,1)S(1)}, u32[]{:S(2)}, u32[]{:S(2)}) collective-permute-start(bf16[640,256]{1,0:T(8,128)(2,1)S(1)} %pad_maximum_fusion.5), channel_id=1, source_target_pairs={{0,16},{4,12},{8,24},{12,4},{16,0},{20,28},{24,8},{28,20},{1,17},{... | collective-permute-start | bytes 983048 | tf_op jit(solution)/shard_map/ppermute | solution.py:354
  49.4 5.0 %collective-permute-done.14 = bf16[640,256]{1,0:T(8,128)(2,1)S(1)} collective-permute-done((bf16[640,256]{1,0:T(8,128)(2,1)S(1)}, bf16[640,256]{1,0:T(8,128)(2,1)S(1)}, u32[]{:S(2)}, u32[]{:S(2)}) %collective-permute-start.14) | collective-permute-done | bytes 327712 | tf_op jit(solution)/shard_map/ppermute | solution.py:354
  54.5 1.1 %collective-permute-start.15 = (bf16[640,256]{1,0:T(8,128)(2,1)S(1)}, bf16[640,256]{1,0:T(8,128)(2,1)S(1)}, u32[]{:S(2)}, u32[]{:S(2)}) collective-permute-start(bf16[640,256]{1,0:T(8,128)(2,1)S(1)} %add_convert_fusion.1), channel_id=1, source_target_pairs={{0,8},{4,20},{8,0},{12,28},{16,24},{20,4},{24,16},{28,12},{1,9},{5... | collective-permute-start | bytes 983048 | tf_op jit(solution)/shard_map/ppermute | solution.py:350
  55.5 2.7 %shard_map.108 = bf16[2048,512]{1,0:T(8,128)(2,1)} custom-call(bf16[640,2048]{1,0:T(8,128)(2,1)S(1)} %get-tuple-element.192.left, bf16[640,512]{1,0:T(8,128)(2,1)S(1)} %get-tuple-element.186.up_grad.right), custom_call_target="tpu_custom_call" | custom-call | flops 1000 | bytes 5373952 | tf_op jit(solution)/shard_map/pallas_call | solution.py:93
  58.2 1.1 %collective-permute-done.16 = bf16[640,256]{1,0:T(8,128)(2,1)S(1)} collective-permute-done((bf16[640,256]{1,0:T(8,128)(2,1)S(1)}, bf16[640,256]{1,0:T(8,128)(2,1)S(1)}, u32[]{:S(2)}, u32[]{:S(2)}) %collective-permute-start.16) | collective-permute-done | bytes 327712 | tf_op jit(solution)/shard_map/ppermute | solution.py:354
  59.3 2.3 %collective-permute-done.15 = bf16[640,256]{1,0:T(8,128)(2,1)S(1)} collective-permute-done((bf16[640,256]{1,0:T(8,128)(2,1)S(1)}, bf16[640,256]{1,0:T(8,128)(2,1)S(1)}, u32[]{:S(2)}, u32[]{:S(2)}) %collective-permute-start.15) | collective-permute-done | bytes 327712 | tf_op jit(solution)/shard_map/ppermute | solution.py:350
  61.8 0.2 collective-permute-start.17
  62.0 2.3 %collective-permute-start.18 = (bf16[160,256]{1,0:T(8,128)(2,1)S(1)}, bf16[160,256]{1,0:T(8,128)(2,1)S(1)}, u32[]{:S(2)}, u32[]{:S(2)}) collective-permute-start(bf16[160,256]{1,0:T(8,128)(2,1)S(1)} %get-tuple-element.213), channel_id=1, source_target_pairs={{0,2},{1,3},{2,0},{3,1},{4,6},{5,7},{6,4},{7,5},{8,10},{9,11},{10,... | collective-permute-start | bytes 245768 | tf_op jit(solution)/shard_map/ppermute | solution.py:336
  64.3 1.9 %collective-permute-start.19 = (bf16[160,256]{1,0:T(8,128)(2,1)S(1)}, bf16[160,256]{1,0:T(8,128)(2,1)S(1)}, u32[]{:S(2)}, u32[]{:S(2)}) collective-permute-start(bf16[160,256]{1,0:T(8,128)(2,1)S(1)} %get-tuple-element.212), channel_id=1, source_target_pairs={{0,3},{1,2},{2,1},{3,0},{4,7},{5,6},{6,5},{7,4},{8,11},{9,10},{10,... | collective-permute-start | bytes 245768 | tf_op jit(solution)/shard_map/ppermute | solution.py:336
  66.2 2.8 %shard_map.109 = bf16[2048,512]{1,0:T(8,128)(2,1)} custom-call(bf16[640,2048]{1,0:T(8,128)(2,1)S(1)} %get-tuple-element.192.left, bf16[640,512]{1,0:T(8,128)(2,1)S(1)} %get-tuple-element.185.gate_grad.right), custom_call_target="tpu_custom_call" | custom-call | flops 1000 | bytes 5373952 | tf_op jit(solution)/shard_map/pallas_call | solution.py:93
  69.1 2.5 %collective-permute-done.18.r2 = bf16[160,256]{1,0:T(8,128)(2,1)S(1)} collective-permute-done((bf16[160,256]{1,0:T(8,128)(2,1)S(1)}, bf16[160,256]{1,0:T(8,128)(2,1)S(1)}, u32[]{:S(2)}, u32[]{:S(2)}) %collective-permute-start.18) | collective-permute-done | bytes 81952 | tf_op jit(solution)/shard_map/ppermute | solution.py:336
  71.6 0.3 shard_map.110.refs_0_
  71.9 1.3 %collective-permute-start.20 = (bf16[256,256]{1,0:T(8,128)(2,1)S(1)}, bf16[256,256]{1,0:T(8,128)(2,1)S(1)}, u32[]{:S(2)}, u32[]{:S(2)}) collective-permute-start(bf16[256,256]{1,0:T(8,128)(2,1)S(1)} %shard_map.110.refs_0_), channel_id=1, source_target_pairs={{0,8},{4,20},{8,0},{12,28},{16,24},{20,4},{24,16},{28,12},{1,9},{5... | collective-permute-start | bytes 393224 | tf_op jit(solution)/shard_map/ppermute | solution.py:350
  73.2 1.7 %collective-permute-start.21 = (bf16[256,256]{1,0:T(8,128)(2,1)S(1)}, bf16[256,256]{1,0:T(8,128)(2,1)S(1)}, u32[]{:S(2)}, u32[]{:S(2)}) collective-permute-start(bf16[256,256]{1,0:T(8,128)(2,1)S(1)} %shard_map.110.refs_0_), channel_id=1, source_target_pairs={{0,16},{4,12},{8,24},{12,4},{16,0},{20,28},{24,8},{28,20},{1,17},{... | collective-permute-start | bytes 393224 | tf_op jit(solution)/shard_map/ppermute | solution.py:354
  74.9 0.5 collective-permute-start.22
  75.4 2.7 %shard_map.111 = bf16[512,2048]{1,0:T(8,128)(2,1)} custom-call(bf16[640,512]{1,0:T(8,128)(2,1)S(1)} %get-tuple-element.196.left, bf16[640,2048]{1,0:T(8,128)(2,1)S(1)} %get-tuple-element.197.right), custom_call_target="tpu_custom_call" | custom-call | flops 1000 | bytes 5373952 | tf_op jit(solution)/shard_map/pallas_call | solution.py:93
  78.1 0.9 %collective-permute-done.21.refs_2_ = bf16[256,256]{1,0:T(8,128)(2,1)S(1)} collective-permute-done((bf16[256,256]{1,0:T(8,128)(2,1)S(1)}, bf16[256,256]{1,0:T(8,128)(2,1)S(1)}, u32[]{:S(2)}, u32[]{:S(2)}) %collective-permute-start.21) | collective-permute-done | bytes 131104 | tf_op jit(solution)/shard_map/ppermute | solution.py:354
  79.0 1.8 %collective-permute-done.22.refs_3_ = bf16[256,256]{1,0:T(8,128)(2,1)S(1)} collective-permute-done((bf16[256,256]{1,0:T(8,128)(2,1)S(1)}, bf16[256,256]{1,0:T(8,128)(2,1)S(1)}, u32[]{:S(2)}, u32[]{:S(2)}) %collective-permute-start.22) | collective-permute-done | bytes 131104 | tf_op jit(solution)/shard_map/ppermute | solution.py:336
  80.9 1.9 %collective-permute-done.23.refs_4_ = bf16[1024,256]{1,0:T(8,128)(2,1)S(1)} collective-permute-done((bf16[1024,256]{1,0:T(8,128)(2,1)S(1)}, bf16[1024,256]{1,0:T(8,128)(2,1)S(1)}, u32[]{:S(2)}, u32[]{:S(2)}) %collective-permute-start.23) | collective-permute-done | bytes 524320 | tf_op jit(solution)/shard_map/ppermute | solution.py:336
  82.8 1.0 %shard_map.112 = bf16[256,2048]{1,0:T(8,128)(2,1)} custom-call(bf16[256,256]{1,0:T(8,128)(2,1)S(1)} %shard_map.110.refs_0_, bf16[256,256]{1,0:T(8,128)(2,1)S(1)} %collective-permute-done.20.refs_1_, bf16[256,256]{1,0:T(8,128)(2,1)S(1)} %collective-permute-done.21.refs_2_, bf16[256,256]{1,0:T(8,128)(2,1)S(1)} %collective-permute-done.22.refs_3_, ...), custom_call_target="tpu_custom_call" | custom-call | flops 1000 | bytes 2097152 | tf_op jit(solution)/shard_map/pallas_call | solution.py:93
  (29 shorter events, 1.1 us)
Async XLA Ops:
  2.3 11.4 %collective-permute-start = (bf16[320,256]{1,0:T(8,128)(2,1)S(1)}, bf16[320,256]{1,0:T(8,128)(2,1)S(1)}, u32[]{:S(2)}, u32[]{:S(2)}) collective-permute-start(bf16[320,256]{1,0:T(8,128)(2,1)S(1)} %get-tuple-element.105), channel_id=1, source_target_pairs={{0,1},{1,0},{2,3},{3,2},{4,5},{5,4},{6,7},{7,6},{8,9},{9,8},{10,11... | collective-permute-start | bytes 491528 | tf_op jit(solution)/shard_map/ppermute | solution.py:336
  5.4 10.0 %collective-permute-start.1 = (bf16[320,256]{1,0:T(8,128)(2,1)S(1)}, bf16[320,256]{1,0:T(8,128)(2,1)S(1)}, u32[]{:S(2)}, u32[]{:S(2)}) collective-permute-start(bf16[320,256]{1,0:T(8,128)(2,1)S(1)} %get-tuple-element.106), channel_id=1, source_target_pairs={{0,3},{1,2},{2,1},{3,0},{4,7},{5,6},{6,5},{7,4},{8,11},{9,10},{10,... | collective-permute-start | bytes 491528 | tf_op jit(solution)/shard_map/ppermute | solution.py:336
  15.5 10.1 %collective-permute-start.2 = (bf16[640,256]{1,0:T(8,128)(2,1)S(1)}, bf16[640,256]{1,0:T(8,128)(2,1)S(1)}, u32[]{:S(2)}, u32[]{:S(2)}) collective-permute-start(bf16[640,256]{1,0:T(8,128)(2,1)S(1)} %pad_maximum_fusion.1.refs_0_), channel_id=1, source_target_pairs={{0,8},{4,20},{8,0},{12,28},{16,24},{20,4},{24,16},{28,12},{1,9},{5... | collective-permute-start | bytes 983048 | tf_op jit(solution)/shard_map/ppermute | solution.py:350
  17.1 8.0 %collective-permute-start.3 = (bf16[320,256]{1,0:T(8,128)(2,1)S(1)}, bf16[320,256]{1,0:T(8,128)(2,1)S(1)}, u32[]{:S(2)}, u32[]{:S(2)}) collective-permute-start(bf16[320,256]{1,0:T(8,128)(2,1)S(1)} %get-tuple-element.130), channel_id=1, source_target_pairs={{0,2},{1,3},{2,0},{3,1},{4,6},{5,7},{6,4},{7,5},{8,10},{9,11},{10,... | collective-permute-start | bytes 491528 | tf_op jit(solution)/shard_map/ppermute | solution.py:336
  18.8 10.3 %collective-permute-start.5 = (bf16[640,256]{1,0:T(8,128)(2,1)S(1)}, bf16[640,256]{1,0:T(8,128)(2,1)S(1)}, u32[]{:S(2)}, u32[]{:S(2)}) collective-permute-start(bf16[640,256]{1,0:T(8,128)(2,1)S(1)} %pad_maximum_fusion.1.refs_0_), channel_id=1, source_target_pairs={{0,16},{4,12},{8,24},{12,4},{16,0},{20,28},{24,8},{28,20},{1,17},{... | collective-permute-start | bytes 983048 | tf_op jit(solution)/shard_map/ppermute | solution.py:354
  25.6 7.8 %collective-permute-start.6 = (bf16[640,256]{1,0:T(8,128)(2,1)S(1)}, bf16[640,256]{1,0:T(8,128)(2,1)S(1)}, u32[]{:S(2)}, u32[]{:S(2)}) collective-permute-start(bf16[640,256]{1,0:T(8,128)(2,1)S(1)} %collective-permute-done.2.refs_1_), channel_id=1, source_target_pairs={{0,16},{4,12},{8,24},{12,4},{16,0},{20,28},{24,8},{28,20},{1,17},{... | collective-permute-start | bytes 983048 | tf_op jit(solution)/shard_map/ppermute | solution.py:354
  27.6 5.3 %collective-permute-start.7 = (bf16[320,256]{1,0:T(8,128)(2,1)S(1)}, bf16[320,256]{1,0:T(8,128)(2,1)S(1)}, u32[]{:S(2)}, u32[]{:S(2)}) collective-permute-start(bf16[320,256]{1,0:T(8,128)(2,1)S(1)} %collective-permute-done.3.refs_0_), channel_id=1, source_target_pairs={{0,8},{4,20},{8,0},{12,28},{16,24},{20,4},{24,16},{28,12},{1,9},{5... | collective-permute-start | bytes 491528 | tf_op jit(solution)/shard_map/ppermute | solution.py:350
  33.5 3.1 %collective-permute-start.10 = (bf16[2560,256]{1,0:T(8,128)(2,1)S(1)}, bf16[2560,256]{1,0:T(8,128)(2,1)S(1)}, u32[]{:S(2)}, u32[]{:S(2)}) collective-permute-start(bf16[2560,256]{1,0:T(8,128)(2,1)S(1)} %constant_dynamic-update-slice_fusion), channel_id=1, source_target_pairs={{0,4},{4,0},{8,12},{12,8},{16,20},{20,16},{24,28},{28,24},{1,5},{5... | collective-permute-start | bytes 3932168 | tf_op jit(solution)/shard_map/ppermute | solution.py:336
  33.6 7.6 %collective-permute-start.9 = (bf16[640,256]{1,0:T(8,128)(2,1)S(1)}, bf16[640,256]{1,0:T(8,128)(2,1)S(1)}, u32[]{:S(2)}, u32[]{:S(2)}) collective-permute-start(bf16[640,256]{1,0:T(8,128)(2,1)S(1)} %pad_maximum_fusion.2), channel_id=1, source_target_pairs={{0,4},{4,0},{8,12},{12,8},{16,20},{20,16},{24,28},{28,24},{1,5},{5... | collective-permute-start | bytes 983048 | tf_op jit(solution)/shard_map/ppermute | solution.py:336
  34.1 6.4 %collective-permute-start.4 = (bf16[320,256]{1,0:T(8,128)(2,1)S(1)}, bf16[320,256]{1,0:T(8,128)(2,1)S(1)}, u32[]{:S(2)}, u32[]{:S(2)}) collective-permute-start(bf16[320,256]{1,0:T(8,128)(2,1)S(1)} %collective-permute-done.3.refs_0_), channel_id=1, source_target_pairs={{0,16},{4,12},{8,24},{12,4},{16,0},{20,28},{24,8},{28,20},{1,17},{... | collective-permute-start | bytes 491528 | tf_op jit(solution)/shard_map/ppermute | solution.py:354
  35.4 5.8 %collective-permute-start.8 = (bf16[320,256]{1,0:T(8,128)(2,1)S(1)}, bf16[320,256]{1,0:T(8,128)(2,1)S(1)}, u32[]{:S(2)}, u32[]{:S(2)}) collective-permute-start(bf16[320,256]{1,0:T(8,128)(2,1)S(1)} %collective-permute-done.7.refs_1_), channel_id=1, source_target_pairs={{0,16},{4,12},{8,24},{12,4},{16,0},{20,28},{24,8},{28,20},{1,17},{... | collective-permute-start | bytes 491528 | tf_op jit(solution)/shard_map/ppermute | solution.py:354
  41.2 1.7 %collective-permute-start.11 = (bf16[640,256]{1,0:T(8,128)(2,1)S(1)}, bf16[640,256]{1,0:T(8,128)(2,1)S(1)}, u32[]{:S(2)}, u32[]{:S(2)}) collective-permute-start(bf16[640,256]{1,0:T(8,128)(2,1)S(1)} %pad_maximum_fusion.3), channel_id=1, source_target_pairs={{0,4},{4,0},{8,12},{12,8},{16,20},{20,16},{24,28},{28,24},{1,5},{5... | collective-permute-start | bytes 983048 | tf_op jit(solution)/shard_map/ppermute | solution.py:336
  42.9 2.6 %collective-permute-start.12 = (bf16[4,480,256]{2,1,0:T(8,128)(2,1)S(1)}, bf16[4,480,256]{2,1,0:T(8,128)(2,1)S(1)}, u32[]{:S(2)}, u32[]{:S(2)}) collective-permute-start(bf16[4,480,256]{2,1,0:T(8,128)(2,1)S(1)} %get-tuple-element.167), channel_id=1, source_target_pairs={{0,4},{4,0},{8,12},{12,8},{16,20},{20,16},{24,28},{28,24},{1,5},{5... | collective-permute-start | bytes 2949128 | tf_op jit(solution)/shard_map/ppermute | solution.py:336
  45.5 1.6 %collective-permute-start.13 = (bf16[4,160,256]{2,1,0:T(8,128)(2,1)S(1)}, bf16[4,160,256]{2,1,0:T(8,128)(2,1)S(1)}, u32[]{:S(2)}, u32[]{:S(2)}) collective-permute-start(bf16[4,160,256]{2,1,0:T(8,128)(2,1)S(1)} %get-tuple-element.184), channel_id=1, source_target_pairs={{0,4},{4,0},{8,12},{12,8},{16,20},{20,16},{24,28},{28,24},{1,5},{5... | collective-permute-start | bytes 983048 | tf_op jit(solution)/shard_map/ppermute | solution.py:336
  47.2 7.1 %collective-permute-start.14 = (bf16[640,256]{1,0:T(8,128)(2,1)S(1)}, bf16[640,256]{1,0:T(8,128)(2,1)S(1)}, u32[]{:S(2)}, u32[]{:S(2)}) collective-permute-start(bf16[640,256]{1,0:T(8,128)(2,1)S(1)} %pad_maximum_fusion.4), channel_id=1, source_target_pairs={{0,16},{4,12},{8,24},{12,4},{16,0},{20,28},{24,8},{28,20},{1,17},{... | collective-permute-start | bytes 983048 | tf_op jit(solution)/shard_map/ppermute | solution.py:354
  48.6 10.7 %collective-permute-start.16 = (bf16[640,256]{1,0:T(8,128)(2,1)S(1)}, bf16[640,256]{1,0:T(8,128)(2,1)S(1)}, u32[]{:S(2)}, u32[]{:S(2)}) collective-permute-start(bf16[640,256]{1,0:T(8,128)(2,1)S(1)} %pad_maximum_fusion.5), channel_id=1, source_target_pairs={{0,16},{4,12},{8,24},{12,4},{16,0},{20,28},{24,8},{28,20},{1,17},{... | collective-permute-start | bytes 983048 | tf_op jit(solution)/shard_map/ppermute | solution.py:354
  54.5 7.1 %collective-permute-start.15 = (bf16[640,256]{1,0:T(8,128)(2,1)S(1)}, bf16[640,256]{1,0:T(8,128)(2,1)S(1)}, u32[]{:S(2)}, u32[]{:S(2)}) collective-permute-start(bf16[640,256]{1,0:T(8,128)(2,1)S(1)} %add_convert_fusion.1), channel_id=1, source_target_pairs={{0,8},{4,20},{8,0},{12,28},{16,24},{20,4},{24,16},{28,12},{1,9},{5... | collective-permute-start | bytes 983048 | tf_op jit(solution)/shard_map/ppermute | solution.py:350
  61.8 7.3 %collective-permute-start.17 = (bf16[160,256]{1,0:T(8,128)(2,1)S(1)}, bf16[160,256]{1,0:T(8,128)(2,1)S(1)}, u32[]{:S(2)}, u32[]{:S(2)}) collective-permute-start(bf16[160,256]{1,0:T(8,128)(2,1)S(1)} %get-tuple-element.214), channel_id=1, source_target_pairs={{0,1},{1,0},{2,3},{3,2},{4,5},{5,4},{6,7},{7,6},{8,9},{9,8},{10,11... | collective-permute-start | bytes 245768 | tf_op jit(solution)/shard_map/ppermute | solution.py:336
  62.0 9.6 %collective-permute-start.18 = (bf16[160,256]{1,0:T(8,128)(2,1)S(1)}, bf16[160,256]{1,0:T(8,128)(2,1)S(1)}, u32[]{:S(2)}, u32[]{:S(2)}) collective-permute-start(bf16[160,256]{1,0:T(8,128)(2,1)S(1)} %get-tuple-element.213), channel_id=1, source_target_pairs={{0,2},{1,3},{2,0},{3,1},{4,6},{5,7},{6,4},{7,5},{8,10},{9,11},{10,... | collective-permute-start | bytes 245768 | tf_op jit(solution)/shard_map/ppermute | solution.py:336
  64.3 7.3 %collective-permute-start.19 = (bf16[160,256]{1,0:T(8,128)(2,1)S(1)}, bf16[160,256]{1,0:T(8,128)(2,1)S(1)}, u32[]{:S(2)}, u32[]{:S(2)}) collective-permute-start(bf16[160,256]{1,0:T(8,128)(2,1)S(1)} %get-tuple-element.212), channel_id=1, source_target_pairs={{0,3},{1,2},{2,1},{3,0},{4,7},{5,6},{6,5},{7,4},{8,11},{9,10},{10,... | collective-permute-start | bytes 245768 | tf_op jit(solution)/shard_map/ppermute | solution.py:336
  71.9 6.2 %collective-permute-start.20 = (bf16[256,256]{1,0:T(8,128)(2,1)S(1)}, bf16[256,256]{1,0:T(8,128)(2,1)S(1)}, u32[]{:S(2)}, u32[]{:S(2)}) collective-permute-start(bf16[256,256]{1,0:T(8,128)(2,1)S(1)} %shard_map.110.refs_0_), channel_id=1, source_target_pairs={{0,8},{4,20},{8,0},{12,28},{16,24},{20,4},{24,16},{28,12},{1,9},{5... | collective-permute-start | bytes 393224 | tf_op jit(solution)/shard_map/ppermute | solution.py:350
  73.2 5.8 %collective-permute-start.21 = (bf16[256,256]{1,0:T(8,128)(2,1)S(1)}, bf16[256,256]{1,0:T(8,128)(2,1)S(1)}, u32[]{:S(2)}, u32[]{:S(2)}) collective-permute-start(bf16[256,256]{1,0:T(8,128)(2,1)S(1)} %shard_map.110.refs_0_), channel_id=1, source_target_pairs={{0,16},{4,12},{8,24},{12,4},{16,0},{20,28},{24,8},{28,20},{1,17},{... | collective-permute-start | bytes 393224 | tf_op jit(solution)/shard_map/ppermute | solution.py:354
  74.9 5.9 %collective-permute-start.22 = (bf16[256,256]{1,0:T(8,128)(2,1)S(1)}, bf16[256,256]{1,0:T(8,128)(2,1)S(1)}, u32[]{:S(2)}, u32[]{:S(2)}) collective-permute-start(bf16[256,256]{1,0:T(8,128)(2,1)S(1)} %shard_map.110.refs_0_), channel_id=1, source_target_pairs={{0,24},{4,28},{8,16},{12,20},{16,8},{20,12},{24,0},{28,4},{1,25},{... | collective-permute-start | bytes 393224 | tf_op jit(solution)/shard_map/ppermute | solution.py:336
  80.8 2.0 %collective-permute-start.23 = (bf16[1024,256]{1,0:T(8,128)(2,1)S(1)}, bf16[1024,256]{1,0:T(8,128)(2,1)S(1)}, u32[]{:S(2)}, u32[]{:S(2)}) collective-permute-start(bf16[1024,256]{1,0:T(8,128)(2,1)S(1)} %pad_maximum_fusion), channel_id=1, source_target_pairs={{0,4},{4,0},{8,12},{12,8},{16,20},{20,16},{24,28},{28,24},{1,5},{5... | collective-permute-start | bytes 1572872 | tf_op jit(solution)/shard_map/ppermute | solution.py:336

commit v5 on v4

--- a/solution.py
+++ b/solution.py
@@ -135,31 +135,32 @@
         (tok.at[:, piece], tok_part),
         (grad.at[:, piece], grad_part),
     )
-    ids_copy.wait()
     count = tok.shape[0]
     places = assign.shape[0]
-    relative = jnp.bitwise_xor(ids[...], here)
-    expert = lax.broadcasted_iota(jnp.int32, (8, count), 0)
-    hit = (relative == expert).astype(F32)
     row = lax.broadcasted_iota(jnp.int32, (count, count), 0)
     col = lax.broadcasted_iota(jnp.int32, (count, count), 1)
     earlier = (row < col).astype(F32).astype(BF16)
+    expert = lax.broadcasted_iota(jnp.int32, (8, count), 0)
+    spots = lax.broadcasted_iota(jnp.int32, (places, count), 0)
+    ids_copy.wait()
+    relative = jnp.bitwise_xor(ids[...], here)
+    hit = (relative == expert).astype(F32)
     before = jnp.dot(hit.astype(BF16), earlier, preferred_element_type=F32)
     slot = jnp.sum(before * hit, axis=0, keepdims=True).astype(jnp.int32)
     target = relative * capacity + slot
-    spots = lax.broadcasted_iota(jnp.int32, (places, count), 0)
-    assign[...] = (target == spots).astype(F32).astype(BF16)
+    chosen = (target == spots).astype(F32).astype(BF16)
+    assign[...] = chosen
     prob_copy.wait()
     weight = column(prob[...])
     tok_copy.wait()
-    for k, ref in ((1, send1), (3, send3), (2, send2)):
-        pick = assign[k * capacity : (k + 1) * capacity]
-        ref[:capacity] = jnp.dot(pick, tok_part[...], preferred_element_type=F32).astype(BF16)
     grad_copy.wait()
     y_part = (weight * grad_part[...].astype(F32)).astype(BF16)
+    both = jnp.concatenate([tok_part[...], y_part], axis=1)
     for k, ref in ((1, send1), (3, send3), (2, send2)):
-        pick = assign[k * capacity : (k + 1) * capacity]
-        ref[capacity:] = jnp.dot(pick, y_part, preferred_element_type=F32).astype(BF16)
+        pick = chosen[k * capacity : (k + 1) * capacity]
+        rows = jnp.dot(pick, both, preferred_element_type=F32).astype(BF16)
+        ref[:capacity] = rows[:, :share]
+        ref[capacity:] = rows[:, share:]
 
 
 def block_order():
@@ -212,8 +213,8 @@
 
 
 def early_kernel(share, *refs):
-    blocks = list(refs[:4]) + parts_of(refs[4], 2)
-    weights, outs = refs[5:8], refs[8:]
+    blocks = parts_of(refs[0], 2) + parts_of(refs[1], 2) + parts_of(refs[2], 2)
+    weights, outs = refs[3:6], refs[6:]
     block = lax.axis_index("dp")
     mine, across = block_order()
     parts = []
@@ -225,9 +226,9 @@
 
 
 def late_kernel(share, rows, *refs):
-    blocks = list(refs[:4]) + parts_of(refs[4], 2) + parts_of(refs[5], 2)
-    early, weights = refs[6:9], refs[9:12]
-    x_all, y_all, hidden, gate_grad, up_grad, odd = refs[17:]
+    blocks = [part for ref in refs[:4] for part in parts_of(ref, 2)]
+    early, weights = refs[4:7], refs[7:10]
+    x_all, y_all, hidden, gate_grad, up_grad, odd = refs[15:]
     block = lax.axis_index("dp")
     mine, across = block_order()
     parts = []
@@ -317,12 +318,11 @@
     out[...] = lax.dot_general(assign[...], rows[...], FIRST, preferred_element_type=F32).astype(BF16)
 
 
-def place_kernel(share, *refs):
+def place_kernel(share, side, count, *refs):
     out, sems = refs[-2:]
     block = lax.axis_index("dp")
-    mine, across = block_order()
-    pieces = [cols(jnp.bitwise_xor(block, k), share) for k in mine + across]
-    blocks = list(refs[:4]) + parts_of(refs[4], 4)
+    pieces = [cols(jnp.bitwise_xor(block, k), share) for k in block_order()[side]]
+    blocks = refs[:4] if count == 4 else parts_of(refs[0], 4)
     for copy in start_copies(sems, *[(b, out.at[:, p]) for b, p in zip(blocks, pieces)]):
         copy.wait()
 
@@ -416,12 +416,12 @@
     first_a, block_b = fence(first_a, block_b)
     third_a = swap_second(first_a)
     first_b = swap_first(block_b)
-    second_b = swap_second(block_b)
     second_a, third_a, first_b = fence(second_a, third_a, first_b)
 
     across_a = swap(jnp.concatenate([block_a, first_a, second_a, third_a]), "dp", 1)
-    third_b = swap_second(first_b)
-    early_b = swap(jnp.concatenate([block_b, first_b]), "dp", 1)
+    pair_b = jnp.concatenate([block_b, first_b])
+    both_b = swap_second(pair_b)
+    early_b = swap(pair_b, "dp", 1)
     out_a = call(
         functools.partial(chunk_kernel, share, chunk_a, chunk_a, 1, 7),
         shared + terms_a,
@@ -430,29 +430,29 @@
         16,
         aliases={8 + j: j for j in range(7)},
     )
-    second_b, third_b, early_b, *out_a = fence(second_b, third_b, early_b, *out_a)
+    both_b, early_b, *out_a = fence(both_b, early_b, *out_a)
 
     partial = call(
         functools.partial(early_kernel, share),
         [shape(capacity, hidden_part, dtype=F32)] * 3,
-        (block_b, first_b, second_b, third_b, early_b) + weights,
+        (pair_b, both_b, early_b) + weights,
         SMALL,
         16,
     )
-    later_b = swap(jnp.concatenate([second_b, third_b]), "dp", 1)
+    later_b = swap(both_b, "dp", 1)
     later_b, *out_a = fence(later_b, *out_a, *partial)
     out_a, partial = out_a[:7], tuple(out_a[7:])
     other_a = swap(out_a[6], "dp", 1)
     out_b = call(
         functools.partial(late_kernel, share, chunk_b),
         shared + terms_b[:1],
-        (block_b, first_b, second_b, third_b, early_b, later_b)
+        (pair_b, both_b, early_b, later_b)
         + partial
         + weights
         + tuple(out_a[:5]),
         SMALL,
         16,
-        aliases={12 + j: j for j in range(5)},
+        aliases={10 + j: j for j in range(5)},
     )
     other_a, *out_b = fence(other_a, *out_b)
     x_all, y_all, hidden, gate_grad, up_grad, odd_b = out_b
@@ -488,14 +488,19 @@
     relay = swap_second(pairs[3])
     late = swap_second(pairs[2])
     (relay,) = fence(relay)
-    last = swap_first(total_of([pairs[1], relay]))
+    half = 2 * capacity
+    step = total_of([pairs[1], relay])
+    last_a = swap_first(step[:half])
+    last_b = swap_first(step[half:])
     up_wgrad = wgrad(x_all, up_grad)
-    last, late, up_wgrad, x_all = fence(last, late, up_wgrad, x_all)
-    summed = total_of([pairs[0], last, late])
-    ret0 = summed[chunk_own]
-    ret3 = swap(summed[capacity : 2 * capacity], "expert", 3)
-    ret1 = swap(summed[:capacity], "expert", 1)
-    ret2 = swap(summed[chunk_b], "expert", 2)
+    last_a, late, up_wgrad, x_all = fence(last_a, late, up_wgrad, x_all)
+    summed_a = total_of([pairs[0][:half], last_a, late[:half]])
+    ret3 = swap(summed_a[capacity:], "expert", 3)
+    ret1 = swap(summed_a[:capacity], "expert", 1)
+    summed_a, last_b = fence(summed_a, last_b)
+    summed_b = total_of([pairs[0][half:], last_b, late[half:]])
+    ret0 = summed_b[:capacity]
+    ret2 = swap(summed_b[capacity:], "expert", 2)
     gate_wgrad = wgrad(x_all, gate_grad)
     ret1, ret2, ret3, gate_wgrad = fence(ret1, ret2, ret3, gate_wgrad)
     (token_cols,) = call(
@@ -512,15 +517,25 @@
     down_wgrad = wgrad(hidden, y_all)
     first, second, sixth, down_wgrad = fence(first, second, sixth, down_wgrad)
     across = swap(jnp.concatenate([token_cols, first, second, sixth]), "dp", 1)
-    (grad_tokens,) = call(
-        functools.partial(place_kernel, share),
+    (placed,) = call(
+        functools.partial(place_kernel, share, 0, 4),
         [shape(count, width)],
-        (token_cols, first, second, sixth, across),
+        (token_cols, first, second, sixth),
         SMALL,
         8,
-        [pltpu.SemaphoreType.DMA((8,))],
+        [pltpu.SemaphoreType.DMA((4,))],
         out_space=HBM,
     )
+    across, placed = fence(across, placed)
+    (grad_tokens,) = pl.pallas_call(
+        functools.partial(place_kernel, share, 1, 1),
+        out_shape=[shape(count, width)],
+        in_specs=[pl.BlockSpec(memory_space=VMEM), pl.BlockSpec(memory_space=HBM)],
+        out_specs=[pl.BlockSpec(memory_space=HBM)],
+        scratch_shapes=[pltpu.SemaphoreType.DMA((4,))],
+        input_output_aliases={1: 0},
+        compiler_params=pltpu.CompilerParams(vmem_limit_bytes=8 << 20),
+    )(across, pltpu.with_memory_space_constraint(placed, HBM))
     return (grad_tokens, gate_wgrad[None], up_wgrad[None], down_wgrad[None])
 
 

time: 84.2 us -> 83 us (0.986)
  waiting for transfers between devices: 29.5 us -> 28.1 us
    ppermute x7 -> x6, waiting for transfers between devices: 8.15 us -> 5.64 us  [swap_second(): lax.ppermute(array, 'dp', [(i, i ^ (2 if i % 2 else 4)) for i in range(8)])]
    ppermute x4 -> x5, waiting for transfers between devices: 6.64 us -> 8.52 us  [swap_first(): lax.ppermute(array, 'dp', [(i, i ^ (4 if i % 2 else 2)) for i in range(8)])]
    ppermute x7 -> x6, starting transfers between devices: 9.4 us -> 7.74 us  [swap_second(): lax.ppermute(array, 'dp', [(i, i ^ (2 if i % 2 else 4)) for i in range(8)])]
    ppermute x4 -> x5, starting transfers between devices: 5.44 us -> 6.46 us  [swap_first(): lax.ppermute(array, 'dp', [(i, i ^ (4 if i % 2 else 2)) for i in range(8)])]
  transfers between devices with their start and end apart: 24 -> 24, of which waited for: 17 -> 17; matrix products, arithmetic and copies ran while one was open for 0% -> 1% of each run, Pallas kernels for 26% -> 27%
where the time goes in v5:
time: 83 us; the launch traced here: 82.8 us
  waiting for transfers between devices  28.1 us (34%)
  starting transfers between devices  28 us (34%)
  Pallas kernels  24.9 us (30%)
  between operations  1.05 us (1%)
    pallas_call x11, Pallas kernels, call(): pl.pallas_call(body, out_shape=outs, in_specs=[pl.BlockSpec(memory_space=...  24 us
    ppermute x13, waiting for transfers between devices, swap(): return lax.ppermute(array, axis, [(i, i ^ distance) for i in range(size)])  13.9 us
    ppermute x13, starting transfers between devices, swap(): return lax.ppermute(array, axis, [(i, i ^ distance) for i in range(size)])  13.8 us
    ppermute x5, waiting for transfers between devices, swap_first(): lax.ppermute(array, 'dp', [(i, i ^ (4 if i % 2 else 2)) for i in range(8)])  8.52 us
    ppermute x6, starting transfers between devices, swap_second(): lax.ppermute(array, 'dp', [(i, i ^ (2 if i % 2 else 4)) for i in range(8)])  7.74 us
    ppermute x5, starting transfers between devices, swap_first(): lax.ppermute(array, 'dp', [(i, i ^ (4 if i % 2 else 2)) for i in range(8)])  6.46 us
    ppermute x6, waiting for transfers between devices, swap_second(): lax.ppermute(array, 'dp', [(i, i ^ (2 if i % 2 else 4)) for i in range(8)])  5.64 us
  transfers between devices with their start and end apart: 24, of which 17 were waited for; matrix products, arithmetic and copies ran while one was open for 1% of the time, Pallas kernels for 27%

profile of v5, /device:TPU:0, one launch (start us, length us, event | category | flops | bytes accessed | tf_op | source)
XLA Modules:
  0.0 82.8 jit_solution(14334627051152138070)
XLA Ops:
  0.6 1.4 %shard_map.102 = (bf16[320,256]{1,0:T(8,128)(2,1)S(1)}, bf16[320,256]{1,0:T(8,128)(2,1)S(1)}, bf16[320,256]{1,0:T(8,128)(2,1)S(1)}, bf16[640,256]{1,0:T(8,128)(2,1)S(1)}) custom-call(s32[1,256]{1,0:T(1,128)} %bitcast.37, f32[1,256]{1,0:T(1,128)} %bitcast.35, bf16[256,2048]{1,0:T(8,128)(2,1)} %tok_far.1, bf16[256,2048]{1,0:T(8,128)(2,1)} %grad_far.1), custom_call_target="tpu_custom_call" | custom-call | flops 1000 | bytes 2918400 | tf_op jit(solution)/shard_map/pallas_call | solution.py:93
  2.1 3.1 %collective-permute-start = (bf16[320,256]{1,0:T(8,128)(2,1)S(1)}, bf16[320,256]{1,0:T(8,128)(2,1)S(1)}, u32[]{:S(2)}, u32[]{:S(2)}) collective-permute-start(bf16[320,256]{1,0:T(8,128)(2,1)S(1)} %get-tuple-element.107), channel_id=1, source_target_pairs={{0,1},{1,0},{2,3},{3,2},{4,5},{5,4},{6,7},{7,6},{8,9},{9,8},{10,11... | collective-permute-start | bytes 491528 | tf_op jit(solution)/shard_map/ppermute | solution.py:336
  5.2 2.5 %collective-permute-start.1 = (bf16[320,256]{1,0:T(8,128)(2,1)S(1)}, bf16[320,256]{1,0:T(8,128)(2,1)S(1)}, u32[]{:S(2)}, u32[]{:S(2)}) collective-permute-start(bf16[320,256]{1,0:T(8,128)(2,1)S(1)} %get-tuple-element.108), channel_id=1, source_target_pairs={{0,3},{1,2},{2,1},{3,0},{4,7},{5,6},{6,5},{7,4},{8,11},{9,10},{10,... | collective-permute-start | bytes 491528 | tf_op jit(solution)/shard_map/ppermute | solution.py:336
  7.7 5.8 %shard_map.103 = (bf16[640,2048]{1,0:T(8,128)(2,1)S(1)}, bf16[640,2048]{1,0:T(8,128)(2,1)S(1)}, bf16[640,512]{1,0:T(8,128)(2,1)S(1)}, bf16[640,512]{1,0:T(8,128)...) custom-call(f32[1,256]{1,0:T(1,128)} %bitcast.36, ...), custom_call_target="tpu_custom_call" | custom-call | flops 1000 | bytes 24183808 | tf_op jit(solution)/shard_map/pallas_call | solution.py:93
  13.5 1.7 %collective-permute-done.1 = bf16[320,256]{1,0:T(8,128)(2,1)S(1)} collective-permute-done((bf16[320,256]{1,0:T(8,128)(2,1)S(1)}, bf16[320,256]{1,0:T(8,128)(2,1)S(1)}, u32[]{:S(2)}, u32[]{:S(2)}) %collective-permute-start.1) | collective-permute-done | bytes 163872 | tf_op jit(solution)/shard_map/ppermute | solution.py:336
  15.3 1.6 %collective-permute-start.2 = (bf16[640,256]{1,0:T(8,128)(2,1)S(1)}, bf16[640,256]{1,0:T(8,128)(2,1)S(1)}, u32[]{:S(2)}, u32[]{:S(2)}) collective-permute-start(bf16[640,256]{1,0:T(8,128)(2,1)S(1)} %pad_maximum_fusion.1.refs_0_), channel_id=1, source_target_pairs={{0,8},{4,20},{8,0},{12,28},{16,24},{20,4},{24,16},{28,12},{1,9},{5... | collective-permute-start | bytes 983048 | tf_op jit(solution)/shard_map/ppermute | solution.py:350
  16.8 1.8 %collective-permute-start.3 = (bf16[320,256]{1,0:T(8,128)(2,1)S(1)}, bf16[320,256]{1,0:T(8,128)(2,1)S(1)}, u32[]{:S(2)}, u32[]{:S(2)}) collective-permute-start(bf16[320,256]{1,0:T(8,128)(2,1)S(1)} %get-tuple-element.132), channel_id=1, source_target_pairs={{0,2},{1,3},{2,0},{3,1},{4,6},{5,7},{6,4},{7,5},{8,10},{9,11},{10,... | collective-permute-start | bytes 491528 | tf_op jit(solution)/shard_map/ppermute | solution.py:336
  18.6 1.5 %collective-permute-start.4 = (bf16[640,256]{1,0:T(8,128)(2,1)S(1)}, bf16[640,256]{1,0:T(8,128)(2,1)S(1)}, u32[]{:S(2)}, u32[]{:S(2)}) collective-permute-start(bf16[640,256]{1,0:T(8,128)(2,1)S(1)} %pad_maximum_fusion.1.refs_0_), channel_id=1, source_target_pairs={{0,16},{4,12},{8,24},{12,4},{16,0},{20,28},{24,8},{28,20},{1,17},{... | collective-permute-start | bytes 983048 | tf_op jit(solution)/shard_map/ppermute | solution.py:354
  20.1 4.7 %collective-permute-done.3 = bf16[320,256]{1,0:T(8,128)(2,1)S(1)} collective-permute-done((bf16[320,256]{1,0:T(8,128)(2,1)S(1)}, bf16[320,256]{1,0:T(8,128)(2,1)S(1)}, u32[]{:S(2)}, u32[]{:S(2)}) %collective-permute-start.3) | collective-permute-done | bytes 163872 | tf_op jit(solution)/shard_map/ppermute | solution.py:336
  24.8 0.5 collective-permute-done.2.refs_1_
  25.4 2.0 %collective-permute-start.5 = (bf16[640,256]{1,0:T(8,128)(2,1)S(1)}, bf16[640,256]{1,0:T(8,128)(2,1)S(1)}, u32[]{:S(2)}, u32[]{:S(2)}) collective-permute-start(bf16[640,256]{1,0:T(8,128)(2,1)S(1)} %collective-permute-done.2.refs_1_), channel_id=1, source_target_pairs={{0,16},{4,12},{8,24},{12,4},{16,0},{20,28},{24,8},{28,20},{1,17},{... | collective-permute-start | bytes 983048 | tf_op jit(solution)/shard_map/ppermute | solution.py:354
  27.4 1.5 %collective-permute-start.6 = (bf16[320,256]{1,0:T(8,128)(2,1)S(1)}, bf16[320,256]{1,0:T(8,128)(2,1)S(1)}, u32[]{:S(2)}, u32[]{:S(2)}) collective-permute-start(bf16[320,256]{1,0:T(8,128)(2,1)S(1)} %collective-permute-done.3), channel_id=1, source_target_pairs={{0,8},{4,20},{8,0},{12,28},{16,24},{20,4},{24,16},{28,12},{1,9},{5... | collective-permute-start | bytes 491528 | tf_op jit(solution)/shard_map/ppermute | solution.py:350
  28.9 3.8 %collective-permute-done.6 = bf16[320,256]{1,0:T(8,128)(2,1)S(1)} collective-permute-done((bf16[320,256]{1,0:T(8,128)(2,1)S(1)}, bf16[320,256]{1,0:T(8,128)(2,1)S(1)}, u32[]{:S(2)}, u32[]{:S(2)}) %collective-permute-start.6) | collective-permute-done | bytes 163872 | tf_op jit(solution)/shard_map/ppermute | solution.py:350
  32.7 0.5 collective-permute-done.5.refs_3_
  33.4 1.3 %collective-permute-start.7 = (bf16[640,256]{1,0:T(8,128)(2,1)S(1)}, bf16[640,256]{1,0:T(8,128)(2,1)S(1)}, u32[]{:S(2)}, u32[]{:S(2)}) collective-permute-start(bf16[640,256]{1,0:T(8,128)(2,1)S(1)} %constant_dynamic-update-slice_fusion.refs_0_), channel_id=1, source_target_pairs={{0,16},{4,12},{8,24},{12,4},{16,0},{20,28},{24,8},{28,20},{1,17},{... | collective-permute-start | bytes 983048 | tf_op jit(solution)/shard_map/ppermute | solution.py:354
  34.7 1.7 %collective-permute-done.9.refs_4_ = bf16[2560,256]{1,0:T(8,128)(2,1)S(1)} collective-permute-done((bf16[2560,256]{1,0:T(8,128)(2,1)S(1)}, bf16[2560,256]{1,0:T(8,128)(2,1)S(1)}, u32[]{:S(2)}, u32[]{:S(2)}) %collective-permute-start.9) | collective-permute-done | bytes 1310752 | tf_op jit(solution)/shard_map/ppermute | solution.py:336
  36.4 4.0 %shard_map.104 = (bf16[640,2048]{1,0:T(8,128)(2,1)S(1)}, bf16[640,2048]{1,0:T(8,128)(2,1)S(1)}, bf16[640,512]{1,0:T(8,128)(2,1)S(1)}, bf16[640,512]{1,0:T(8,128)...) custom-call(bf16[640,256]{1,0:T(8,128)(2,1)S(1)} %pad_maximum_fusion, ...), custom_call_target="tpu_custom_call", output_to_operand_aliasing={{0}: (8, {}), {1}: (9, {}), {2}: (10, {}), {3}: (11, {}), {... | custom-call | flops 1000 | bytes 27262976 | tf_op jit(solution)/shard_map/pallas_call | solution.py:93
  40.3 0.2 collective-permute-done.7.refs_1_
  40.6 1.2 %shard_map.105 = (f32[160,512]{1,0:T(8,128)S(1)}, f32[160,512]{1,0:T(8,128)S(1)}, f32[160,512]{1,0:T(8,128)S(1)}) custom-call(bf16[640,256]{1,0:T(8,128)(2,1)S(1)} %constant_dynamic-update-slice_fusion.refs_0_, bf16[640,256]{1,0:T(8,128)(2,1)S(1)} %collective-permute-done.7.refs_1_, bf16[640,256]{1,0:T(8,128)(2,1)S(1)} %collective-permute-done.8.refs_2_, ...), custom_call_target="tpu_custom_call" | custom-call | flops 1000 | bytes 8257536 | tf_op jit(solution)/shard_map/pallas_call | solution.py:93
  41.8 0.4 collective-permute-done.10.refs_3_
  42.1 0.1 collective-permute-start.11
  42.3 1.5 %shard_map.106 = (bf16[640,2048]{1,0:T(8,128)(2,1)S(1)}, bf16[640,2048]{1,0:T(8,128)(2,1)S(1)}, bf16[640,512]{1,0:T(8,128)(2,1)S(1)}, bf16[640,512]{1,0:T(8,128)...) custom-call(bf16[640,256]{1,0:T(8,128)(2,1)S(1)} %constant_dynamic-u, ...), custom_call_target="tpu_custom_call", output_to_operand_aliasing={{0}: (10, {}), {1}: (11, {}), {2}: (12, {}), {3}: (13, {}),... | custom-call | flops 1000 | bytes 23330816 | tf_op jit(solution)/shard_map/pallas_call | solution.py:93
  43.7 1.0 %collective-permute-done.11 = bf16[4,480,256]{2,1,0:T(8,128)(2,1)S(1)} collective-permute-done((bf16[4,480,256]{2,1,0:T(8,128)(2,1)S(1)}, bf16[4,480,256]{2,1,0:T(8,128)(2,1)S(1)}, u32[]{:S(2)}, u32[]{:S(2)}) %collective-permute-start.11) | collective-permute-done | bytes 983072 | tf_op jit(solution)/shard_map/ppermute | solution.py:336
  44.9 0.8 %shard_map.107 = bf16[4,160,256]{2,1,0:T(8,128)(2,1)S(1)} custom-call(bf16[640,512]{1,0:T(8,128)(2,1)S(1)} %get-tuple-element.186.gate_grad.right, bf16[640,512]{1,0:T(8,128)(2,1)S(1)} %get-tuple-element.187.up_grad.right, bf16[2048,512]{1,0:T(8,128)(2,1)S(1)} %get-tuple-element.138.refs_5_.refs_3_.refs_7_.w_gate, ...), custom_call_target="tpu_custom_call" | custom-call | flops 1000 | bytes 5832704 | tf_op jit(solution)/shard_map/pallas_call | solution.py:93
  45.7 0.2 add_convert_fusion.4
  45.9 0.4 collective-permute-done.12
  46.5 1.3 %collective-permute-start.13 = (bf16[640,256]{1,0:T(8,128)(2,1)S(1)}, bf16[640,256]{1,0:T(8,128)(2,1)S(1)}, u32[]{:S(2)}, u32[]{:S(2)}) collective-permute-start(bf16[640,256]{1,0:T(8,128)(2,1)S(1)} %pad_maximum_fusion.2), channel_id=1, source_target_pairs={{0,16},{4,12},{8,24},{12,4},{16,0},{20,28},{24,8},{28,20},{1,17},{... | collective-permute-start | bytes 983048 | tf_op jit(solution)/shard_map/ppermute | solution.py:354
  47.8 0.8 %collective-permute-start.15 = (bf16[640,256]{1,0:T(8,128)(2,1)S(1)}, bf16[640,256]{1,0:T(8,128)(2,1)S(1)}, u32[]{:S(2)}, u32[]{:S(2)}) collective-permute-start(bf16[640,256]{1,0:T(8,128)(2,1)S(1)} %pad_maximum_fusion.3), channel_id=1, source_target_pairs={{0,16},{4,12},{8,24},{12,4},{16,0},{20,28},{24,8},{28,20},{1,17},{... | collective-permute-start | bytes 983048 | tf_op jit(solution)/shard_map/ppermute | solution.py:354
  48.6 5.0 %collective-permute-done.13 = bf16[640,256]{1,0:T(8,128)(2,1)S(1)} collective-permute-done((bf16[640,256]{1,0:T(8,128)(2,1)S(1)}, bf16[640,256]{1,0:T(8,128)(2,1)S(1)}, u32[]{:S(2)}, u32[]{:S(2)}) %collective-permute-start.13) | collective-permute-done | bytes 327712 | tf_op jit(solution)/shard_map/ppermute | solution.py:354
  53.7 1.1 %collective-permute-start.14 = (bf16[320,256]{1,0:T(8,128)(2,1)S(1)}, bf16[320,256]{1,0:T(8,128)(2,1)S(1)}, u32[]{:S(2)}, u32[]{:S(2)}) collective-permute-start(bf16[320,256]{1,0:T(8,128)(2,1)S(1)} %get-tuple-element.217), channel_id=1, source_target_pairs={{0,8},{4,20},{8,0},{12,28},{16,24},{20,4},{24,16},{28,12},{1,9},{5... | collective-permute-start | bytes 491528 | tf_op jit(solution)/shard_map/ppermute | solution.py:350
  54.8 2.7 %shard_map.108 = bf16[2048,512]{1,0:T(8,128)(2,1)} custom-call(bf16[640,2048]{1,0:T(8,128)(2,1)S(1)} %get-tuple-element.194.left, bf16[640,512]{1,0:T(8,128)(2,1)S(1)} %get-tuple-element.187.up_grad.right), custom_call_target="tpu_custom_call" | custom-call | flops 1000 | bytes 5373952 | tf_op jit(solution)/shard_map/pallas_call | solution.py:93
  57.4 1.1 %collective-permute-start.16 = (bf16[320,256]{1,0:T(8,128)(2,1)S(1)}, bf16[320,256]{1,0:T(8,128)(2,1)S(1)}, u32[]{:S(2)}, u32[]{:S(2)}) collective-permute-start(bf16[320,256]{1,0:T(8,128)(2,1)S(1)} %get-tuple-element.216), channel_id=1, source_target_pairs={{0,8},{4,20},{8,0},{12,28},{16,24},{20,4},{24,16},{28,12},{1,9},{5... | collective-permute-start | bytes 491528 | tf_op jit(solution)/shard_map/ppermute | solution.py:350
  58.5 0.6 collective-permute-done.14
  59.2 3.6 %collective-permute-done.16 = bf16[320,256]{1,0:T(8,128)(2,1)S(1)} collective-permute-done((bf16[320,256]{1,0:T(8,128)(2,1)S(1)}, bf16[320,256]{1,0:T(8,128)(2,1)S(1)}, u32[]{:S(2)}, u32[]{:S(2)}) %collective-permute-start.16) | collective-permute-done | bytes 163872 | tf_op jit(solution)/shard_map/ppermute | solution.py:350
  62.9 2.1 %collective-permute-start.18 = (bf16[160,256]{1,0:T(8,128)(2,1)S(1)}, bf16[160,256]{1,0:T(8,128)(2,1)S(1)}, u32[]{:S(2)}, u32[]{:S(2)}) collective-permute-start(bf16[160,256]{1,0:T(8,128)(2,1)S(1)} %get-tuple-element.220), channel_id=1, source_target_pairs={{0,2},{1,3},{2,0},{3,1},{4,6},{5,7},{6,4},{7,5},{8,10},{9,11},{10,... | collective-permute-start | bytes 245768 | tf_op jit(solution)/shard_map/ppermute | solution.py:336
  65.0 0.3 collective-permute-start.17
  65.3 2.1 %collective-permute-start.19 = (bf16[160,256]{1,0:T(8,128)(2,1)S(1)}, bf16[160,256]{1,0:T(8,128)(2,1)S(1)}, u32[]{:S(2)}, u32[]{:S(2)}) collective-permute-start(bf16[160,256]{1,0:T(8,128)(2,1)S(1)} %get-tuple-element.218), channel_id=1, source_target_pairs={{0,3},{1,2},{2,1},{3,0},{4,7},{5,6},{6,5},{7,4},{8,11},{9,10},{10,... | collective-permute-start | bytes 245768 | tf_op jit(solution)/shard_map/ppermute | solution.py:336
  67.4 2.8 %shard_map.109 = bf16[2048,512]{1,0:T(8,128)(2,1)} custom-call(bf16[640,2048]{1,0:T(8,128)(2,1)S(1)} %get-tuple-element.194.left, bf16[640,512]{1,0:T(8,128)(2,1)S(1)} %get-tuple-element.186.gate_grad.right), custom_call_target="tpu_custom_call" | custom-call | flops 1000 | bytes 5373952 | tf_op jit(solution)/shard_map/pallas_call | solution.py:93
  70.3 1.3 %collective-permute-done.19.r3 = bf16[160,256]{1,0:T(8,128)(2,1)S(1)} collective-permute-done((bf16[160,256]{1,0:T(8,128)(2,1)S(1)}, bf16[160,256]{1,0:T(8,128)(2,1)S(1)}, u32[]{:S(2)}, u32[]{:S(2)}) %collective-permute-start.19) | collective-permute-done | bytes 81952 | tf_op jit(solution)/shard_map/ppermute | solution.py:336
  71.6 0.3 shard_map.110.refs_0_
  71.9 1.3 %collective-permute-start.20 = (bf16[256,256]{1,0:T(8,128)(2,1)S(1)}, bf16[256,256]{1,0:T(8,128)(2,1)S(1)}, u32[]{:S(2)}, u32[]{:S(2)}) collective-permute-start(bf16[256,256]{1,0:T(8,128)(2,1)S(1)} %shard_map.110.refs_0_), channel_id=1, source_target_pairs={{0,8},{4,20},{8,0},{12,28},{16,24},{20,4},{24,16},{28,12},{1,9},{5... | collective-permute-start | bytes 393224 | tf_op jit(solution)/shard_map/ppermute | solution.py:350
  73.2 0.8 collective-permute-start.21
  74.0 1.5 %collective-permute-start.22 = (bf16[256,256]{1,0:T(8,128)(2,1)S(1)}, bf16[256,256]{1,0:T(8,128)(2,1)S(1)}, u32[]{:S(2)}, u32[]{:S(2)}) collective-permute-start(bf16[256,256]{1,0:T(8,128)(2,1)S(1)} %shard_map.110.refs_0_), channel_id=1, source_target_pairs={{0,24},{4,28},{8,16},{12,20},{16,8},{20,12},{24,0},{28,4},{1,25},{... | collective-permute-start | bytes 393224 | tf_op jit(solution)/shard_map/ppermute | solution.py:336
  75.5 2.7 %shard_map.111 = bf16[512,2048]{1,0:T(8,128)(2,1)} custom-call(bf16[640,512]{1,0:T(8,128)(2,1)S(1)} %get-tuple-element.198.left, bf16[640,2048]{1,0:T(8,128)(2,1)S(1)} %get-tuple-element.199.right), custom_call_target="tpu_custom_call" | custom-call | flops 1000 | bytes 5373952 | tf_op jit(solution)/shard_map/pallas_call | solution.py:93
  78.2 1.7 %collective-permute-done.22.refs_3_ = bf16[256,256]{1,0:T(8,128)(2,1)S(1)} collective-permute-done((bf16[256,256]{1,0:T(8,128)(2,1)S(1)}, bf16[256,256]{1,0:T(8,128)(2,1)S(1)}, u32[]{:S(2)}, u32[]{:S(2)}) %collective-permute-start.22) | collective-permute-done | bytes 131104 | tf_op jit(solution)/shard_map/ppermute | solution.py:336
  79.9 0.8 %shard_map.112.refs_1_ = bf16[256,2048]{1,0:T(8,128)(2,1)} custom-call(bf16[256,256]{1,0:T(8,128)(2,1)S(1)} %shard_map.110.refs_0_, bf16[256,256]{1,0:T(8,128)(2,1)S(1)} %collective-permute-done.20.refs_1_, bf16[256,256]{1,0:T(8,128)(2,1)S(1)} %collective-permute-done.21.refs_2_, bf16[256,256]{1,0:T(8,128)(2,1)S(1)} %collective-permute-done.22.refs_3_), custom_call_target="tpu_custom_call" | custom-call | flops 1000 | bytes 1572864 | tf_op jit(solution)/shard_map/pallas_call | solution.py:93
  80.8 1.1 %collective-permute-done.23.refs_0_ = bf16[1024,256]{1,0:T(8,128)(2,1)S(1)} collective-permute-done((bf16[1024,256]{1,0:T(8,128)(2,1)S(1)}, bf16[1024,256]{1,0:T(8,128)(2,1)S(1)}, u32[]{:S(2)}, u32[]{:S(2)}) %collective-permute-start.23) | collective-permute-done | bytes 524320 | tf_op jit(solution)/shard_map/ppermute | solution.py:336
  81.8 0.8 shard_map.113
  (33 shorter events, 1.0 us)
Async XLA Ops:
  2.1 11.4 %collective-permute-start = (bf16[320,256]{1,0:T(8,128)(2,1)S(1)}, bf16[320,256]{1,0:T(8,128)(2,1)S(1)}, u32[]{:S(2)}, u32[]{:S(2)}) collective-permute-start(bf16[320,256]{1,0:T(8,128)(2,1)S(1)} %get-tuple-element.107), channel_id=1, source_target_pairs={{0,1},{1,0},{2,3},{3,2},{4,5},{5,4},{6,7},{7,6},{8,9},{9,8},{10,11... | collective-permute-start | bytes 491528 | tf_op jit(solution)/shard_map/ppermute | solution.py:336
  5.2 10.0 %collective-permute-start.1 = (bf16[320,256]{1,0:T(8,128)(2,1)S(1)}, bf16[320,256]{1,0:T(8,128)(2,1)S(1)}, u32[]{:S(2)}, u32[]{:S(2)}) collective-permute-start(bf16[320,256]{1,0:T(8,128)(2,1)S(1)} %get-tuple-element.108), channel_id=1, source_target_pairs={{0,3},{1,2},{2,1},{3,0},{4,7},{5,6},{6,5},{7,4},{8,11},{9,10},{10,... | collective-permute-start | bytes 491528 | tf_op jit(solution)/shard_map/ppermute | solution.py:336
  15.3 10.1 %collective-permute-start.2 = (bf16[640,256]{1,0:T(8,128)(2,1)S(1)}, bf16[640,256]{1,0:T(8,128)(2,1)S(1)}, u32[]{:S(2)}, u32[]{:S(2)}) collective-permute-start(bf16[640,256]{1,0:T(8,128)(2,1)S(1)} %pad_maximum_fusion.1.refs_0_), channel_id=1, source_target_pairs={{0,8},{4,20},{8,0},{12,28},{16,24},{20,4},{24,16},{28,12},{1,9},{5... | collective-permute-start | bytes 983048 | tf_op jit(solution)/shard_map/ppermute | solution.py:350
  16.8 8.0 %collective-permute-start.3 = (bf16[320,256]{1,0:T(8,128)(2,1)S(1)}, bf16[320,256]{1,0:T(8,128)(2,1)S(1)}, u32[]{:S(2)}, u32[]{:S(2)}) collective-permute-start(bf16[320,256]{1,0:T(8,128)(2,1)S(1)} %get-tuple-element.132), channel_id=1, source_target_pairs={{0,2},{1,3},{2,0},{3,1},{4,6},{5,7},{6,4},{7,5},{8,10},{9,11},{10,... | collective-permute-start | bytes 491528 | tf_op jit(solution)/shard_map/ppermute | solution.py:336
  18.6 10.3 %collective-permute-start.4 = (bf16[640,256]{1,0:T(8,128)(2,1)S(1)}, bf16[640,256]{1,0:T(8,128)(2,1)S(1)}, u32[]{:S(2)}, u32[]{:S(2)}) collective-permute-start(bf16[640,256]{1,0:T(8,128)(2,1)S(1)} %pad_maximum_fusion.1.refs_0_), channel_id=1, source_target_pairs={{0,16},{4,12},{8,24},{12,4},{16,0},{20,28},{24,8},{28,20},{1,17},{... | collective-permute-start | bytes 983048 | tf_op jit(solution)/shard_map/ppermute | solution.py:354
  25.4 7.8 %collective-permute-start.5 = (bf16[640,256]{1,0:T(8,128)(2,1)S(1)}, bf16[640,256]{1,0:T(8,128)(2,1)S(1)}, u32[]{:S(2)}, u32[]{:S(2)}) collective-permute-start(bf16[640,256]{1,0:T(8,128)(2,1)S(1)} %collective-permute-done.2.refs_1_), channel_id=1, source_target_pairs={{0,16},{4,12},{8,24},{12,4},{16,0},{20,28},{24,8},{28,20},{1,17},{... | collective-permute-start | bytes 983048 | tf_op jit(solution)/shard_map/ppermute | solution.py:354
  27.4 5.3 %collective-permute-start.6 = (bf16[320,256]{1,0:T(8,128)(2,1)S(1)}, bf16[320,256]{1,0:T(8,128)(2,1)S(1)}, u32[]{:S(2)}, u32[]{:S(2)}) collective-permute-start(bf16[320,256]{1,0:T(8,128)(2,1)S(1)} %collective-permute-done.3), channel_id=1, source_target_pairs={{0,8},{4,20},{8,0},{12,28},{16,24},{20,4},{24,16},{28,12},{1,9},{5... | collective-permute-start | bytes 491528 | tf_op jit(solution)/shard_map/ppermute | solution.py:350
  33.2 3.1 %collective-permute-start.9 = (bf16[2560,256]{1,0:T(8,128)(2,1)S(1)}, bf16[2560,256]{1,0:T(8,128)(2,1)S(1)}, u32[]{:S(2)}, u32[]{:S(2)}) collective-permute-start(bf16[2560,256]{1,0:T(8,128)(2,1)S(1)} %constant_dynamic-update-slice_fusion.2), channel_id=1, source_target_pairs={{0,4},{4,0},{8,12},{12,8},{16,20},{20,16},{24,28},{28,24},{1,5},{5... | collective-permute-start | bytes 3932168 | tf_op jit(solution)/shard_map/ppermute | solution.py:336
  33.4 7.1 %collective-permute-start.7 = (bf16[640,256]{1,0:T(8,128)(2,1)S(1)}, bf16[640,256]{1,0:T(8,128)(2,1)S(1)}, u32[]{:S(2)}, u32[]{:S(2)}) collective-permute-start(bf16[640,256]{1,0:T(8,128)(2,1)S(1)} %constant_dynamic-update-slice_fusion.refs_0_), channel_id=1, source_target_pairs={{0,16},{4,12},{8,24},{12,4},{16,0},{20,28},{24,8},{28,20},{1,17},{... | collective-permute-start | bytes 983048 | tf_op jit(solution)/shard_map/ppermute | solution.py:354
  34.7 5.8 %collective-permute-start.8 = (bf16[640,256]{1,0:T(8,128)(2,1)S(1)}, bf16[640,256]{1,0:T(8,128)(2,1)S(1)}, u32[]{:S(2)}, u32[]{:S(2)}) collective-permute-start(bf16[640,256]{1,0:T(8,128)(2,1)S(1)} %constant_dynamic-update-slice_fusion.refs_0_), channel_id=1, source_target_pairs={{0,4},{4,0},{8,12},{12,8},{16,20},{20,16},{24,28},{28,24},{1,5},{5... | collective-permute-start | bytes 983048 | tf_op jit(solution)/shard_map/ppermute | solution.py:336
  40.5 1.6 %collective-permute-start.10 = (bf16[640,256]{1,0:T(8,128)(2,1)S(1)}, bf16[640,256]{1,0:T(8,128)(2,1)S(1)}, u32[]{:S(2)}, u32[]{:S(2)}) collective-permute-start(bf16[640,256]{1,0:T(8,128)(2,1)S(1)} %collective-permute-done.7.refs_1_), channel_id=1, source_target_pairs={{0,4},{4,0},{8,12},{12,8},{16,20},{20,16},{24,28},{28,24},{1,5},{5... | collective-permute-start | bytes 983048 | tf_op jit(solution)/shard_map/ppermute | solution.py:336
  42.1 2.6 %collective-permute-start.11 = (bf16[4,480,256]{2,1,0:T(8,128)(2,1)S(1)}, bf16[4,480,256]{2,1,0:T(8,128)(2,1)S(1)}, u32[]{:S(2)}, u32[]{:S(2)}) collective-permute-start(bf16[4,480,256]{2,1,0:T(8,128)(2,1)S(1)} %get-tuple-element.168), channel_id=1, source_target_pairs={{0,4},{4,0},{8,12},{12,8},{16,20},{20,16},{24,28},{28,24},{1,5},{5... | collective-permute-start | bytes 2949128 | tf_op jit(solution)/shard_map/ppermute | solution.py:336
  44.7 1.6 %collective-permute-start.12 = (bf16[4,160,256]{2,1,0:T(8,128)(2,1)S(1)}, bf16[4,160,256]{2,1,0:T(8,128)(2,1)S(1)}, u32[]{:S(2)}, u32[]{:S(2)}) collective-permute-start(bf16[4,160,256]{2,1,0:T(8,128)(2,1)S(1)} %get-tuple-element.185), channel_id=1, source_target_pairs={{0,4},{4,0},{8,12},{12,8},{16,20},{20,16},{24,28},{28,24},{1,5},{5... | collective-permute-start | bytes 983048 | tf_op jit(solution)/shard_map/ppermute | solution.py:336
  46.5 7.1 %collective-permute-start.13 = (bf16[640,256]{1,0:T(8,128)(2,1)S(1)}, bf16[640,256]{1,0:T(8,128)(2,1)S(1)}, u32[]{:S(2)}, u32[]{:S(2)}) collective-permute-start(bf16[640,256]{1,0:T(8,128)(2,1)S(1)} %pad_maximum_fusion.2), channel_id=1, source_target_pairs={{0,16},{4,12},{8,24},{12,4},{16,0},{20,28},{24,8},{28,20},{1,17},{... | collective-permute-start | bytes 983048 | tf_op jit(solution)/shard_map/ppermute | solution.py:354
  47.8 10.7 %collective-permute-start.15 = (bf16[640,256]{1,0:T(8,128)(2,1)S(1)}, bf16[640,256]{1,0:T(8,128)(2,1)S(1)}, u32[]{:S(2)}, u32[]{:S(2)}) collective-permute-start(bf16[640,256]{1,0:T(8,128)(2,1)S(1)} %pad_maximum_fusion.3), channel_id=1, source_target_pairs={{0,16},{4,12},{8,24},{12,4},{16,0},{20,28},{24,8},{28,20},{1,17},{... | collective-permute-start | bytes 983048 | tf_op jit(solution)/shard_map/ppermute | solution.py:354
  53.7 5.4 %collective-permute-start.14 = (bf16[320,256]{1,0:T(8,128)(2,1)S(1)}, bf16[320,256]{1,0:T(8,128)(2,1)S(1)}, u32[]{:S(2)}, u32[]{:S(2)}) collective-permute-start(bf16[320,256]{1,0:T(8,128)(2,1)S(1)} %get-tuple-element.217), channel_id=1, source_target_pairs={{0,8},{4,20},{8,0},{12,28},{16,24},{20,4},{24,16},{28,12},{1,9},{5... | collective-permute-start | bytes 491528 | tf_op jit(solution)/shard_map/ppermute | solution.py:350
  57.4 5.4 %collective-permute-start.16 = (bf16[320,256]{1,0:T(8,128)(2,1)S(1)}, bf16[320,256]{1,0:T(8,128)(2,1)S(1)}, u32[]{:S(2)}, u32[]{:S(2)}) collective-permute-start(bf16[320,256]{1,0:T(8,128)(2,1)S(1)} %get-tuple-element.216), channel_id=1, source_target_pairs={{0,8},{4,20},{8,0},{12,28},{16,24},{20,4},{24,16},{28,12},{1,9},{5... | collective-permute-start | bytes 491528 | tf_op jit(solution)/shard_map/ppermute | solution.py:350
  62.9 7.3 %collective-permute-start.18 = (bf16[160,256]{1,0:T(8,128)(2,1)S(1)}, bf16[160,256]{1,0:T(8,128)(2,1)S(1)}, u32[]{:S(2)}, u32[]{:S(2)}) collective-permute-start(bf16[160,256]{1,0:T(8,128)(2,1)S(1)} %get-tuple-element.220), channel_id=1, source_target_pairs={{0,2},{1,3},{2,0},{3,1},{4,6},{5,7},{6,4},{7,5},{8,10},{9,11},{10,... | collective-permute-start | bytes 245768 | tf_op jit(solution)/shard_map/ppermute | solution.py:336
  65.0 5.3 %collective-permute-start.17 = (bf16[160,256]{1,0:T(8,128)(2,1)S(1)}, bf16[160,256]{1,0:T(8,128)(2,1)S(1)}, u32[]{:S(2)}, u32[]{:S(2)}) collective-permute-start(bf16[160,256]{1,0:T(8,128)(2,1)S(1)} %get-tuple-element.219), channel_id=1, source_target_pairs={{0,1},{1,0},{2,3},{3,2},{4,5},{5,4},{6,7},{7,6},{8,9},{9,8},{10,11... | collective-permute-start | bytes 245768 | tf_op jit(solution)/shard_map/ppermute | solution.py:336
  65.3 6.3 %collective-permute-start.19 = (bf16[160,256]{1,0:T(8,128)(2,1)S(1)}, bf16[160,256]{1,0:T(8,128)(2,1)S(1)}, u32[]{:S(2)}, u32[]{:S(2)}) collective-permute-start(bf16[160,256]{1,0:T(8,128)(2,1)S(1)} %get-tuple-element.218), channel_id=1, source_target_pairs={{0,3},{1,2},{2,1},{3,0},{4,7},{5,6},{6,5},{7,4},{8,11},{9,10},{10,... | collective-permute-start | bytes 245768 | tf_op jit(solution)/shard_map/ppermute | solution.py:336
  71.9 6.2 %collective-permute-start.20 = (bf16[256,256]{1,0:T(8,128)(2,1)S(1)}, bf16[256,256]{1,0:T(8,128)(2,1)S(1)}, u32[]{:S(2)}, u32[]{:S(2)}) collective-permute-start(bf16[256,256]{1,0:T(8,128)(2,1)S(1)} %shard_map.110.refs_0_), channel_id=1, source_target_pairs={{0,8},{4,20},{8,0},{12,28},{16,24},{20,4},{24,16},{28,12},{1,9},{5... | collective-permute-start | bytes 393224 | tf_op jit(solution)/shard_map/ppermute | solution.py:350
  73.2 5.0 %collective-permute-start.21 = (bf16[256,256]{1,0:T(8,128)(2,1)S(1)}, bf16[256,256]{1,0:T(8,128)(2,1)S(1)}, u32[]{:S(2)}, u32[]{:S(2)}) collective-permute-start(bf16[256,256]{1,0:T(8,128)(2,1)S(1)} %shard_map.110.refs_0_), channel_id=1, source_target_pairs={{0,16},{4,12},{8,24},{12,4},{16,0},{20,28},{24,8},{28,20},{1,17},{... | collective-permute-start | bytes 393224 | tf_op jit(solution)/shard_map/ppermute | solution.py:354
  74.0 5.9 %collective-permute-start.22 = (bf16[256,256]{1,0:T(8,128)(2,1)S(1)}, bf16[256,256]{1,0:T(8,128)(2,1)S(1)}, u32[]{:S(2)}, u32[]{:S(2)}) collective-permute-start(bf16[256,256]{1,0:T(8,128)(2,1)S(1)} %shard_map.110.refs_0_), channel_id=1, source_target_pairs={{0,24},{4,28},{8,16},{12,20},{16,8},{20,12},{24,0},{28,4},{1,25},{... | collective-permute-start | bytes 393224 | tf_op jit(solution)/shard_map/ppermute | solution.py:336
  79.9 2.0 %collective-permute-start.23 = (bf16[1024,256]{1,0:T(8,128)(2,1)S(1)}, bf16[1024,256]{1,0:T(8,128)(2,1)S(1)}, u32[]{:S(2)}, u32[]{:S(2)}) collective-permute-start(bf16[1024,256]{1,0:T(8,128)(2,1)S(1)} %pad_maximum_fusion), channel_id=1, source_target_pairs={{0,4},{4,0},{8,12},{12,8},{16,20},{20,16},{24,28},{28,24},{1,5},{5... | collective-permute-start | bytes 1572872 | tf_op jit(solution)/shard_map/ppermute | solution.py:336

commit v6 on v5

--- a/solution.py
+++ b/solution.py
@@ -515,7 +515,7 @@
     first = swap_first(token_cols)
     second = swap_second(token_cols)
     down_wgrad = wgrad(hidden, y_all)
-    first, second, sixth, down_wgrad = fence(first, second, sixth, down_wgrad)
+    sixth, first, second, down_wgrad = fence(sixth, first, second, down_wgrad)
     across = swap(jnp.concatenate([token_cols, first, second, sixth]), "dp", 1)
     (placed,) = call(
         functools.partial(place_kernel, share, 0, 4),

time: 83 us -> 82.9 us (level)
    ppermute x13, waiting for transfers between devices: 13.9 us -> 12.3 us  [swap(): return lax.ppermute(array, axis, [(i, i ^ distance) for i in range(size)])]
    ppermute x5, waiting for transfers between devices: 8.52 us -> 9.45 us  [swap_first(): lax.ppermute(array, 'dp', [(i, i ^ (4 if i % 2 else 2)) for i in range(8)])]
  transfers between devices with their start and end apart: 24 -> 24, of which waited for: 17 -> 18; matrix products, arithmetic and copies ran while one was open for 1% -> 1% of each run, Pallas kernels for 27% -> 27%
where the time goes in v6:
time: 82.9 us; the launch traced here: 82.7 us
  starting transfers between devices  28 us (34%)
  waiting for transfers between devices  28 us (34%)
  Pallas kernels  24.9 us (30%)
  between operations  1.04 us (1%)
    pallas_call x11, Pallas kernels, call(): pl.pallas_call(body, out_shape=outs, in_specs=[pl.BlockSpec(memory_space=...  24 us
    ppermute x13, starting transfers between devices, swap(): return lax.ppermute(array, axis, [(i, i ^ distance) for i in range(size)])  13.7 us
    ppermute x13, waiting for transfers between devices, swap(): return lax.ppermute(array, axis, [(i, i ^ distance) for i in range(size)])  12.3 us
    ppermute x5, waiting for transfers between devices, swap_first(): lax.ppermute(array, 'dp', [(i, i ^ (4 if i % 2 else 2)) for i in range(8)])  9.45 us
    ppermute x6, starting transfers between devices, swap_second(): lax.ppermute(array, 'dp', [(i, i ^ (2 if i % 2 else 4)) for i in range(8)])  7.72 us
    ppermute x5, starting transfers between devices, swap_first(): lax.ppermute(array, 'dp', [(i, i ^ (4 if i % 2 else 2)) for i in range(8)])  6.56 us
    ppermute x6, waiting for transfers between devices, swap_second(): lax.ppermute(array, 'dp', [(i, i ^ (2 if i % 2 else 4)) for i in range(8)])  6.26 us
  transfers between devices with their start and end apart: 24, of which 18 were waited for; matrix products, arithmetic and copies ran while one was open for 1% of the time, Pallas kernels for 27%

profile of v6, /device:TPU:0, one launch (start us, length us, event | category | flops | bytes accessed | tf_op | source)
XLA Modules:
  0.0 82.7 jit_solution(7059301575287527594)
XLA Ops:
  0.6 1.4 %shard_map.102 = (bf16[320,256]{1,0:T(8,128)(2,1)S(1)}, bf16[320,256]{1,0:T(8,128)(2,1)S(1)}, bf16[320,256]{1,0:T(8,128)(2,1)S(1)}, bf16[640,256]{1,0:T(8,128)(2,1)S(1)}) custom-call(s32[1,256]{1,0:T(1,128)} %bitcast.37, f32[1,256]{1,0:T(1,128)} %bitcast.35, bf16[256,2048]{1,0:T(8,128)(2,1)} %tok_far.1, bf16[256,2048]{1,0:T(8,128)(2,1)} %grad_far.1), custom_call_target="tpu_custom_call" | custom-call | flops 1000 | bytes 2918400 | tf_op jit(solution)/shard_map/pallas_call | solution.py:93
  2.1 3.1 %collective-permute-start = (bf16[320,256]{1,0:T(8,128)(2,1)S(1)}, bf16[320,256]{1,0:T(8,128)(2,1)S(1)}, u32[]{:S(2)}, u32[]{:S(2)}) collective-permute-start(bf16[320,256]{1,0:T(8,128)(2,1)S(1)} %get-tuple-element.107), channel_id=1, source_target_pairs={{0,1},{1,0},{2,3},{3,2},{4,5},{5,4},{6,7},{7,6},{8,9},{9,8},{10,11... | collective-permute-start | bytes 491528 | tf_op jit(solution)/shard_map/ppermute | solution.py:336
  5.2 2.5 %collective-permute-start.1 = (bf16[320,256]{1,0:T(8,128)(2,1)S(1)}, bf16[320,256]{1,0:T(8,128)(2,1)S(1)}, u32[]{:S(2)}, u32[]{:S(2)}) collective-permute-start(bf16[320,256]{1,0:T(8,128)(2,1)S(1)} %get-tuple-element.108), channel_id=1, source_target_pairs={{0,3},{1,2},{2,1},{3,0},{4,7},{5,6},{6,5},{7,4},{8,11},{9,10},{10,... | collective-permute-start | bytes 491528 | tf_op jit(solution)/shard_map/ppermute | solution.py:336
  7.7 5.8 %shard_map.103 = (bf16[640,2048]{1,0:T(8,128)(2,1)S(1)}, bf16[640,2048]{1,0:T(8,128)(2,1)S(1)}, bf16[640,512]{1,0:T(8,128)(2,1)S(1)}, bf16[640,512]{1,0:T(8,128)...) custom-call(f32[1,256]{1,0:T(1,128)} %bitcast.36, ...), custom_call_target="tpu_custom_call" | custom-call | flops 1000 | bytes 24183808 | tf_op jit(solution)/shard_map/pallas_call | solution.py:93
  13.5 1.7 %collective-permute-done.1 = bf16[320,256]{1,0:T(8,128)(2,1)S(1)} collective-permute-done((bf16[320,256]{1,0:T(8,128)(2,1)S(1)}, bf16[320,256]{1,0:T(8,128)(2,1)S(1)}, u32[]{:S(2)}, u32[]{:S(2)}) %collective-permute-start.1) | collective-permute-done | bytes 163872 | tf_op jit(solution)/shard_map/ppermute | solution.py:336
  15.3 1.6 %collective-permute-start.2 = (bf16[640,256]{1,0:T(8,128)(2,1)S(1)}, bf16[640,256]{1,0:T(8,128)(2,1)S(1)}, u32[]{:S(2)}, u32[]{:S(2)}) collective-permute-start(bf16[640,256]{1,0:T(8,128)(2,1)S(1)} %pad_maximum_fusion.1.refs_0_), channel_id=1, source_target_pairs={{0,8},{4,20},{8,0},{12,28},{16,24},{20,4},{24,16},{28,12},{1,9},{5... | collective-permute-start | bytes 983048 | tf_op jit(solution)/shard_map/ppermute | solution.py:350
  16.8 1.8 %collective-permute-start.3 = (bf16[320,256]{1,0:T(8,128)(2,1)S(1)}, bf16[320,256]{1,0:T(8,128)(2,1)S(1)}, u32[]{:S(2)}, u32[]{:S(2)}) collective-permute-start(bf16[320,256]{1,0:T(8,128)(2,1)S(1)} %get-tuple-element.132), channel_id=1, source_target_pairs={{0,2},{1,3},{2,0},{3,1},{4,6},{5,7},{6,4},{7,5},{8,10},{9,11},{10,... | collective-permute-start | bytes 491528 | tf_op jit(solution)/shard_map/ppermute | solution.py:336
  18.6 1.5 %collective-permute-start.4 = (bf16[640,256]{1,0:T(8,128)(2,1)S(1)}, bf16[640,256]{1,0:T(8,128)(2,1)S(1)}, u32[]{:S(2)}, u32[]{:S(2)}) collective-permute-start(bf16[640,256]{1,0:T(8,128)(2,1)S(1)} %pad_maximum_fusion.1.refs_0_), channel_id=1, source_target_pairs={{0,16},{4,12},{8,24},{12,4},{16,0},{20,28},{24,8},{28,20},{1,17},{... | collective-permute-start | bytes 983048 | tf_op jit(solution)/shard_map/ppermute | solution.py:354
  20.1 4.7 %collective-permute-done.3 = bf16[320,256]{1,0:T(8,128)(2,1)S(1)} collective-permute-done((bf16[320,256]{1,0:T(8,128)(2,1)S(1)}, bf16[320,256]{1,0:T(8,128)(2,1)S(1)}, u32[]{:S(2)}, u32[]{:S(2)}) %collective-permute-start.3) | collective-permute-done | bytes 163872 | tf_op jit(solution)/shard_map/ppermute | solution.py:336
  24.8 0.5 collective-permute-done.2.refs_1_
  25.4 2.0 %collective-permute-start.5 = (bf16[640,256]{1,0:T(8,128)(2,1)S(1)}, bf16[640,256]{1,0:T(8,128)(2,1)S(1)}, u32[]{:S(2)}, u32[]{:S(2)}) collective-permute-start(bf16[640,256]{1,0:T(8,128)(2,1)S(1)} %collective-permute-done.2.refs_1_), channel_id=1, source_target_pairs={{0,16},{4,12},{8,24},{12,4},{16,0},{20,28},{24,8},{28,20},{1,17},{... | collective-permute-start | bytes 983048 | tf_op jit(solution)/shard_map/ppermute | solution.py:354
  27.4 1.5 %collective-permute-start.6 = (bf16[320,256]{1,0:T(8,128)(2,1)S(1)}, bf16[320,256]{1,0:T(8,128)(2,1)S(1)}, u32[]{:S(2)}, u32[]{:S(2)}) collective-permute-start(bf16[320,256]{1,0:T(8,128)(2,1)S(1)} %collective-permute-done.3), channel_id=1, source_target_pairs={{0,8},{4,20},{8,0},{12,28},{16,24},{20,4},{24,16},{28,12},{1,9},{5... | collective-permute-start | bytes 491528 | tf_op jit(solution)/shard_map/ppermute | solution.py:350
  28.9 3.8 %collective-permute-done.6 = bf16[320,256]{1,0:T(8,128)(2,1)S(1)} collective-permute-done((bf16[320,256]{1,0:T(8,128)(2,1)S(1)}, bf16[320,256]{1,0:T(8,128)(2,1)S(1)}, u32[]{:S(2)}, u32[]{:S(2)}) %collective-permute-start.6) | collective-permute-done | bytes 163872 | tf_op jit(solution)/shard_map/ppermute | solution.py:350
  32.7 0.5 collective-permute-done.5.refs_3_
  33.4 1.3 %collective-permute-start.7 = (bf16[640,256]{1,0:T(8,128)(2,1)S(1)}, bf16[640,256]{1,0:T(8,128)(2,1)S(1)}, u32[]{:S(2)}, u32[]{:S(2)}) collective-permute-start(bf16[640,256]{1,0:T(8,128)(2,1)S(1)} %constant_dynamic-update-slice_fusion.refs_0_), channel_id=1, source_target_pairs={{0,16},{4,12},{8,24},{12,4},{16,0},{20,28},{24,8},{28,20},{1,17},{... | collective-permute-start | bytes 983048 | tf_op jit(solution)/shard_map/ppermute | solution.py:354
  34.7 1.7 %collective-permute-done.9.refs_4_ = bf16[2560,256]{1,0:T(8,128)(2,1)S(1)} collective-permute-done((bf16[2560,256]{1,0:T(8,128)(2,1)S(1)}, bf16[2560,256]{1,0:T(8,128)(2,1)S(1)}, u32[]{:S(2)}, u32[]{:S(2)}) %collective-permute-start.9) | collective-permute-done | bytes 1310752 | tf_op jit(solution)/shard_map/ppermute | solution.py:336
  36.4 4.0 %shard_map.104 = (bf16[640,2048]{1,0:T(8,128)(2,1)S(1)}, bf16[640,2048]{1,0:T(8,128)(2,1)S(1)}, bf16[640,512]{1,0:T(8,128)(2,1)S(1)}, bf16[640,512]{1,0:T(8,128)...) custom-call(bf16[640,256]{1,0:T(8,128)(2,1)S(1)} %pad_maximum_fusion, ...), custom_call_target="tpu_custom_call", output_to_operand_aliasing={{0}: (8, {}), {1}: (9, {}), {2}: (10, {}), {3}: (11, {}), {... | custom-call | flops 1000 | bytes 27262976 | tf_op jit(solution)/shard_map/pallas_call | solution.py:93
  40.3 0.2 collective-permute-done.7.refs_1_
  40.6 1.2 %shard_map.105 = (f32[160,512]{1,0:T(8,128)S(1)}, f32[160,512]{1,0:T(8,128)S(1)}, f32[160,512]{1,0:T(8,128)S(1)}) custom-call(bf16[640,256]{1,0:T(8,128)(2,1)S(1)} %constant_dynamic-update-slice_fusion.refs_0_, bf16[640,256]{1,0:T(8,128)(2,1)S(1)} %collective-permute-done.7.refs_1_, bf16[640,256]{1,0:T(8,128)(2,1)S(1)} %collective-permute-done.8.refs_2_, ...), custom_call_target="tpu_custom_call" | custom-call | flops 1000 | bytes 8257536 | tf_op jit(solution)/shard_map/pallas_call | solution.py:93
  41.8 0.4 collective-permute-done.10.refs_3_
  42.3 1.5 %shard_map.106 = (bf16[640,2048]{1,0:T(8,128)(2,1)S(1)}, bf16[640,2048]{1,0:T(8,128)(2,1)S(1)}, bf16[640,512]{1,0:T(8,128)(2,1)S(1)}, bf16[640,512]{1,0:T(8,128)...) custom-call(bf16[640,256]{1,0:T(8,128)(2,1)S(1)} %constant_dynamic-u, ...), custom_call_target="tpu_custom_call", output_to_operand_aliasing={{0}: (10, {}), {1}: (11, {}), {2}: (12, {}), {3}: (13, {}),... | custom-call | flops 1000 | bytes 23330816 | tf_op jit(solution)/shard_map/pallas_call | solution.py:93
  43.7 1.0 %collective-permute-done.11 = bf16[4,480,256]{2,1,0:T(8,128)(2,1)S(1)} collective-permute-done((bf16[4,480,256]{2,1,0:T(8,128)(2,1)S(1)}, bf16[4,480,256]{2,1,0:T(8,128)(2,1)S(1)}, u32[]{:S(2)}, u32[]{:S(2)}) %collective-permute-start.11) | collective-permute-done | bytes 983072 | tf_op jit(solution)/shard_map/ppermute | solution.py:336
  44.9 0.8 %shard_map.107 = bf16[4,160,256]{2,1,0:T(8,128)(2,1)S(1)} custom-call(bf16[640,512]{1,0:T(8,128)(2,1)S(1)} %get-tuple-element.186.gate_grad.right, bf16[640,512]{1,0:T(8,128)(2,1)S(1)} %get-tuple-element.187.up_grad.right, bf16[2048,512]{1,0:T(8,128)(2,1)S(1)} %get-tuple-element.138.refs_5_.refs_3_.refs_7_.w_gate, ...), custom_call_target="tpu_custom_call" | custom-call | flops 1000 | bytes 5832704 | tf_op jit(solution)/shard_map/pallas_call | solution.py:93
  45.7 0.2 add_convert_fusion.4
  45.9 0.4 collective-permute-done.12
  46.5 1.3 %collective-permute-start.13 = (bf16[640,256]{1,0:T(8,128)(2,1)S(1)}, bf16[640,256]{1,0:T(8,128)(2,1)S(1)}, u32[]{:S(2)}, u32[]{:S(2)}) collective-permute-start(bf16[640,256]{1,0:T(8,128)(2,1)S(1)} %pad_maximum_fusion.2), channel_id=1, source_target_pairs={{0,16},{4,12},{8,24},{12,4},{16,0},{20,28},{24,8},{28,20},{1,17},{... | collective-permute-start | bytes 983048 | tf_op jit(solution)/shard_map/ppermute | solution.py:354
  47.8 0.8 %collective-permute-start.15 = (bf16[640,256]{1,0:T(8,128)(2,1)S(1)}, bf16[640,256]{1,0:T(8,128)(2,1)S(1)}, u32[]{:S(2)}, u32[]{:S(2)}) collective-permute-start(bf16[640,256]{1,0:T(8,128)(2,1)S(1)} %pad_maximum_fusion.3), channel_id=1, source_target_pairs={{0,16},{4,12},{8,24},{12,4},{16,0},{20,28},{24,8},{28,20},{1,17},{... | collective-permute-start | bytes 983048 | tf_op jit(solution)/shard_map/ppermute | solution.py:354
  48.6 5.0 %collective-permute-done.13 = bf16[640,256]{1,0:T(8,128)(2,1)S(1)} collective-permute-done((bf16[640,256]{1,0:T(8,128)(2,1)S(1)}, bf16[640,256]{1,0:T(8,128)(2,1)S(1)}, u32[]{:S(2)}, u32[]{:S(2)}) %collective-permute-start.13) | collective-permute-done | bytes 327712 | tf_op jit(solution)/shard_map/ppermute | solution.py:354
  53.7 1.1 %collective-permute-start.14 = (bf16[320,256]{1,0:T(8,128)(2,1)S(1)}, bf16[320,256]{1,0:T(8,128)(2,1)S(1)}, u32[]{:S(2)}, u32[]{:S(2)}) collective-permute-start(bf16[320,256]{1,0:T(8,128)(2,1)S(1)} %get-tuple-element.217), channel_id=1, source_target_pairs={{0,8},{4,20},{8,0},{12,28},{16,24},{20,4},{24,16},{28,12},{1,9},{5... | collective-permute-start | bytes 491528 | tf_op jit(solution)/shard_map/ppermute | solution.py:350
  54.8 2.7 %shard_map.108 = bf16[2048,512]{1,0:T(8,128)(2,1)} custom-call(bf16[640,2048]{1,0:T(8,128)(2,1)S(1)} %get-tuple-element.194.left, bf16[640,512]{1,0:T(8,128)(2,1)S(1)} %get-tuple-element.187.up_grad.right), custom_call_target="tpu_custom_call" | custom-call | flops 1000 | bytes 5373952 | tf_op jit(solution)/shard_map/pallas_call | solution.py:93
  57.4 1.1 %collective-permute-start.16 = (bf16[320,256]{1,0:T(8,128)(2,1)S(1)}, bf16[320,256]{1,0:T(8,128)(2,1)S(1)}, u32[]{:S(2)}, u32[]{:S(2)}) collective-permute-start(bf16[320,256]{1,0:T(8,128)(2,1)S(1)} %get-tuple-element.216), channel_id=1, source_target_pairs={{0,8},{4,20},{8,0},{12,28},{16,24},{20,4},{24,16},{28,12},{1,9},{5... | collective-permute-start | bytes 491528 | tf_op jit(solution)/shard_map/ppermute | solution.py:350
  58.5 0.6 collective-permute-done.14
  59.2 3.6 %collective-permute-done.16 = bf16[320,256]{1,0:T(8,128)(2,1)S(1)} collective-permute-done((bf16[320,256]{1,0:T(8,128)(2,1)S(1)}, bf16[320,256]{1,0:T(8,128)(2,1)S(1)}, u32[]{:S(2)}, u32[]{:S(2)}) %collective-permute-start.16) | collective-permute-done | bytes 163872 | tf_op jit(solution)/shard_map/ppermute | solution.py:350
  62.9 2.1 %collective-permute-start.18 = (bf16[160,256]{1,0:T(8,128)(2,1)S(1)}, bf16[160,256]{1,0:T(8,128)(2,1)S(1)}, u32[]{:S(2)}, u32[]{:S(2)}) collective-permute-start(bf16[160,256]{1,0:T(8,128)(2,1)S(1)} %get-tuple-element.220), channel_id=1, source_target_pairs={{0,2},{1,3},{2,0},{3,1},{4,6},{5,7},{6,4},{7,5},{8,10},{9,11},{10,... | collective-permute-start | bytes 245768 | tf_op jit(solution)/shard_map/ppermute | solution.py:336
  65.0 0.3 collective-permute-start.17
  65.3 2.1 %collective-permute-start.19 = (bf16[160,256]{1,0:T(8,128)(2,1)S(1)}, bf16[160,256]{1,0:T(8,128)(2,1)S(1)}, u32[]{:S(2)}, u32[]{:S(2)}) collective-permute-start(bf16[160,256]{1,0:T(8,128)(2,1)S(1)} %get-tuple-element.218), channel_id=1, source_target_pairs={{0,3},{1,2},{2,1},{3,0},{4,7},{5,6},{6,5},{7,4},{8,11},{9,10},{10,... | collective-permute-start | bytes 245768 | tf_op jit(solution)/shard_map/ppermute | solution.py:336
  67.4 2.8 %shard_map.109 = bf16[2048,512]{1,0:T(8,128)(2,1)} custom-call(bf16[640,2048]{1,0:T(8,128)(2,1)S(1)} %get-tuple-element.194.left, bf16[640,512]{1,0:T(8,128)(2,1)S(1)} %get-tuple-element.186.gate_grad.right), custom_call_target="tpu_custom_call" | custom-call | flops 1000 | bytes 5373952 | tf_op jit(solution)/shard_map/pallas_call | solution.py:93
  70.3 1.3 %collective-permute-done.19.r3 = bf16[160,256]{1,0:T(8,128)(2,1)S(1)} collective-permute-done((bf16[160,256]{1,0:T(8,128)(2,1)S(1)}, bf16[160,256]{1,0:T(8,128)(2,1)S(1)}, u32[]{:S(2)}, u32[]{:S(2)}) %collective-permute-start.19) | collective-permute-done | bytes 81952 | tf_op jit(solution)/shard_map/ppermute | solution.py:336
  71.6 0.3 shard_map.110.refs_0_
  71.9 1.5 %collective-permute-start.20 = (bf16[256,256]{1,0:T(8,128)(2,1)S(1)}, bf16[256,256]{1,0:T(8,128)(2,1)S(1)}, u32[]{:S(2)}, u32[]{:S(2)}) collective-permute-start(bf16[256,256]{1,0:T(8,128)(2,1)S(1)} %shard_map.110.refs_0_), channel_id=1, source_target_pairs={{0,24},{4,28},{8,16},{12,20},{16,8},{20,12},{24,0},{28,4},{1,25},{... | collective-permute-start | bytes 393224 | tf_op jit(solution)/shard_map/ppermute | solution.py:336
  73.4 1.4 %collective-permute-start.21 = (bf16[256,256]{1,0:T(8,128)(2,1)S(1)}, bf16[256,256]{1,0:T(8,128)(2,1)S(1)}, u32[]{:S(2)}, u32[]{:S(2)}) collective-permute-start(bf16[256,256]{1,0:T(8,128)(2,1)S(1)} %shard_map.110.refs_0_), channel_id=1, source_target_pairs={{0,8},{4,20},{8,0},{12,28},{16,24},{20,4},{24,16},{28,12},{1,9},{5... | collective-permute-start | bytes 393224 | tf_op jit(solution)/shard_map/ppermute | solution.py:350
  74.7 0.7 collective-permute-start.22
  75.5 2.7 %shard_map.111 = bf16[512,2048]{1,0:T(8,128)(2,1)} custom-call(bf16[640,512]{1,0:T(8,128)(2,1)S(1)} %get-tuple-element.198.left, bf16[640,2048]{1,0:T(8,128)(2,1)S(1)} %get-tuple-element.199.right), custom_call_target="tpu_custom_call" | custom-call | flops 1000 | bytes 5373952 | tf_op jit(solution)/shard_map/pallas_call | solution.py:93
  78.2 0.9 %collective-permute-done.21.refs_1_ = bf16[256,256]{1,0:T(8,128)(2,1)S(1)} collective-permute-done((bf16[256,256]{1,0:T(8,128)(2,1)S(1)}, bf16[256,256]{1,0:T(8,128)(2,1)S(1)}, u32[]{:S(2)}, u32[]{:S(2)}) %collective-permute-start.21) | collective-permute-done | bytes 131104 | tf_op jit(solution)/shard_map/ppermute | solution.py:350
  79.1 0.6 collective-permute-done.22.refs_2_
  79.8 0.8 %shard_map.112.refs_1_ = bf16[256,2048]{1,0:T(8,128)(2,1)} custom-call(bf16[256,256]{1,0:T(8,128)(2,1)S(1)} %shard_map.110.refs_0_, bf16[256,256]{1,0:T(8,128)(2,1)S(1)} %collective-permute-done.21.refs_1_, bf16[256,256]{1,0:T(8,128)(2,1)S(1)} %collective-permute-done.22.refs_2_, bf16[256,256]{1,0:T(8,128)(2,1)S(1)} %collective-permute-done.20.refs_3_), custom_call_target="tpu_custom_call" | custom-call | flops 1000 | bytes 1572864 | tf_op jit(solution)/shard_map/pallas_call | solution.py:93
  80.7 1.1 %collective-permute-done.23.refs_0_ = bf16[1024,256]{1,0:T(8,128)(2,1)S(1)} collective-permute-done((bf16[1024,256]{1,0:T(8,128)(2,1)S(1)}, bf16[1024,256]{1,0:T(8,128)(2,1)S(1)}, u32[]{:S(2)}, u32[]{:S(2)}) %collective-permute-start.23) | collective-permute-done | bytes 524320 | tf_op jit(solution)/shard_map/ppermute | solution.py:336
  81.7 0.8 shard_map.113
  (33 shorter events, 1.2 us)
Async XLA Ops:
  2.1 11.4 %collective-permute-start = (bf16[320,256]{1,0:T(8,128)(2,1)S(1)}, bf16[320,256]{1,0:T(8,128)(2,1)S(1)}, u32[]{:S(2)}, u32[]{:S(2)}) collective-permute-start(bf16[320,256]{1,0:T(8,128)(2,1)S(1)} %get-tuple-element.107), channel_id=1, source_target_pairs={{0,1},{1,0},{2,3},{3,2},{4,5},{5,4},{6,7},{7,6},{8,9},{9,8},{10,11... | collective-permute-start | bytes 491528 | tf_op jit(solution)/shard_map/ppermute | solution.py:336
  5.2 10.0 %collective-permute-start.1 = (bf16[320,256]{1,0:T(8,128)(2,1)S(1)}, bf16[320,256]{1,0:T(8,128)(2,1)S(1)}, u32[]{:S(2)}, u32[]{:S(2)}) collective-permute-start(bf16[320,256]{1,0:T(8,128)(2,1)S(1)} %get-tuple-element.108), channel_id=1, source_target_pairs={{0,3},{1,2},{2,1},{3,0},{4,7},{5,6},{6,5},{7,4},{8,11},{9,10},{10,... | collective-permute-start | bytes 491528 | tf_op jit(solution)/shard_map/ppermute | solution.py:336
  15.3 10.1 %collective-permute-start.2 = (bf16[640,256]{1,0:T(8,128)(2,1)S(1)}, bf16[640,256]{1,0:T(8,128)(2,1)S(1)}, u32[]{:S(2)}, u32[]{:S(2)}) collective-permute-start(bf16[640,256]{1,0:T(8,128)(2,1)S(1)} %pad_maximum_fusion.1.refs_0_), channel_id=1, source_target_pairs={{0,8},{4,20},{8,0},{12,28},{16,24},{20,4},{24,16},{28,12},{1,9},{5... | collective-permute-start | bytes 983048 | tf_op jit(solution)/shard_map/ppermute | solution.py:350
  16.8 8.0 %collective-permute-start.3 = (bf16[320,256]{1,0:T(8,128)(2,1)S(1)}, bf16[320,256]{1,0:T(8,128)(2,1)S(1)}, u32[]{:S(2)}, u32[]{:S(2)}) collective-permute-start(bf16[320,256]{1,0:T(8,128)(2,1)S(1)} %get-tuple-element.132), channel_id=1, source_target_pairs={{0,2},{1,3},{2,0},{3,1},{4,6},{5,7},{6,4},{7,5},{8,10},{9,11},{10,... | collective-permute-start | bytes 491528 | tf_op jit(solution)/shard_map/ppermute | solution.py:336
  18.6 10.3 %collective-permute-start.4 = (bf16[640,256]{1,0:T(8,128)(2,1)S(1)}, bf16[640,256]{1,0:T(8,128)(2,1)S(1)}, u32[]{:S(2)}, u32[]{:S(2)}) collective-permute-start(bf16[640,256]{1,0:T(8,128)(2,1)S(1)} %pad_maximum_fusion.1.refs_0_), channel_id=1, source_target_pairs={{0,16},{4,12},{8,24},{12,4},{16,0},{20,28},{24,8},{28,20},{1,17},{... | collective-permute-start | bytes 983048 | tf_op jit(solution)/shard_map/ppermute | solution.py:354
  25.4 7.8 %collective-permute-start.5 = (bf16[640,256]{1,0:T(8,128)(2,1)S(1)}, bf16[640,256]{1,0:T(8,128)(2,1)S(1)}, u32[]{:S(2)}, u32[]{:S(2)}) collective-permute-start(bf16[640,256]{1,0:T(8,128)(2,1)S(1)} %collective-permute-done.2.refs_1_), channel_id=1, source_target_pairs={{0,16},{4,12},{8,24},{12,4},{16,0},{20,28},{24,8},{28,20},{1,17},{... | collective-permute-start | bytes 983048 | tf_op jit(solution)/shard_map/ppermute | solution.py:354
  27.4 5.3 %collective-permute-start.6 = (bf16[320,256]{1,0:T(8,128)(2,1)S(1)}, bf16[320,256]{1,0:T(8,128)(2,1)S(1)}, u32[]{:S(2)}, u32[]{:S(2)}) collective-permute-start(bf16[320,256]{1,0:T(8,128)(2,1)S(1)} %collective-permute-done.3), channel_id=1, source_target_pairs={{0,8},{4,20},{8,0},{12,28},{16,24},{20,4},{24,16},{28,12},{1,9},{5... | collective-permute-start | bytes 491528 | tf_op jit(solution)/shard_map/ppermute | solution.py:350
  33.2 3.1 %collective-permute-start.9 = (bf16[2560,256]{1,0:T(8,128)(2,1)S(1)}, bf16[2560,256]{1,0:T(8,128)(2,1)S(1)}, u32[]{:S(2)}, u32[]{:S(2)}) collective-permute-start(bf16[2560,256]{1,0:T(8,128)(2,1)S(1)} %constant_dynamic-update-slice_fusion.2), channel_id=1, source_target_pairs={{0,4},{4,0},{8,12},{12,8},{16,20},{20,16},{24,28},{28,24},{1,5},{5... | collective-permute-start | bytes 3932168 | tf_op jit(solution)/shard_map/ppermute | solution.py:336
  33.4 7.1 %collective-permute-start.7 = (bf16[640,256]{1,0:T(8,128)(2,1)S(1)}, bf16[640,256]{1,0:T(8,128)(2,1)S(1)}, u32[]{:S(2)}, u32[]{:S(2)}) collective-permute-start(bf16[640,256]{1,0:T(8,128)(2,1)S(1)} %constant_dynamic-update-slice_fusion.refs_0_), channel_id=1, source_target_pairs={{0,16},{4,12},{8,24},{12,4},{16,0},{20,28},{24,8},{28,20},{1,17},{... | collective-permute-start | bytes 983048 | tf_op jit(solution)/shard_map/ppermute | solution.py:354
  34.7 5.8 %collective-permute-start.8 = (bf16[640,256]{1,0:T(8,128)(2,1)S(1)}, bf16[640,256]{1,0:T(8,128)(2,1)S(1)}, u32[]{:S(2)}, u32[]{:S(2)}) collective-permute-start(bf16[640,256]{1,0:T(8,128)(2,1)S(1)} %constant_dynamic-update-slice_fusion.refs_0_), channel_id=1, source_target_pairs={{0,4},{4,0},{8,12},{12,8},{16,20},{20,16},{24,28},{28,24},{1,5},{5... | collective-permute-start | bytes 983048 | tf_op jit(solution)/shard_map/ppermute | solution.py:336
  40.5 1.6 %collective-permute-start.10 = (bf16[640,256]{1,0:T(8,128)(2,1)S(1)}, bf16[640,256]{1,0:T(8,128)(2,1)S(1)}, u32[]{:S(2)}, u32[]{:S(2)}) collective-permute-start(bf16[640,256]{1,0:T(8,128)(2,1)S(1)} %collective-permute-done.7.refs_1_), channel_id=1, source_target_pairs={{0,4},{4,0},{8,12},{12,8},{16,20},{20,16},{24,28},{28,24},{1,5},{5... | collective-permute-start | bytes 983048 | tf_op jit(solution)/shard_map/ppermute | solution.py:336
  42.1 2.6 %collective-permute-start.11 = (bf16[4,480,256]{2,1,0:T(8,128)(2,1)S(1)}, bf16[4,480,256]{2,1,0:T(8,128)(2,1)S(1)}, u32[]{:S(2)}, u32[]{:S(2)}) collective-permute-start(bf16[4,480,256]{2,1,0:T(8,128)(2,1)S(1)} %get-tuple-element.168), channel_id=1, source_target_pairs={{0,4},{4,0},{8,12},{12,8},{16,20},{20,16},{24,28},{28,24},{1,5},{5... | collective-permute-start | bytes 2949128 | tf_op jit(solution)/shard_map/ppermute | solution.py:336
  44.7 1.6 %collective-permute-start.12 = (bf16[4,160,256]{2,1,0:T(8,128)(2,1)S(1)}, bf16[4,160,256]{2,1,0:T(8,128)(2,1)S(1)}, u32[]{:S(2)}, u32[]{:S(2)}) collective-permute-start(bf16[4,160,256]{2,1,0:T(8,128)(2,1)S(1)} %get-tuple-element.185), channel_id=1, source_target_pairs={{0,4},{4,0},{8,12},{12,8},{16,20},{20,16},{24,28},{28,24},{1,5},{5... | collective-permute-start | bytes 983048 | tf_op jit(solution)/shard_map/ppermute | solution.py:336
  46.5 7.1 %collective-permute-start.13 = (bf16[640,256]{1,0:T(8,128)(2,1)S(1)}, bf16[640,256]{1,0:T(8,128)(2,1)S(1)}, u32[]{:S(2)}, u32[]{:S(2)}) collective-permute-start(bf16[640,256]{1,0:T(8,128)(2,1)S(1)} %pad_maximum_fusion.2), channel_id=1, source_target_pairs={{0,16},{4,12},{8,24},{12,4},{16,0},{20,28},{24,8},{28,20},{1,17},{... | collective-permute-start | bytes 983048 | tf_op jit(solution)/shard_map/ppermute | solution.py:354
  47.8 10.7 %collective-permute-start.15 = (bf16[640,256]{1,0:T(8,128)(2,1)S(1)}, bf16[640,256]{1,0:T(8,128)(2,1)S(1)}, u32[]{:S(2)}, u32[]{:S(2)}) collective-permute-start(bf16[640,256]{1,0:T(8,128)(2,1)S(1)} %pad_maximum_fusion.3), channel_id=1, source_target_pairs={{0,16},{4,12},{8,24},{12,4},{16,0},{20,28},{24,8},{28,20},{1,17},{... | collective-permute-start | bytes 983048 | tf_op jit(solution)/shard_map/ppermute | solution.py:354
  53.7 5.4 %collective-permute-start.14 = (bf16[320,256]{1,0:T(8,128)(2,1)S(1)}, bf16[320,256]{1,0:T(8,128)(2,1)S(1)}, u32[]{:S(2)}, u32[]{:S(2)}) collective-permute-start(bf16[320,256]{1,0:T(8,128)(2,1)S(1)} %get-tuple-element.217), channel_id=1, source_target_pairs={{0,8},{4,20},{8,0},{12,28},{16,24},{20,4},{24,16},{28,12},{1,9},{5... | collective-permute-start | bytes 491528 | tf_op jit(solution)/shard_map/ppermute | solution.py:350
  57.4 5.4 %collective-permute-start.16 = (bf16[320,256]{1,0:T(8,128)(2,1)S(1)}, bf16[320,256]{1,0:T(8,128)(2,1)S(1)}, u32[]{:S(2)}, u32[]{:S(2)}) collective-permute-start(bf16[320,256]{1,0:T(8,128)(2,1)S(1)} %get-tuple-element.216), channel_id=1, source_target_pairs={{0,8},{4,20},{8,0},{12,28},{16,24},{20,4},{24,16},{28,12},{1,9},{5... | collective-permute-start | bytes 491528 | tf_op jit(solution)/shard_map/ppermute | solution.py:350
  62.9 7.3 %collective-permute-start.18 = (bf16[160,256]{1,0:T(8,128)(2,1)S(1)}, bf16[160,256]{1,0:T(8,128)(2,1)S(1)}, u32[]{:S(2)}, u32[]{:S(2)}) collective-permute-start(bf16[160,256]{1,0:T(8,128)(2,1)S(1)} %get-tuple-element.220), channel_id=1, source_target_pairs={{0,2},{1,3},{2,0},{3,1},{4,6},{5,7},{6,4},{7,5},{8,10},{9,11},{10,... | collective-permute-start | bytes 245768 | tf_op jit(solution)/shard_map/ppermute | solution.py:336
  65.0 5.3 %collective-permute-start.17 = (bf16[160,256]{1,0:T(8,128)(2,1)S(1)}, bf16[160,256]{1,0:T(8,128)(2,1)S(1)}, u32[]{:S(2)}, u32[]{:S(2)}) collective-permute-start(bf16[160,256]{1,0:T(8,128)(2,1)S(1)} %get-tuple-element.219), channel_id=1, source_target_pairs={{0,1},{1,0},{2,3},{3,2},{4,5},{5,4},{6,7},{7,6},{8,9},{9,8},{10,11... | collective-permute-start | bytes 245768 | tf_op jit(solution)/shard_map/ppermute | solution.py:336
  65.3 6.3 %collective-permute-start.19 = (bf16[160,256]{1,0:T(8,128)(2,1)S(1)}, bf16[160,256]{1,0:T(8,128)(2,1)S(1)}, u32[]{:S(2)}, u32[]{:S(2)}) collective-permute-start(bf16[160,256]{1,0:T(8,128)(2,1)S(1)} %get-tuple-element.218), channel_id=1, source_target_pairs={{0,3},{1,2},{2,1},{3,0},{4,7},{5,6},{6,5},{7,4},{8,11},{9,10},{10,... | collective-permute-start | bytes 245768 | tf_op jit(solution)/shard_map/ppermute | solution.py:336
  71.9 6.2 %collective-permute-start.20 = (bf16[256,256]{1,0:T(8,128)(2,1)S(1)}, bf16[256,256]{1,0:T(8,128)(2,1)S(1)}, u32[]{:S(2)}, u32[]{:S(2)}) collective-permute-start(bf16[256,256]{1,0:T(8,128)(2,1)S(1)} %shard_map.110.refs_0_), channel_id=1, source_target_pairs={{0,24},{4,28},{8,16},{12,20},{16,8},{20,12},{24,0},{28,4},{1,25},{... | collective-permute-start | bytes 393224 | tf_op jit(solution)/shard_map/ppermute | solution.py:336
  73.4 5.7 %collective-permute-start.21 = (bf16[256,256]{1,0:T(8,128)(2,1)S(1)}, bf16[256,256]{1,0:T(8,128)(2,1)S(1)}, u32[]{:S(2)}, u32[]{:S(2)}) collective-permute-start(bf16[256,256]{1,0:T(8,128)(2,1)S(1)} %shard_map.110.refs_0_), channel_id=1, source_target_pairs={{0,8},{4,20},{8,0},{12,28},{16,24},{20,4},{24,16},{28,12},{1,9},{5... | collective-permute-start | bytes 393224 | tf_op jit(solution)/shard_map/ppermute | solution.py:350
  74.7 5.0 %collective-permute-start.22 = (bf16[256,256]{1,0:T(8,128)(2,1)S(1)}, bf16[256,256]{1,0:T(8,128)(2,1)S(1)}, u32[]{:S(2)}, u32[]{:S(2)}) collective-permute-start(bf16[256,256]{1,0:T(8,128)(2,1)S(1)} %shard_map.110.refs_0_), channel_id=1, source_target_pairs={{0,16},{4,12},{8,24},{12,4},{16,0},{20,28},{24,8},{28,20},{1,17},{... | collective-permute-start | bytes 393224 | tf_op jit(solution)/shard_map/ppermute | solution.py:354
  79.8 2.0 %collective-permute-start.23 = (bf16[1024,256]{1,0:T(8,128)(2,1)S(1)}, bf16[1024,256]{1,0:T(8,128)(2,1)S(1)}, u32[]{:S(2)}, u32[]{:S(2)}) collective-permute-start(bf16[1024,256]{1,0:T(8,128)(2,1)S(1)} %pad_maximum_fusion), channel_id=1, source_target_pairs={{0,4},{4,0},{8,12},{12,8},{16,20},{20,16},{24,28},{28,24},{1,5},{5... | collective-permute-start | bytes 1572872 | tf_op jit(solution)/shard_map/ppermute | solution.py:336

commit v7 on v5

--- a/solution.py
+++ b/solution.py
@@ -440,9 +440,9 @@
         16,
     )
     later_b = swap(both_b, "dp", 1)
-    later_b, *out_a = fence(later_b, *out_a, *partial)
+    other_a = swap(out_a[6], "dp", 1)
+    later_b, other_a, *out_a = fence(later_b, other_a, *out_a, *partial)
     out_a, partial = out_a[:7], tuple(out_a[7:])
-    other_a = swap(out_a[6], "dp", 1)
     out_b = call(
         functools.partial(late_kernel, share, chunk_b),
         shared + terms_b[:1],
@@ -454,7 +454,7 @@
         16,
         aliases={10 + j: j for j in range(5)},
     )
-    other_a, *out_b = fence(other_a, *out_b)
+    out_b = fence(*out_b)
     x_all, y_all, hidden, gate_grad, up_grad, odd_b = out_b
     (even_b,) = call(
         functools.partial(even_kernel, share, chunk_b),

time: 83 us -> 83.2 us (level)
  transfers between devices with their start and end apart: 24 -> 24, of which waited for: 17 -> 16; matrix products, arithmetic and copies ran while one was open for 1% -> 1% of each run, Pallas kernels for 27% -> 25%
where the time goes in v7:
time: 83.2 us; the launch traced here: 83.1 us
  starting transfers between devices  28.3 us (34%)
  waiting for transfers between devices  28 us (34%)
  Pallas kernels  24.9 us (30%)
  between operations  1.05 us (1%)
    pallas_call x11, Pallas kernels, call(): pl.pallas_call(body, out_shape=outs, in_specs=[pl.BlockSpec(memory_space=...  24 us
    ppermute x13, starting transfers between devices, swap(): return lax.ppermute(array, axis, [(i, i ^ distance) for i in range(size)])  14.3 us
    ppermute x13, waiting for transfers between devices, swap(): return lax.ppermute(array, axis, [(i, i ^ distance) for i in range(size)])  13.8 us
    ppermute x5, waiting for transfers between devices, swap_first(): lax.ppermute(array, 'dp', [(i, i ^ (4 if i % 2 else 2)) for i in range(8)])  8.51 us
    ppermute x6, starting transfers between devices, swap_second(): lax.ppermute(array, 'dp', [(i, i ^ (2 if i % 2 else 4)) for i in range(8)])  7.62 us
    ppermute x5, starting transfers between devices, swap_first(): lax.ppermute(array, 'dp', [(i, i ^ (4 if i % 2 else 2)) for i in range(8)])  6.46 us
    ppermute x6, waiting for transfers between devices, swap_second(): lax.ppermute(array, 'dp', [(i, i ^ (2 if i % 2 else 4)) for i in range(8)])  5.64 us
  transfers between devices with their start and end apart: 24, of which 16 were waited for; matrix products, arithmetic and copies ran while one was open for 1% of the time, Pallas kernels for 25%

profile of v7, /device:TPU:0, one launch (start us, length us, event | category | flops | bytes accessed | tf_op | source)
XLA Modules:
  0.0 83.1 jit_solution(3024627758038539807)
XLA Ops:
  0.6 1.4 %shard_map.102 = (bf16[320,256]{1,0:T(8,128)(2,1)S(1)}, bf16[320,256]{1,0:T(8,128)(2,1)S(1)}, bf16[320,256]{1,0:T(8,128)(2,1)S(1)}, bf16[640,256]{1,0:T(8,128)(2,1)S(1)}) custom-call(s32[1,256]{1,0:T(1,128)} %bitcast.37, f32[1,256]{1,0:T(1,128)} %bitcast.35, bf16[256,2048]{1,0:T(8,128)(2,1)} %tok_far.1, bf16[256,2048]{1,0:T(8,128)(2,1)} %grad_far.1), custom_call_target="tpu_custom_call" | custom-call | flops 1000 | bytes 2918400 | tf_op jit(solution)/shard_map/pallas_call | solution.py:93
  2.1 3.1 %collective-permute-start = (bf16[320,256]{1,0:T(8,128)(2,1)S(1)}, bf16[320,256]{1,0:T(8,128)(2,1)S(1)}, u32[]{:S(2)}, u32[]{:S(2)}) collective-permute-start(bf16[320,256]{1,0:T(8,128)(2,1)S(1)} %get-tuple-element.100), channel_id=1, source_target_pairs={{0,1},{1,0},{2,3},{3,2},{4,5},{5,4},{6,7},{7,6},{8,9},{9,8},{10,11... | collective-permute-start | bytes 491528 | tf_op jit(solution)/shard_map/ppermute | solution.py:336
  5.2 2.5 %collective-permute-start.1 = (bf16[320,256]{1,0:T(8,128)(2,1)S(1)}, bf16[320,256]{1,0:T(8,128)(2,1)S(1)}, u32[]{:S(2)}, u32[]{:S(2)}) collective-permute-start(bf16[320,256]{1,0:T(8,128)(2,1)S(1)} %get-tuple-element.101), channel_id=1, source_target_pairs={{0,3},{1,2},{2,1},{3,0},{4,7},{5,6},{6,5},{7,4},{8,11},{9,10},{10,... | collective-permute-start | bytes 491528 | tf_op jit(solution)/shard_map/ppermute | solution.py:336
  7.7 5.8 %shard_map.103 = (bf16[640,2048]{1,0:T(8,128)(2,1)S(1)}, bf16[640,2048]{1,0:T(8,128)(2,1)S(1)}, bf16[640,512]{1,0:T(8,128)(2,1)S(1)}, bf16[640,512]{1,0:T(8,128)...) custom-call(f32[1,256]{1,0:T(1,128)} %bitcast.36, ...), custom_call_target="tpu_custom_call" | custom-call | flops 1000 | bytes 24183808 | tf_op jit(solution)/shard_map/pallas_call | solution.py:93
  13.5 1.7 %collective-permute-done.1 = bf16[320,256]{1,0:T(8,128)(2,1)S(1)} collective-permute-done((bf16[320,256]{1,0:T(8,128)(2,1)S(1)}, bf16[320,256]{1,0:T(8,128)(2,1)S(1)}, u32[]{:S(2)}, u32[]{:S(2)}) %collective-permute-start.1) | collective-permute-done | bytes 163872 | tf_op jit(solution)/shard_map/ppermute | solution.py:336
  15.3 1.6 %collective-permute-start.2 = (bf16[640,256]{1,0:T(8,128)(2,1)S(1)}, bf16[640,256]{1,0:T(8,128)(2,1)S(1)}, u32[]{:S(2)}, u32[]{:S(2)}) collective-permute-start(bf16[640,256]{1,0:T(8,128)(2,1)S(1)} %pad_maximum_fusion.1.refs_0_), channel_id=1, source_target_pairs={{0,8},{4,20},{8,0},{12,28},{16,24},{20,4},{24,16},{28,12},{1,9},{5... | collective-permute-start | bytes 983048 | tf_op jit(solution)/shard_map/ppermute | solution.py:350
  16.8 1.8 %collective-permute-start.3 = (bf16[320,256]{1,0:T(8,128)(2,1)S(1)}, bf16[320,256]{1,0:T(8,128)(2,1)S(1)}, u32[]{:S(2)}, u32[]{:S(2)}) collective-permute-start(bf16[320,256]{1,0:T(8,128)(2,1)S(1)} %get-tuple-element.125), channel_id=1, source_target_pairs={{0,2},{1,3},{2,0},{3,1},{4,6},{5,7},{6,4},{7,5},{8,10},{9,11},{10,... | collective-permute-start | bytes 491528 | tf_op jit(solution)/shard_map/ppermute | solution.py:336
  18.6 1.5 %collective-permute-start.4 = (bf16[640,256]{1,0:T(8,128)(2,1)S(1)}, bf16[640,256]{1,0:T(8,128)(2,1)S(1)}, u32[]{:S(2)}, u32[]{:S(2)}) collective-permute-start(bf16[640,256]{1,0:T(8,128)(2,1)S(1)} %pad_maximum_fusion.1.refs_0_), channel_id=1, source_target_pairs={{0,16},{4,12},{8,24},{12,4},{16,0},{20,28},{24,8},{28,20},{1,17},{... | collective-permute-start | bytes 983048 | tf_op jit(solution)/shard_map/ppermute | solution.py:354
  20.1 4.7 %collective-permute-done.3 = bf16[320,256]{1,0:T(8,128)(2,1)S(1)} collective-permute-done((bf16[320,256]{1,0:T(8,128)(2,1)S(1)}, bf16[320,256]{1,0:T(8,128)(2,1)S(1)}, u32[]{:S(2)}, u32[]{:S(2)}) %collective-permute-start.3) | collective-permute-done | bytes 163872 | tf_op jit(solution)/shard_map/ppermute | solution.py:336
  24.8 0.5 collective-permute-done.2.refs_1_
  25.4 2.0 %collective-permute-start.5 = (bf16[640,256]{1,0:T(8,128)(2,1)S(1)}, bf16[640,256]{1,0:T(8,128)(2,1)S(1)}, u32[]{:S(2)}, u32[]{:S(2)}) collective-permute-start(bf16[640,256]{1,0:T(8,128)(2,1)S(1)} %collective-permute-done.2.refs_1_), channel_id=1, source_target_pairs={{0,16},{4,12},{8,24},{12,4},{16,0},{20,28},{24,8},{28,20},{1,17},{... | collective-permute-start | bytes 983048 | tf_op jit(solution)/shard_map/ppermute | solution.py:354
  27.4 1.5 %collective-permute-start.6 = (bf16[320,256]{1,0:T(8,128)(2,1)S(1)}, bf16[320,256]{1,0:T(8,128)(2,1)S(1)}, u32[]{:S(2)}, u32[]{:S(2)}) collective-permute-start(bf16[320,256]{1,0:T(8,128)(2,1)S(1)} %collective-permute-done.3), channel_id=1, source_target_pairs={{0,8},{4,20},{8,0},{12,28},{16,24},{20,4},{24,16},{28,12},{1,9},{5... | collective-permute-start | bytes 491528 | tf_op jit(solution)/shard_map/ppermute | solution.py:350
  28.9 3.8 %collective-permute-done.6 = bf16[320,256]{1,0:T(8,128)(2,1)S(1)} collective-permute-done((bf16[320,256]{1,0:T(8,128)(2,1)S(1)}, bf16[320,256]{1,0:T(8,128)(2,1)S(1)}, u32[]{:S(2)}, u32[]{:S(2)}) %collective-permute-start.6) | collective-permute-done | bytes 163872 | tf_op jit(solution)/shard_map/ppermute | solution.py:350
  32.7 0.5 collective-permute-done.5.refs_3_
  33.4 1.3 %collective-permute-start.7 = (bf16[640,256]{1,0:T(8,128)(2,1)S(1)}, bf16[640,256]{1,0:T(8,128)(2,1)S(1)}, u32[]{:S(2)}, u32[]{:S(2)}) collective-permute-start(bf16[640,256]{1,0:T(8,128)(2,1)S(1)} %constant_dynamic-update-slice_fusion.refs_0_), channel_id=1, source_target_pairs={{0,16},{4,12},{8,24},{12,4},{16,0},{20,28},{24,8},{28,20},{1,17},{... | collective-permute-start | bytes 983048 | tf_op jit(solution)/shard_map/ppermute | solution.py:354
  34.7 1.7 %collective-permute-done.9.refs_4_ = bf16[2560,256]{1,0:T(8,128)(2,1)S(1)} collective-permute-done((bf16[2560,256]{1,0:T(8,128)(2,1)S(1)}, bf16[2560,256]{1,0:T(8,128)(2,1)S(1)}, u32[]{:S(2)}, u32[]{:S(2)}) %collective-permute-start.9) | collective-permute-done | bytes 1310752 | tf_op jit(solution)/shard_map/ppermute | solution.py:336
  36.4 4.0 %shard_map.104 = (bf16[640,2048]{1,0:T(8,128)(2,1)S(1)}, bf16[640,2048]{1,0:T(8,128)(2,1)S(1)}, bf16[640,512]{1,0:T(8,128)(2,1)S(1)}, bf16[640,512]{1,0:T(8,128)...) custom-call(bf16[640,256]{1,0:T(8,128)(2,1)S(1)} %pad_maximum_fusion, ...), custom_call_target="tpu_custom_call", output_to_operand_aliasing={{0}: (8, {}), {1}: (9, {}), {2}: (10, {}), {3}: (11, {}), {... | custom-call | flops 1000 | bytes 27262976 | tf_op jit(solution)/shard_map/pallas_call | solution.py:93
  40.3 0.2 collective-permute-done.7.refs_1_
  40.6 0.5 collective-permute-start.10
  41.0 1.2 %shard_map.105 = (f32[160,512]{1,0:T(8,128)S(1)}, f32[160,512]{1,0:T(8,128)S(1)}, f32[160,512]{1,0:T(8,128)S(1)}) custom-call(bf16[640,256]{1,0:T(8,128)(2,1)S(1)} %constant_dynamic-update-slice_fusion.refs_0_, bf16[640,256]{1,0:T(8,128)(2,1)S(1)} %collective-permute-done.7.refs_1_, bf16[640,256]{1,0:T(8,128)(2,1)S(1)} %collective-permute-done.8.refs_2_, ...), custom_call_target="tpu_custom_call" | custom-call | flops 1000 | bytes 8257536 | tf_op jit(solution)/shard_map/pallas_call | solution.py:93
  42.2 1.3 %collective-permute-done.10.refs_3_ = bf16[640,256]{1,0:T(8,128)(2,1)S(1)} collective-permute-done((bf16[640,256]{1,0:T(8,128)(2,1)S(1)}, bf16[640,256]{1,0:T(8,128)(2,1)S(1)}, u32[]{:S(2)}, u32[]{:S(2)}) %collective-permute-start.10) | collective-permute-done | bytes 327712 | tf_op jit(solution)/shard_map/ppermute | solution.py:336
  43.6 1.5 %shard_map.106 = (bf16[640,2048]{1,0:T(8,128)(2,1)S(1)}, bf16[640,2048]{1,0:T(8,128)(2,1)S(1)}, bf16[640,512]{1,0:T(8,128)(2,1)S(1)}, bf16[640,512]{1,0:T(8,128)...) custom-call(bf16[640,256]{1,0:T(8,128)(2,1)S(1)} %constant_dynamic-u, ...), custom_call_target="tpu_custom_call", output_to_operand_aliasing={{0}: (10, {}), {1}: (11, {}), {2}: (12, {}), {3}: (13, {}),... | custom-call | flops 1000 | bytes 23330816 | tf_op jit(solution)/shard_map/pallas_call | solution.py:93
  45.0 0.2 collective-permute-start.12
  45.2 0.8 %shard_map.107 = bf16[4,160,256]{2,1,0:T(8,128)(2,1)S(1)} custom-call(bf16[640,512]{1,0:T(8,128)(2,1)S(1)} %get-tuple-element.172.gate_grad.right, bf16[640,512]{1,0:T(8,128)(2,1)S(1)} %get-tuple-element.173.up_grad.right, bf16[2048,512]{1,0:T(8,128)(2,1)S(1)} %get-tuple-element.131.refs_5_.refs_3_.refs_7_.w_gate, ...), custom_call_target="tpu_custom_call" | custom-call | flops 1000 | bytes 5832704 | tf_op jit(solution)/shard_map/pallas_call | solution.py:93
  46.0 0.2 add_convert_fusion.4
  46.3 0.4 collective-permute-done.12
  46.8 1.3 %collective-permute-start.13 = (bf16[640,256]{1,0:T(8,128)(2,1)S(1)}, bf16[640,256]{1,0:T(8,128)(2,1)S(1)}, u32[]{:S(2)}, u32[]{:S(2)}) collective-permute-start(bf16[640,256]{1,0:T(8,128)(2,1)S(1)} %pad_maximum_fusion.2), channel_id=1, source_target_pairs={{0,16},{4,12},{8,24},{12,4},{16,0},{20,28},{24,8},{28,20},{1,17},{... | collective-permute-start | bytes 983048 | tf_op jit(solution)/shard_map/ppermute | solution.py:354
  48.2 0.8 %collective-permute-start.15 = (bf16[640,256]{1,0:T(8,128)(2,1)S(1)}, bf16[640,256]{1,0:T(8,128)(2,1)S(1)}, u32[]{:S(2)}, u32[]{:S(2)}) collective-permute-start(bf16[640,256]{1,0:T(8,128)(2,1)S(1)} %pad_maximum_fusion.3), channel_id=1, source_target_pairs={{0,16},{4,12},{8,24},{12,4},{16,0},{20,28},{24,8},{28,20},{1,17},{... | collective-permute-start | bytes 983048 | tf_op jit(solution)/shard_map/ppermute | solution.py:354
  49.0 5.0 %collective-permute-done.13 = bf16[640,256]{1,0:T(8,128)(2,1)S(1)} collective-permute-done((bf16[640,256]{1,0:T(8,128)(2,1)S(1)}, bf16[640,256]{1,0:T(8,128)(2,1)S(1)}, u32[]{:S(2)}, u32[]{:S(2)}) %collective-permute-start.13) | collective-permute-done | bytes 327712 | tf_op jit(solution)/shard_map/ppermute | solution.py:354
  54.1 1.0 %collective-permute-start.14 = (bf16[320,256]{1,0:T(8,128)(2,1)S(1)}, bf16[320,256]{1,0:T(8,128)(2,1)S(1)}, u32[]{:S(2)}, u32[]{:S(2)}) collective-permute-start(bf16[320,256]{1,0:T(8,128)(2,1)S(1)} %get-tuple-element.203), channel_id=1, source_target_pairs={{0,8},{4,20},{8,0},{12,28},{16,24},{20,4},{24,16},{28,12},{1,9},{5... | collective-permute-start | bytes 491528 | tf_op jit(solution)/shard_map/ppermute | solution.py:350
  55.1 2.7 %shard_map.108 = bf16[2048,512]{1,0:T(8,128)(2,1)} custom-call(bf16[640,2048]{1,0:T(8,128)(2,1)S(1)} %get-tuple-element.180.left, bf16[640,512]{1,0:T(8,128)(2,1)S(1)} %get-tuple-element.173.up_grad.right), custom_call_target="tpu_custom_call" | custom-call | flops 1000 | bytes 5373952 | tf_op jit(solution)/shard_map/pallas_call | solution.py:93
  57.8 1.1 %collective-permute-start.16 = (bf16[320,256]{1,0:T(8,128)(2,1)S(1)}, bf16[320,256]{1,0:T(8,128)(2,1)S(1)}, u32[]{:S(2)}, u32[]{:S(2)}) collective-permute-start(bf16[320,256]{1,0:T(8,128)(2,1)S(1)} %get-tuple-element.202), channel_id=1, source_target_pairs={{0,8},{4,20},{8,0},{12,28},{16,24},{20,4},{24,16},{28,12},{1,9},{5... | collective-permute-start | bytes 491528 | tf_op jit(solution)/shard_map/ppermute | solution.py:350
  58.9 0.6 collective-permute-done.14
  59.6 3.6 %collective-permute-done.16 = bf16[320,256]{1,0:T(8,128)(2,1)S(1)} collective-permute-done((bf16[320,256]{1,0:T(8,128)(2,1)S(1)}, bf16[320,256]{1,0:T(8,128)(2,1)S(1)}, u32[]{:S(2)}, u32[]{:S(2)}) %collective-permute-start.16) | collective-permute-done | bytes 163872 | tf_op jit(solution)/shard_map/ppermute | solution.py:350
  63.3 2.1 %collective-permute-start.18 = (bf16[160,256]{1,0:T(8,128)(2,1)S(1)}, bf16[160,256]{1,0:T(8,128)(2,1)S(1)}, u32[]{:S(2)}, u32[]{:S(2)}) collective-permute-start(bf16[160,256]{1,0:T(8,128)(2,1)S(1)} %get-tuple-element.206), channel_id=1, source_target_pairs={{0,2},{1,3},{2,0},{3,1},{4,6},{5,7},{6,4},{7,5},{8,10},{9,11},{10,... | collective-permute-start | bytes 245768 | tf_op jit(solution)/shard_map/ppermute | solution.py:336
  65.4 0.3 collective-permute-start.17
  65.6 2.1 %collective-permute-start.19 = (bf16[160,256]{1,0:T(8,128)(2,1)S(1)}, bf16[160,256]{1,0:T(8,128)(2,1)S(1)}, u32[]{:S(2)}, u32[]{:S(2)}) collective-permute-start(bf16[160,256]{1,0:T(8,128)(2,1)S(1)} %get-tuple-element.204), channel_id=1, source_target_pairs={{0,3},{1,2},{2,1},{3,0},{4,7},{5,6},{6,5},{7,4},{8,11},{9,10},{10,... | collective-permute-start | bytes 245768 | tf_op jit(solution)/shard_map/ppermute | solution.py:336
  67.7 2.8 %shard_map.109 = bf16[2048,512]{1,0:T(8,128)(2,1)} custom-call(bf16[640,2048]{1,0:T(8,128)(2,1)S(1)} %get-tuple-element.180.left, bf16[640,512]{1,0:T(8,128)(2,1)S(1)} %get-tuple-element.172.gate_grad.right), custom_call_target="tpu_custom_call" | custom-call | flops 1000 | bytes 5373952 | tf_op jit(solution)/shard_map/pallas_call | solution.py:93
  70.7 1.3 %collective-permute-done.19.r3 = bf16[160,256]{1,0:T(8,128)(2,1)S(1)} collective-permute-done((bf16[160,256]{1,0:T(8,128)(2,1)S(1)}, bf16[160,256]{1,0:T(8,128)(2,1)S(1)}, u32[]{:S(2)}, u32[]{:S(2)}) %collective-permute-start.19) | collective-permute-done | bytes 81952 | tf_op jit(solution)/shard_map/ppermute | solution.py:336
  72.0 0.3 shard_map.110.refs_0_
  72.3 1.3 %collective-permute-start.20 = (bf16[256,256]{1,0:T(8,128)(2,1)S(1)}, bf16[256,256]{1,0:T(8,128)(2,1)S(1)}, u32[]{:S(2)}, u32[]{:S(2)}) collective-permute-start(bf16[256,256]{1,0:T(8,128)(2,1)S(1)} %shard_map.110.refs_0_), channel_id=1, source_target_pairs={{0,8},{4,20},{8,0},{12,28},{16,24},{20,4},{24,16},{28,12},{1,9},{5... | collective-permute-start | bytes 393224 | tf_op jit(solution)/shard_map/ppermute | solution.py:350
  73.6 0.6 collective-permute-start.21
  74.2 1.7 %collective-permute-start.22 = (bf16[256,256]{1,0:T(8,128)(2,1)S(1)}, bf16[256,256]{1,0:T(8,128)(2,1)S(1)}, u32[]{:S(2)}, u32[]{:S(2)}) collective-permute-start(bf16[256,256]{1,0:T(8,128)(2,1)S(1)} %shard_map.110.refs_0_), channel_id=1, source_target_pairs={{0,24},{4,28},{8,16},{12,20},{16,8},{20,12},{24,0},{28,4},{1,25},{... | collective-permute-start | bytes 393224 | tf_op jit(solution)/shard_map/ppermute | solution.py:336
  75.8 2.6 %shard_map.111 = bf16[512,2048]{1,0:T(8,128)(2,1)} custom-call(bf16[640,512]{1,0:T(8,128)(2,1)S(1)} %get-tuple-element.184.left, bf16[640,2048]{1,0:T(8,128)(2,1)S(1)} %get-tuple-element.185.right), custom_call_target="tpu_custom_call" | custom-call | flops 1000 | bytes 5373952 | tf_op jit(solution)/shard_map/pallas_call | solution.py:93
  78.5 1.5 %collective-permute-done.22.refs_3_ = bf16[256,256]{1,0:T(8,128)(2,1)S(1)} collective-permute-done((bf16[256,256]{1,0:T(8,128)(2,1)S(1)}, bf16[256,256]{1,0:T(8,128)(2,1)S(1)}, u32[]{:S(2)}, u32[]{:S(2)}) %collective-permute-start.22) | collective-permute-done | bytes 131104 | tf_op jit(solution)/shard_map/ppermute | solution.py:336
  80.2 0.8 shard_map.112.refs_1_
  81.0 1.1 %collective-permute-done.23.refs_0_ = bf16[1024,256]{1,0:T(8,128)(2,1)S(1)} collective-permute-done((bf16[1024,256]{1,0:T(8,128)(2,1)S(1)}, bf16[1024,256]{1,0:T(8,128)(2,1)S(1)}, u32[]{:S(2)}, u32[]{:S(2)}) %collective-permute-start.23) | collective-permute-done | bytes 524320 | tf_op jit(solution)/shard_map/ppermute | solution.py:336
  82.1 0.8 shard_map.113
  (33 shorter events, 0.9 us)
Async XLA Ops:
  2.1 11.4 %collective-permute-start = (bf16[320,256]{1,0:T(8,128)(2,1)S(1)}, bf16[320,256]{1,0:T(8,128)(2,1)S(1)}, u32[]{:S(2)}, u32[]{:S(2)}) collective-permute-start(bf16[320,256]{1,0:T(8,128)(2,1)S(1)} %get-tuple-element.100), channel_id=1, source_target_pairs={{0,1},{1,0},{2,3},{3,2},{4,5},{5,4},{6,7},{7,6},{8,9},{9,8},{10,11... | collective-permute-start | bytes 491528 | tf_op jit(solution)/shard_map/ppermute | solution.py:336
  5.2 10.0 %collective-permute-start.1 = (bf16[320,256]{1,0:T(8,128)(2,1)S(1)}, bf16[320,256]{1,0:T(8,128)(2,1)S(1)}, u32[]{:S(2)}, u32[]{:S(2)}) collective-permute-start(bf16[320,256]{1,0:T(8,128)(2,1)S(1)} %get-tuple-element.101), channel_id=1, source_target_pairs={{0,3},{1,2},{2,1},{3,0},{4,7},{5,6},{6,5},{7,4},{8,11},{9,10},{10,... | collective-permute-start | bytes 491528 | tf_op jit(solution)/shard_map/ppermute | solution.py:336
  15.3 10.1 %collective-permute-start.2 = (bf16[640,256]{1,0:T(8,128)(2,1)S(1)}, bf16[640,256]{1,0:T(8,128)(2,1)S(1)}, u32[]{:S(2)}, u32[]{:S(2)}) collective-permute-start(bf16[640,256]{1,0:T(8,128)(2,1)S(1)} %pad_maximum_fusion.1.refs_0_), channel_id=1, source_target_pairs={{0,8},{4,20},{8,0},{12,28},{16,24},{20,4},{24,16},{28,12},{1,9},{5... | collective-permute-start | bytes 983048 | tf_op jit(solution)/shard_map/ppermute | solution.py:350
  16.8 8.0 %collective-permute-start.3 = (bf16[320,256]{1,0:T(8,128)(2,1)S(1)}, bf16[320,256]{1,0:T(8,128)(2,1)S(1)}, u32[]{:S(2)}, u32[]{:S(2)}) collective-permute-start(bf16[320,256]{1,0:T(8,128)(2,1)S(1)} %get-tuple-element.125), channel_id=1, source_target_pairs={{0,2},{1,3},{2,0},{3,1},{4,6},{5,7},{6,4},{7,5},{8,10},{9,11},{10,... | collective-permute-start | bytes 491528 | tf_op jit(solution)/shard_map/ppermute | solution.py:336
  18.6 10.3 %collective-permute-start.4 = (bf16[640,256]{1,0:T(8,128)(2,1)S(1)}, bf16[640,256]{1,0:T(8,128)(2,1)S(1)}, u32[]{:S(2)}, u32[]{:S(2)}) collective-permute-start(bf16[640,256]{1,0:T(8,128)(2,1)S(1)} %pad_maximum_fusion.1.refs_0_), channel_id=1, source_target_pairs={{0,16},{4,12},{8,24},{12,4},{16,0},{20,28},{24,8},{28,20},{1,17},{... | collective-permute-start | bytes 983048 | tf_op jit(solution)/shard_map/ppermute | solution.py:354
  25.4 7.8 %collective-permute-start.5 = (bf16[640,256]{1,0:T(8,128)(2,1)S(1)}, bf16[640,256]{1,0:T(8,128)(2,1)S(1)}, u32[]{:S(2)}, u32[]{:S(2)}) collective-permute-start(bf16[640,256]{1,0:T(8,128)(2,1)S(1)} %collective-permute-done.2.refs_1_), channel_id=1, source_target_pairs={{0,16},{4,12},{8,24},{12,4},{16,0},{20,28},{24,8},{28,20},{1,17},{... | collective-permute-start | bytes 983048 | tf_op jit(solution)/shard_map/ppermute | solution.py:354
  27.4 5.3 %collective-permute-start.6 = (bf16[320,256]{1,0:T(8,128)(2,1)S(1)}, bf16[320,256]{1,0:T(8,128)(2,1)S(1)}, u32[]{:S(2)}, u32[]{:S(2)}) collective-permute-start(bf16[320,256]{1,0:T(8,128)(2,1)S(1)} %collective-permute-done.3), channel_id=1, source_target_pairs={{0,8},{4,20},{8,0},{12,28},{16,24},{20,4},{24,16},{28,12},{1,9},{5... | collective-permute-start | bytes 491528 | tf_op jit(solution)/shard_map/ppermute | solution.py:350
  33.2 3.1 %collective-permute-start.9 = (bf16[2560,256]{1,0:T(8,128)(2,1)S(1)}, bf16[2560,256]{1,0:T(8,128)(2,1)S(1)}, u32[]{:S(2)}, u32[]{:S(2)}) collective-permute-start(bf16[2560,256]{1,0:T(8,128)(2,1)S(1)} %constant_dynamic-update-slice_fusion.2), channel_id=1, source_target_pairs={{0,4},{4,0},{8,12},{12,8},{16,20},{20,16},{24,28},{28,24},{1,5},{5... | collective-permute-start | bytes 3932168 | tf_op jit(solution)/shard_map/ppermute | solution.py:336
  33.4 7.1 %collective-permute-start.7 = (bf16[640,256]{1,0:T(8,128)(2,1)S(1)}, bf16[640,256]{1,0:T(8,128)(2,1)S(1)}, u32[]{:S(2)}, u32[]{:S(2)}) collective-permute-start(bf16[640,256]{1,0:T(8,128)(2,1)S(1)} %constant_dynamic-update-slice_fusion.refs_0_), channel_id=1, source_target_pairs={{0,16},{4,12},{8,24},{12,4},{16,0},{20,28},{24,8},{28,20},{1,17},{... | collective-permute-start | bytes 983048 | tf_op jit(solution)/shard_map/ppermute | solution.py:354
  34.7 5.8 %collective-permute-start.8 = (bf16[640,256]{1,0:T(8,128)(2,1)S(1)}, bf16[640,256]{1,0:T(8,128)(2,1)S(1)}, u32[]{:S(2)}, u32[]{:S(2)}) collective-permute-start(bf16[640,256]{1,0:T(8,128)(2,1)S(1)} %constant_dynamic-update-slice_fusion.refs_0_), channel_id=1, source_target_pairs={{0,4},{4,0},{8,12},{12,8},{16,20},{20,16},{24,28},{28,24},{1,5},{5... | collective-permute-start | bytes 983048 | tf_op jit(solution)/shard_map/ppermute | solution.py:336
  40.5 3.0 %collective-permute-start.11 = (bf16[4,480,256]{2,1,0:T(8,128)(2,1)S(1)}, bf16[4,480,256]{2,1,0:T(8,128)(2,1)S(1)}, u32[]{:S(2)}, u32[]{:S(2)}) collective-permute-start(bf16[4,480,256]{2,1,0:T(8,128)(2,1)S(1)} %get-tuple-element.149), channel_id=1, source_target_pairs={{0,4},{4,0},{8,12},{12,8},{16,20},{20,16},{24,28},{28,24},{1,5},{5... | collective-permute-start | bytes 2949128 | tf_op jit(solution)/shard_map/ppermute | solution.py:336
  40.6 3.0 %collective-permute-start.10 = (bf16[640,256]{1,0:T(8,128)(2,1)S(1)}, bf16[640,256]{1,0:T(8,128)(2,1)S(1)}, u32[]{:S(2)}, u32[]{:S(2)}) collective-permute-start(bf16[640,256]{1,0:T(8,128)(2,1)S(1)} %collective-permute-done.7.refs_1_), channel_id=1, source_target_pairs={{0,4},{4,0},{8,12},{12,8},{16,20},{20,16},{24,28},{28,24},{1,5},{5... | collective-permute-start | bytes 983048 | tf_op jit(solution)/shard_map/ppermute | solution.py:336
  45.0 1.7 %collective-permute-start.12 = (bf16[4,160,256]{2,1,0:T(8,128)(2,1)S(1)}, bf16[4,160,256]{2,1,0:T(8,128)(2,1)S(1)}, u32[]{:S(2)}, u32[]{:S(2)}) collective-permute-start(bf16[4,160,256]{2,1,0:T(8,128)(2,1)S(1)} %get-tuple-element.171), channel_id=1, source_target_pairs={{0,4},{4,0},{8,12},{12,8},{16,20},{20,16},{24,28},{28,24},{1,5},{5... | collective-permute-start | bytes 983048 | tf_op jit(solution)/shard_map/ppermute | solution.py:336
  46.8 7.1 %collective-permute-start.13 = (bf16[640,256]{1,0:T(8,128)(2,1)S(1)}, bf16[640,256]{1,0:T(8,128)(2,1)S(1)}, u32[]{:S(2)}, u32[]{:S(2)}) collective-permute-start(bf16[640,256]{1,0:T(8,128)(2,1)S(1)} %pad_maximum_fusion.2), channel_id=1, source_target_pairs={{0,16},{4,12},{8,24},{12,4},{16,0},{20,28},{24,8},{28,20},{1,17},{... | collective-permute-start | bytes 983048 | tf_op jit(solution)/shard_map/ppermute | solution.py:354
  48.2 10.7 %collective-permute-start.15 = (bf16[640,256]{1,0:T(8,128)(2,1)S(1)}, bf16[640,256]{1,0:T(8,128)(2,1)S(1)}, u32[]{:S(2)}, u32[]{:S(2)}) collective-permute-start(bf16[640,256]{1,0:T(8,128)(2,1)S(1)} %pad_maximum_fusion.3), channel_id=1, source_target_pairs={{0,16},{4,12},{8,24},{12,4},{16,0},{20,28},{24,8},{28,20},{1,17},{... | collective-permute-start | bytes 983048 | tf_op jit(solution)/shard_map/ppermute | solution.py:354
  54.1 5.4 %collective-permute-start.14 = (bf16[320,256]{1,0:T(8,128)(2,1)S(1)}, bf16[320,256]{1,0:T(8,128)(2,1)S(1)}, u32[]{:S(2)}, u32[]{:S(2)}) collective-permute-start(bf16[320,256]{1,0:T(8,128)(2,1)S(1)} %get-tuple-element.203), channel_id=1, source_target_pairs={{0,8},{4,20},{8,0},{12,28},{16,24},{20,4},{24,16},{28,12},{1,9},{5... | collective-permute-start | bytes 491528 | tf_op jit(solution)/shard_map/ppermute | solution.py:350
  57.8 5.4 %collective-permute-start.16 = (bf16[320,256]{1,0:T(8,128)(2,1)S(1)}, bf16[320,256]{1,0:T(8,128)(2,1)S(1)}, u32[]{:S(2)}, u32[]{:S(2)}) collective-permute-start(bf16[320,256]{1,0:T(8,128)(2,1)S(1)} %get-tuple-element.202), channel_id=1, source_target_pairs={{0,8},{4,20},{8,0},{12,28},{16,24},{20,4},{24,16},{28,12},{1,9},{5... | collective-permute-start | bytes 491528 | tf_op jit(solution)/shard_map/ppermute | solution.py:350
  63.3 7.3 %collective-permute-start.18 = (bf16[160,256]{1,0:T(8,128)(2,1)S(1)}, bf16[160,256]{1,0:T(8,128)(2,1)S(1)}, u32[]{:S(2)}, u32[]{:S(2)}) collective-permute-start(bf16[160,256]{1,0:T(8,128)(2,1)S(1)} %get-tuple-element.206), channel_id=1, source_target_pairs={{0,2},{1,3},{2,0},{3,1},{4,6},{5,7},{6,4},{7,5},{8,10},{9,11},{10,... | collective-permute-start | bytes 245768 | tf_op jit(solution)/shard_map/ppermute | solution.py:336
  65.4 5.3 %collective-permute-start.17 = (bf16[160,256]{1,0:T(8,128)(2,1)S(1)}, bf16[160,256]{1,0:T(8,128)(2,1)S(1)}, u32[]{:S(2)}, u32[]{:S(2)}) collective-permute-start(bf16[160,256]{1,0:T(8,128)(2,1)S(1)} %get-tuple-element.205), channel_id=1, source_target_pairs={{0,1},{1,0},{2,3},{3,2},{4,5},{5,4},{6,7},{7,6},{8,9},{9,8},{10,11... | collective-permute-start | bytes 245768 | tf_op jit(solution)/shard_map/ppermute | solution.py:336
  65.6 6.3 %collective-permute-start.19 = (bf16[160,256]{1,0:T(8,128)(2,1)S(1)}, bf16[160,256]{1,0:T(8,128)(2,1)S(1)}, u32[]{:S(2)}, u32[]{:S(2)}) collective-permute-start(bf16[160,256]{1,0:T(8,128)(2,1)S(1)} %get-tuple-element.204), channel_id=1, source_target_pairs={{0,3},{1,2},{2,1},{3,0},{4,7},{5,6},{6,5},{7,4},{8,11},{9,10},{10,... | collective-permute-start | bytes 245768 | tf_op jit(solution)/shard_map/ppermute | solution.py:336
  72.3 6.2 %collective-permute-start.20 = (bf16[256,256]{1,0:T(8,128)(2,1)S(1)}, bf16[256,256]{1,0:T(8,128)(2,1)S(1)}, u32[]{:S(2)}, u32[]{:S(2)}) collective-permute-start(bf16[256,256]{1,0:T(8,128)(2,1)S(1)} %shard_map.110.refs_0_), channel_id=1, source_target_pairs={{0,8},{4,20},{8,0},{12,28},{16,24},{20,4},{24,16},{28,12},{1,9},{5... | collective-permute-start | bytes 393224 | tf_op jit(solution)/shard_map/ppermute | solution.py:350
  73.6 5.0 %collective-permute-start.21 = (bf16[256,256]{1,0:T(8,128)(2,1)S(1)}, bf16[256,256]{1,0:T(8,128)(2,1)S(1)}, u32[]{:S(2)}, u32[]{:S(2)}) collective-permute-start(bf16[256,256]{1,0:T(8,128)(2,1)S(1)} %shard_map.110.refs_0_), channel_id=1, source_target_pairs={{0,16},{4,12},{8,24},{12,4},{16,0},{20,28},{24,8},{28,20},{1,17},{... | collective-permute-start | bytes 393224 | tf_op jit(solution)/shard_map/ppermute | solution.py:354
  74.2 5.9 %collective-permute-start.22 = (bf16[256,256]{1,0:T(8,128)(2,1)S(1)}, bf16[256,256]{1,0:T(8,128)(2,1)S(1)}, u32[]{:S(2)}, u32[]{:S(2)}) collective-permute-start(bf16[256,256]{1,0:T(8,128)(2,1)S(1)} %shard_map.110.refs_0_), channel_id=1, source_target_pairs={{0,24},{4,28},{8,16},{12,20},{16,8},{20,12},{24,0},{28,4},{1,25},{... | collective-permute-start | bytes 393224 | tf_op jit(solution)/shard_map/ppermute | solution.py:336
  80.1 2.0 %collective-permute-start.23 = (bf16[1024,256]{1,0:T(8,128)(2,1)S(1)}, bf16[1024,256]{1,0:T(8,128)(2,1)S(1)}, u32[]{:S(2)}, u32[]{:S(2)}) collective-permute-start(bf16[1024,256]{1,0:T(8,128)(2,1)S(1)} %pad_maximum_fusion), channel_id=1, source_target_pairs={{0,4},{4,0},{8,12},{12,8},{16,20},{20,16},{24,28},{28,24},{1,5},{5... | collective-permute-start | bytes 1572872 | tf_op jit(solution)/shard_map/ppermute | solution.py:336
